TPU v7x, 512 devices: a whole 4x4x16 slice. The times are simulated.
512 devices in a mesh: seq: 128 (over x, y_hi, z), fsdp: 4 (over y_lo, core).
Axes of the slice: x: 4, y: 4 (y_hi: 2, y_lo: 2; y = y_hi * 2 + y_lo), z: 16, core: 2. Of those that a mesh axis runs over, the one named last changes fastest.
Arguments:
- block_input: bfloat16 [8, 16384, 1536], P('fsdp', 'seq'), may hold values from -6 to 6
- dilated_weight: bfloat16 [3, 1536, 768], P(None, 'fsdp'), may hold values from -0.09375 to 0.09375
- w_project: bfloat16 [768, 1536], P('fsdp'), may hold values from -0.21875 to 0.21875
- gain_first: float32 [1536], replicated, may hold values from 0.5 to 1.5
- gain_second: float32 [768], replicated, may hold values from 0.5 to 1.5
- grad_output: bfloat16 [8, 16384, 1536], P('fsdp', 'seq'), may hold values from -6 to 6
Outputs:
- grad_input: bfloat16 [8, 16384, 1536], P('fsdp', 'seq')
- grad_gain_first: float32 [1536], replicated
- grad_gain_second: float32 [768], replicated
All inputs are finite; a program needn't handle non-finite values.
Results may differ from a plain program's by a relative error of at most 0.008.
Values may be sent and summed in bfloat16 or wider, within the bound.
No kernel may reach another device: no remote copies, remote signals or barrier semaphores. Data moves between devices by JAX's collectives and lax.ppermute only.
A program may use at most 64 MiB of HBM per device.

v0:
```python
import jax
import jax.numpy as jnp
from jax import lax
from jax.sharding import PartitionSpec as P


def shifted(value, axis, steps):
    count = lax.axis_size(axis)
    initial, last = (max(0, -steps), min(count, count - steps))
    return lax.ppermute(value, axis, [(source, source + steps) for source in range(initial, last)])


def norm_act(values, factor):
    centre = values - jnp.mean(values, axis=-1, keepdims=True)
    spread = jnp.mean(centre * centre, axis=-1, keepdims=True)
    return jax.nn.gelu(centre * lax.rsqrt(spread + 1e-05) * factor)


def far_inputs(values, amount):
    return shifted(values, "seq", amount)


def far_grads(values, amount):
    return shifted(values, "seq", amount)


def three_taps(lagging, hidden_state, leading, w_full):
    mixed_state = jnp.einsum("sbc,ch->sbh", lagging, w_full[0], preferred_element_type=jnp.float32)
    mixed_state = mixed_state + jnp.einsum(
        "sbc,ch->sbh", hidden_state, w_full[1], preferred_element_type=jnp.float32
    )
    return mixed_state + jnp.einsum(
        "sbc,ch->sbh", leading, w_full[2], preferred_element_type=jnp.float32
    )


def block_grads(
    inputs, cotangent, w_full, proj_full, gain_first, gain_second, forward_mix, taps_grad
):
    widened = inputs.astype(jnp.float32)
    hidden_state = norm_act(widened, gain_first).astype(jnp.bfloat16)
    mixed_state = forward_mix(hidden_state).astype(jnp.bfloat16)
    grad_hidden2 = jnp.einsum(
        "sbc,hc->sbh", cotangent, proj_full, preferred_element_type=jnp.float32
    )
    unused, pull_second = jax.vjp(norm_act, mixed_state.astype(jnp.float32), gain_second)
    mixed_gradient, grad_second = pull_second(grad_hidden2)
    mixed_gradient = mixed_gradient.astype(jnp.bfloat16)
    grad_ahead, grad_behind = taps_grad(mixed_gradient)
    hidden_gradient = jnp.einsum(
        "sbh,ch->sbc", grad_ahead, w_full[0], preferred_element_type=jnp.float32
    )
    hidden_gradient = hidden_gradient + jnp.einsum(
        "sbh,ch->sbc", mixed_gradient, w_full[1], preferred_element_type=jnp.float32
    )
    hidden_gradient = hidden_gradient + jnp.einsum(
        "sbh,ch->sbc", grad_behind, w_full[2], preferred_element_type=jnp.float32
    )
    unused2, pull_first = jax.vjp(norm_act, widened, gain_first)
    grad_branch, grad_first = pull_first(hidden_gradient)
    grad_local = (cotangent.astype(jnp.float32) + grad_branch).astype(jnp.bfloat16)
    return (grad_local, grad_first, grad_second)


def body(block_input, dilated_weight, w_project, gain_first, gain_second, grad_output):
    w_full, proj_full = (
        lax.all_gather(dilated_weight, "fsdp", axis=1, tiled=True),
        lax.all_gather(w_project, "fsdp", axis=0, tiled=True),
    )
    reach = lax.axis_size("seq") // 8

    def remote_mix(hidden_state):
        return three_taps(
            far_inputs(hidden_state, reach), hidden_state, far_inputs(hidden_state, -reach), w_full
        )

    def remote_grads(values):
        return (far_grads(values, -reach), far_grads(values, reach))

    grad_input, first_sum, second_sum = block_grads(
        block_input,
        grad_output,
        w_full,
        proj_full,
        gain_first,
        gain_second,
        remote_mix,
        remote_grads,
    )
    totals = lax.psum((first_sum, second_sum), ("seq", "fsdp"))
    return (grad_input, totals[0], totals[1])


def solution(mesh):
    in_specs = (
        P("fsdp", "seq", None),
        P(None, "fsdp", None),
        P("fsdp", None),
        P(),
        P(),
        P("fsdp", "seq", None),
    )
    out_specs = (P("fsdp", "seq", None), P(), P())
    return jax.shard_map(body, mesh=mesh, in_specs=in_specs, out_specs=out_specs, check_vma=False)
```

profile of v0, /device:TPU:1, one launch (start us, length us, event | category | flops | bytes accessed | tf_op | source)
XLA Modules:
  0.0 298.8 jit_solution(9477924018864004862)
XLA Ops:
  7.2 0.7 all-gather.5.cloned.1.call-update
  8.0 0.7 all-gather.3.cloned.1.call-update
  8.9 0.3 fusion.23
  9.2 0.8 fusion.19
  10.0 1.3 collective-permute-start.1
  11.3 6.3 %collective-permute-start = (bf16[2,128,1536]{2,1,0:T(8,128)(2,1)S(1)}, bf16[2,128,1536]{2,1,0:T(8,128)(2,1)S(1)}, u32[]{:S(2)}, u32[]{:S(2)}) collective-permute-start(bf16[2,128,1536]{2,1,0:T(8,128)(2,1)S(1)} %fusion.19), channel_id=1, source_target_pairs={{0,64},{4,68},{8,72},{12,76},{16,80},{20,84},{24,88},{28,92},{32,9... | collective-permute-start | bytes 2359304 | tf_op jit(solution)/shard_map/ppermute | solution.py:10
  17.7 91.2 %all-gather.5.cloned.1.call-done = bf16[3,1536,768]{2,1,0:T(8,128)(2,1)} async-done(((bf16[3,384,768]{2,1,0:T(8,128)(2,1)}), bf16[3,1536,768]{2,1,0:T(8,128)(2,1)}) %all-gather.5.cloned.1.call-update) | async-done | bytes 7077904 | tf_op jit(solution)/shard_map/all_gather | solution.py:67
  108.8 2.4 fusion.5
  111.3 2.4 fusion.7
  113.8 2.6 fusion.44
  116.4 0.2 multiply_reduce_fusion.2
  116.6 36.3 %all-gather.3.cloned.1.call-done = bf16[768,1536]{1,0:T(8,128)(2,1)} async-done(((bf16[192,1536]{1,0:T(8,128)(2,1)}), bf16[768,1536]{1,0:T(8,128)(2,1)}) %all-gather.3.cloned.1.call-update) | async-done | bytes 2359312 | tf_op jit(solution)/shard_map/all_gather | solution.py:68
  153.0 3.0 multiply_reduce_fusion.1
  156.0 0.5 multiply_reduce_fusion
  156.4 0.3 add_convert_fusion.1
  156.7 4.4 %collective-permute-start.3 = (bf16[2,128,768]{2,1,0:T(8,128)(2,1)S(1)}, bf16[2,128,768]{2,1,0:T(8,128)(2,1)S(1)}, u32[]{:S(2)}, u32[]{:S(2)}) collective-permute-start(bf16[2,128,768]{2,1,0:T(8,128)(2,1)S(1)} %add_convert_fusion.1), channel_id=1, source_target_pairs={{0,64},{4,68},{8,72},{12,76},{16,80},{20,84},{24,88},{28,92},{32,9... | collective-permute-start | bytes 1179656 | tf_op jit(solution)/shard_map/ppermute | solution.py:10
  161.1 1.3 collective-permute-start.2
  162.4 2.5 fusion.4
  164.9 13.1 %collective-permute-done.3 = bf16[2,128,768]{2,1,0:T(8,128)(2,1)S(1)} collective-permute-done((bf16[2,128,768]{2,1,0:T(8,128)(2,1)S(1)}, bf16[2,128,768]{2,1,0:T(8,128)(2,1)S(1)}, u32[]{:S(2)}, u32[]{:S(2)}) %collective-permute-start.3) | collective-permute-done | bytes 393248 | tf_op jit(solution)/shard_map/ppermute | solution.py:10
  178.0 2.5 fusion.6
  180.5 3.7 %fusion.24 = (f32[2,128]{1,0:T(2,128)S(1)}, f32[2,128,1536]{2,1,0:T(8,128)S(1)}) fusion(bf16[2,128,1536]{2,1,0:T(8,128)(2,1)S(1)} %copy-done, f32[1536]{0:T(1024)S(1)} %copy-done.2, f32[2,128]{1,0:T(2,128)S(1)} %broadcast_multiply_fusion.1, f32[2,128]{1,0:T(2,128)S(1)} %fusion.42, f32[2,128,1536]{2,1,0:T(8,128)S(1)} %fusion.6, ...), kind=kOutput, calls=%fused_computation.33 | convolution fusion | flops 614989568 | bytes 8266752 | tf_op jit(solution)/shard_map/sbh,ch->sbc/dot_general | solution.py:50
  184.2 0.7 fusion.22
  185.0 1.5 add_convert_fusion
  186.5 105.5 %all-reduce = (f32[1536]{0:T(1024)}, f32[768]{0:T(1024)}) all-reduce(f32[1536]{0:T(1024)S(1)} %get-tuple-element.3, f32[768]{0:T(1024)S(1)} %get-tuple-element.5), channel_id=1, replica_groups=mesh['seq'=128,'fsdp'=4] {'seq','fsdp'}, use_global_device_ids=true, to_apply=%region_9.0 | all-reduce | flops 2304 | bytes 18432 | tf_op jit(solution)/shard_map/psum | solution.py:90
  (22 shorter events, 0.4 us)
Async XLA Ops:
  7.2 1.5 copy-start
  7.2 2.1 copy-start.2
  7.2 101.7 %all-gather.5.cloned.1.call-start = ((), (), s32[]{:S(2)}) async-start(), calls=%async_computation.1 | async-start | bytes 8847360 | tf_op jit(solution)/shard_map/all_gather | solution.py:67
  7.9 145.0 %all-gather.3.cloned.1.call-start = ((), (), s32[]{:S(2)}) async-start(), calls=%async_computation | async-start | bytes 2949120 | tf_op jit(solution)/shard_map/all_gather | solution.py:68
  10.0 101.3 %collective-permute-start.1 = (bf16[2,128,1536]{2,1,0:T(8,128)(2,1)S(1)}, bf16[2,128,1536]{2,1,0:T(8,128)(2,1)S(1)}, u32[]{:S(2)}, u32[]{:S(2)}) collective-permute-start(bf16[2,128,1536]{2,1,0:T(8,128)(2,1)S(1)} %fusion.19), channel_id=1, source_target_pairs={{64,0},{68,4},{72,8},{76,12},{80,16},{84,20},{88,24},{92,28},{96,3... | collective-permute-start | bytes 2359304 | tf_op jit(solution)/shard_map/ppermute | solution.py:10
  11.3 102.4 %collective-permute-start = (bf16[2,128,1536]{2,1,0:T(8,128)(2,1)S(1)}, bf16[2,128,1536]{2,1,0:T(8,128)(2,1)S(1)}, u32[]{:S(2)}, u32[]{:S(2)}) collective-permute-start(bf16[2,128,1536]{2,1,0:T(8,128)(2,1)S(1)} %fusion.19), channel_id=1, source_target_pairs={{0,64},{4,68},{8,72},{12,76},{16,80},{20,84},{24,88},{28,92},{32,9... | collective-permute-start | bytes 2359304 | tf_op jit(solution)/shard_map/ppermute | solution.py:10
  113.7 39.2 %copy-start.1 = (bf16[2,128,1536]{2,1,0:T(8,128)(2,1)S(1)}, bf16[2,128,1536]{2,1,0:T(8,128)(2,1)}, u32[]{:S(2)}) copy-start(bf16[2,128,1536]{2,1,0:T(8,128)(2,1)} %param.11) | copy-start | bytes 2359300
  113.8 39.2 %copy-start.3 = (f32[768]{0:T(1024)S(1)}, f32[768]{0:T(1024)}, u32[]{:S(2)}) copy-start(f32[768]{0:T(1024)} %param.10) | copy-start | bytes 9220
  156.7 21.3 %collective-permute-start.3 = (bf16[2,128,768]{2,1,0:T(8,128)(2,1)S(1)}, bf16[2,128,768]{2,1,0:T(8,128)(2,1)S(1)}, u32[]{:S(2)}, u32[]{:S(2)}) collective-permute-start(bf16[2,128,768]{2,1,0:T(8,128)(2,1)S(1)} %add_convert_fusion.1), channel_id=1, source_target_pairs={{0,64},{4,68},{8,72},{12,76},{16,80},{20,84},{24,88},{28,92},{32,9... | collective-permute-start | bytes 1179656 | tf_op jit(solution)/shard_map/ppermute | solution.py:10
  161.1 19.4 %collective-permute-start.2 = (bf16[2,128,768]{2,1,0:T(8,128)(2,1)S(1)}, bf16[2,128,768]{2,1,0:T(8,128)(2,1)S(1)}, u32[]{:S(2)}, u32[]{:S(2)}) collective-permute-start(bf16[2,128,768]{2,1,0:T(8,128)(2,1)S(1)} %add_convert_fusion.1), channel_id=1, source_target_pairs={{64,0},{68,4},{72,8},{76,12},{80,16},{84,20},{88,24},{92,28},{96,3... | collective-permute-start | bytes 1179656 | tf_op jit(solution)/shard_map/ppermute | solution.py:10
Sparse Core Ops, SparseCore 0:
  10.1 98.6 all-gather.4
  110.9 41.9 all-gather.2
where the time goes:
time: 299 us
  waiting for transfers between devices  142 us (47%)
  blocking collectives  106 us (35%)
  matrix products  19.1 us (6%)
  between operations  14.2 us (5%)
  starting transfers between devices  13.3 us (4%)
  other arithmetic  4.61 us (2%)
    psum x1, blocking collectives, body(): totals = lax.psum((first_sum, second_sum), ('seq', 'fsdp'))  106 us
    all_gather x1, waiting for transfers between devices, body(): lax.all_gather(dilated_weight, 'fsdp', axis=1, tiled=True)  91.2 us
    all_gather x1, waiting for transfers between devices, body(): lax.all_gather(w_project, 'fsdp', axis=0, tiled=True)  36.3 us
    ppermute x4, starting transfers between devices, shifted(): lax.ppermute(value, axis, [(source, source + steps) for source in range(i...  13.3 us
    ppermute x4, waiting for transfers between devices, shifted(): lax.ppermute(value, axis, [(source, source + steps) for source in range(i...  13.1 us
  transfers between devices with their start and end apart: 6, of which 3 were waited for; matrix products, arithmetic and copies ran while one was open for 5% of the time, Pallas kernels for 0%

commit v1 on v0

v1 whole, which is shorter than its diff:
```python
import jax
import jax.numpy as jnp
import numpy as np
from jax import lax
from jax.sharding import Mesh
from jax.sharding import PartitionSpec as P

AXES = ("x", "yh", "z", "yl", "c")
SIZES = (4, 2, 16, 2, 2)
SEQ = ("x", "yh", "z")
FSDP = ("yl", "c")


def permute(value, target):
    pairs = []
    for place in np.ndindex(*SIZES):
        to = target(*place)
        if to is not None:
            pairs.append(
                (int(np.ravel_multi_index(place, SIZES)), int(np.ravel_multi_index(to, SIZES)))
            )
    return lax.ppermute(value, AXES, pairs)


def along_y(steps):
    def target(x, yh, z, yl, c):
        y = (2 * yh + yl + steps) % 4
        return (x, y // 2, z, y % 2, c)

    return target


def sister(x, yh, z, yl, c):
    return (x, yh, z, yl, 1 - c)


def along_bins(steps):
    def target(x, yh, z, yl, c):
        k = 2 * x + yh + steps
        return (k // 2, k % 2, z, yl, c) if 0 <= k < 8 else None

    return target


def total(value, axes):
    count = lax.axis_size(axes)
    copies = lax.optimization_barrier(jnp.broadcast_to(value[None], (count,) + value.shape))
    return jnp.sum(lax.all_to_all(copies, axes, 0, 0), axis=0)


def norm_act(values, factor):
    centre = values - jnp.mean(values, axis=-1, keepdims=True)
    spread = jnp.mean(centre * centre, axis=-1, keepdims=True)
    return jax.nn.gelu(centre * lax.rsqrt(spread + 1e-05) * factor)


def dot(a, b):
    return lax.dot_general(a, b, (((1,), (0,)), ((), ())), preferred_element_type=jnp.float32)


def dot_t(a, b):
    return lax.dot_general(a, b, (((1,), (1,)), ((), ())), preferred_element_type=jnp.float32)


def body(block_input, weight, project, gain_first, gain_second, grad_output):
    samples, bins, channels = block_input.shape
    rows = samples * bins
    part = weight.shape[1]
    part_h = project.shape[0]
    inputs = block_input.reshape(rows, channels)
    cotangent = grad_output.reshape(rows, channels)

    own = lax.axis_index(FSDP)
    order = [own, own ^ 1, own ^ 2, own ^ 3]

    w_up = permute(weight[:, : part // 2], along_y(1))
    w_down = permute(weight[:, part // 2 :], along_y(-1))
    w_sister = permute(weight, sister)
    p_up = permute(project[: part_h // 2], along_y(1))
    p_down = permute(project[part_h // 2 :], along_y(-1))
    p_sister = permute(project, sister)
    w_all = jnp.concatenate(
        [weight, w_sister, w_up, w_down, permute(w_up, sister), permute(w_down, sister)], axis=1
    )
    p_all = jnp.concatenate(
        [project, p_sister, p_up, p_down, permute(p_up, sister), permute(p_down, sister)], axis=0
    )

    def reorder(value, width):
        return jnp.concatenate(
            [lax.dynamic_slice_in_dim(value, f * width, width, axis=1) for f in order], axis=1
        )

    widened = inputs.astype(jnp.float32)
    hidden = norm_act(widened, gain_first).astype(jnp.bfloat16)
    hidden = reorder(hidden, part)
    lagging = permute(hidden, along_bins(1))
    leading = permute(hidden, along_bins(-1))
    mixed = dot(lagging, w_all[0]) + dot(hidden, w_all[1]) + dot(leading, w_all[2])
    mixed = mixed.astype(jnp.bfloat16)
    grad_hidden2 = reorder(dot_t(cotangent, p_all), part_h)
    unused, pull_second = jax.vjp(norm_act, mixed.astype(jnp.float32), gain_second)
    grad_mixed, second = pull_second(grad_hidden2)
    grad_mixed = grad_mixed.astype(jnp.bfloat16)
    ahead = permute(grad_mixed, along_bins(-1))
    behind = permute(grad_mixed, along_bins(1))
    grad_hidden = dot_t(ahead, w_all[0]) + dot_t(grad_mixed, w_all[1]) + dot_t(behind, w_all[2])
    grad_hidden = reorder(grad_hidden, part)
    unused2, pull_first = jax.vjp(norm_act, widened, gain_first)
    grad_branch, first = pull_first(grad_hidden)
    grad_input = (cotangent.astype(jnp.float32) + grad_branch).astype(jnp.bfloat16)

    sums = jnp.concatenate([first, second]).reshape(-1, 128)
    sums = total(total(sums, ("x", "yh", "yl", "c")), "z").reshape(-1)
    return (grad_input.reshape(block_input.shape), sums[:channels], sums[channels:])


def solution(mesh):
    fine = Mesh(mesh.devices.reshape(SIZES), AXES)
    in_specs = (
        P(FSDP, SEQ, None),
        P(None, FSDP, None),
        P(FSDP, None),
        P(),
        P(),
        P(FSDP, SEQ, None),
    )
    out_specs = (P(FSDP, SEQ, None), P(), P())
    return jax.shard_map(body, mesh=fine, in_specs=in_specs, out_specs=out_specs, check_vma=False)
```

time: 299 us -> 187 us (0.63); the launches traced: 299 us -> 184 us
  blocking collectives: 106 us -> 0 us
  waiting for transfers between devices: 142 us -> 71.9 us
  starting transfers between devices: 13.3 us -> 81.5 us
  between operations: 14.2 us -> 1.22 us
  matrix products: 19.1 us -> 6.47 us
  local copies, waits for them, and re-layouts: 0.02 us -> 12.5 us
  other arithmetic: 4.61 us -> 10.1 us
    all_gather x2 -> x0, waiting for transfers between devices: 128 us -> none  [the longest x1 91.2 us: body(): lax.all_gather(dilated_weight, 'fsdp', axis=1, tiled=True)]
    psum x1 -> x0, blocking collectives: 106 us -> none  [body(): totals = lax.psum((first_sum, second_sum), ('seq', 'fsdp'))]
    ppermute x4 -> x14, waiting for transfers between devices: 13.1 us -> 51.8 us  [permute(): return lax.ppermute(value, AXES, pairs)]
    all_to_all x0 -> x2, starting transfers between devices: none -> 34.5 us  [total(): return jnp.sum(lax.all_to_all(copies, axes, 0, 0), axis=0)]
    ppermute x4 -> x14, starting transfers between devices: 13.3 us -> 47 us  [permute(): return lax.ppermute(value, AXES, pairs)]
    all_to_all x0 -> x2, waiting for transfers between devices: none -> 20.1 us  [total(): return jnp.sum(lax.all_to_all(copies, axes, 0, 0), axis=0)]
    dot_general x7, matrix products: 19.1 us -> 6.47 us  [the longest x4 3.27 us: dot_t(): lax.dot_general(a, b, (((1,), (1,)), ((), ())), preferred_element_type=jn...]
    unnamed x8 -> x28, local copies, waits for them, and re-layouts: 0.02 us -> 5.13 us
  transfers between devices with their start and end apart: 6 -> 16, of which waited for: 3 -> 5; matrix products, arithmetic and copies ran while one was open for 5% -> 8% of each run, Pallas kernels for 0% -> 0%
where the time goes in v1:
time: 187 us; the launch traced here: 184 us
  starting transfers between devices  81.5 us (44%)
  waiting for transfers between devices  71.9 us (38%)
  local copies, waits for them, and re-layouts  12.5 us (7%)
  other arithmetic  10.1 us (5%)
  matrix products  6.47 us (3%)
    ppermute x14, waiting for transfers between devices, permute(): return lax.ppermute(value, AXES, pairs)  51.8 us
    ppermute x14, starting transfers between devices, permute(): return lax.ppermute(value, AXES, pairs)  47 us
    all_to_all x2, starting transfers between devices, total(): return jnp.sum(lax.all_to_all(copies, axes, 0, 0), axis=0)  34.5 us
    all_to_all x2, waiting for transfers between devices, total(): return jnp.sum(lax.all_to_all(copies, axes, 0, 0), axis=0)  20.1 us
    unnamed x28, local copies, waits for them, and re-layouts  5.13 us
    reduce_sum x4, other arithmetic, norm_act(): return jax.nn.gelu(centre * lax.rsqrt(spread + 1e-05) * factor)  4.15 us
  transfers between devices with their start and end apart: 16, of which 5 were waited for; matrix products, arithmetic and copies ran while one was open for 8% of the time, Pallas kernels for 0%

profile of v1, /device:TPU:1, one launch (start us, length us, event | category | flops | bytes accessed | tf_op | source)
XLA Modules:
  0.0 183.7 jit_solution(10426003999776991398)
XLA Ops:
  0.6 8.9 %collective-permute-start.6 = (bf16[3,384,768]{2,1,0:T(8,128)(2,1)}, bf16[3,384,768]{2,1,0:T(8,128)(2,1)S(1)}, u32[]{:S(2)}, u32[]{:S(2)}) collective-permute-start(bf16[3,384,768]{2,1,0:T(8,128)(2,1)} %param.7), channel_id=1, source_target_pairs={{0,1},{1,0},{2,3},{3,2},{4,5},{5,4},{6,7},{7,6},{8,9},{9,8},{10,11... | collective-permute-start | bytes 5308424 | tf_op jit(solution)/shard_map/ppermute | solution.py:22
  9.6 2.8 %fusion.40 = (bf16[3,192,768]{2,1,0:T(8,128)(2,1)}, bf16[3,192,768]{2,1,0:T(8,128)(2,1)}) fusion(bf16[3,384,768]{2,1,0:T(8,128)(2,1)} %param.7), kind=kLoop, calls=%fused_computation.97 | loop fusion | bytes 3538944 | tf_op jit(solution)/shard_map/slice | solution.py:77
  12.4 2.0 %collective-permute-start.7 = (bf16[3,192,768]{2,1,0:T(8,128)(2,1)}, bf16[3,192,768]{2,1,0:T(8,128)(2,1)}, u32[]{:S(2)}, u32[]{:S(2)}) collective-permute-start(bf16[3,192,768]{2,1,0:T(8,128)(2,1)} %get-tuple-element.12), channel_id=1, source_target_pairs={{0,2},{1,3},{2,64},{3,65},{4,6},{5,7},{6,68},{7,69},{8,10},{9,11},... | collective-permute-start | bytes 2654216 | tf_op jit(solution)/shard_map/ppermute | solution.py:22
  14.4 1.9 %collective-permute-start = (bf16[192,1536]{1,0:T(8,128)(2,1)S(1)}, bf16[192,1536]{1,0:T(8,128)(2,1)}, u32[]{:S(2)}, u32[]{:S(2)}) collective-permute-start(bf16[192,1536]{1,0:T(8,128)(2,1)S(1)} %copy-done.2), channel_id=1, source_target_pairs={{0,1},{1,0},{2,3},{3,2},{4,5},{5,4},{6,7},{7,6},{8,9},{9,8},{10,11... | collective-permute-start | bytes 1769480 | tf_op jit(solution)/shard_map/ppermute | solution.py:22
  17.2 1.9 %collective-permute-start.1 = (bf16[96,1536]{1,0:T(8,128)(2,1)}, bf16[96,1536]{1,0:T(8,128)(2,1)}, u32[]{:S(2)}, u32[]{:S(2)}) collective-permute-start(bf16[96,1536]{1,0:T(8,128)(2,1)} %get-tuple-element.26), channel_id=1, source_target_pairs={{0,2},{1,3},{2,64},{3,65},{4,6},{5,7},{6,68},{7,69},{8,10},{9,11},... | collective-permute-start | bytes 884744 | tf_op jit(solution)/shard_map/ppermute | solution.py:22
  19.1 4.9 %collective-permute-start.2 = (bf16[96,1536]{1,0:T(8,128)(2,1)}, bf16[96,1536]{1,0:T(8,128)(2,1)S(1)}, u32[]{:S(2)}, u32[]{:S(2)}) collective-permute-start(bf16[96,1536]{1,0:T(8,128)(2,1)} %get-tuple-element.25), channel_id=1, source_target_pairs={{0,66},{1,67},{2,0},{3,1},{4,70},{5,71},{6,4},{7,5},{8,74},{9,75},... | collective-permute-start | bytes 884744 | tf_op jit(solution)/shard_map/ppermute | solution.py:22
  27.1 16.4 %collective-permute-done.1 = bf16[96,1536]{1,0:T(8,128)(2,1)} collective-permute-done((bf16[96,1536]{1,0:T(8,128)(2,1)}, bf16[96,1536]{1,0:T(8,128)(2,1)}, u32[]{:S(2)}, u32[]{:S(2)}) %collective-permute-start.1) | collective-permute-done | bytes 294944 | tf_op jit(solution)/shard_map/ppermute | solution.py:22
  43.5 2.0 %collective-permute-start.8 = (bf16[3,192,768]{2,1,0:T(8,128)(2,1)S(1)}, bf16[3,192,768]{2,1,0:T(8,128)(2,1)S(1)}, u32[]{:S(2)}, u32[]{:S(2)}) collective-permute-start(bf16[3,192,768]{2,1,0:T(8,128)(2,1)S(1)} %copy-done.3), channel_id=1, source_target_pairs={{0,66},{1,67},{2,0},{3,1},{4,70},{5,71},{6,4},{7,5},{8,74},{9,75},... | collective-permute-start | bytes 2654216 | tf_op jit(solution)/shard_map/ppermute | solution.py:22
  45.5 2.7 %collective-permute-start.3 = (bf16[96,1536]{1,0:T(8,128)(2,1)}, bf16[96,1536]{1,0:T(8,128)(2,1)S(1)}, u32[]{:S(2)}, u32[]{:S(2)}) collective-permute-start(bf16[96,1536]{1,0:T(8,128)(2,1)} %collective-permute-done.1), channel_id=1, source_target_pairs={{0,1},{1,0},{2,3},{3,2},{4,5},{5,4},{6,7},{7,6},{8,9},{9,8},{10,11... | collective-permute-start | bytes 884744 | tf_op jit(solution)/shard_map/ppermute | solution.py:22
  48.3 1.9 %collective-permute-start.4 = (bf16[96,1536]{1,0:T(8,128)(2,1)S(1)}, bf16[96,1536]{1,0:T(8,128)(2,1)S(1)}, u32[]{:S(2)}, u32[]{:S(2)}) collective-permute-start(bf16[96,1536]{1,0:T(8,128)(2,1)S(1)} %collective-permute-done.2), channel_id=1, source_target_pairs={{0,1},{1,0},{2,3},{3,2},{4,5},{5,4},{6,7},{7,6},{8,9},{9,8},{10,11... | collective-permute-start | bytes 884744 | tf_op jit(solution)/shard_map/ppermute | solution.py:22
  53.7 5.5 %collective-permute-start.5 = (bf16[256,1536]{1,0:T(8,128)(2,1)S(1)}, bf16[256,1536]{1,0:T(8,128)(2,1)S(1)}, u32[]{:S(2)}, u32[]{:S(2)}) collective-permute-start(bf16[256,1536]{1,0:T(8,128)(2,1)S(1)} %pad_maximum_fusion.2), channel_id=1, source_target_pairs={{0,64},{1,65},{2,66},{3,67},{4,68},{5,69},{6,70},{7,71},{8,72},{9,... | collective-permute-start | bytes 2359304 | tf_op jit(solution)/shard_map/ppermute | solution.py:22
  59.2 3.0 %collective-permute-start.9 = (bf16[3,192,768]{2,1,0:T(8,128)(2,1)}, bf16[3,192,768]{2,1,0:T(8,128)(2,1)S(1)}, u32[]{:S(2)}, u32[]{:S(2)}) collective-permute-start(bf16[3,192,768]{2,1,0:T(8,128)(2,1)} %collective-permute-done.7), channel_id=1, source_target_pairs={{0,1},{1,0},{2,3},{3,2},{4,5},{5,4},{6,7},{7,6},{8,9},{9,8},{10,11... | collective-permute-start | bytes 2654216 | tf_op jit(solution)/shard_map/ppermute | solution.py:22
  62.2 20.5 %collective-permute-done.8 = bf16[3,192,768]{2,1,0:T(8,128)(2,1)S(1)} collective-permute-done((bf16[3,192,768]{2,1,0:T(8,128)(2,1)S(1)}, bf16[3,192,768]{2,1,0:T(8,128)(2,1)S(1)}, u32[]{:S(2)}, u32[]{:S(2)}) %collective-permute-start.8) | collective-permute-done | bytes 884768 | tf_op jit(solution)/shard_map/ppermute | solution.py:22
  82.7 4.9 %collective-permute-start.10 = (bf16[3,192,768]{2,1,0:T(8,128)(2,1)S(1)}, bf16[3,192,768]{2,1,0:T(8,128)(2,1)S(1)}, u32[]{:S(2)}, u32[]{:S(2)}) collective-permute-start(bf16[3,192,768]{2,1,0:T(8,128)(2,1)S(1)} %collective-permute-done.8), channel_id=1, source_target_pairs={{0,1},{1,0},{2,3},{3,2},{4,5},{5,4},{6,7},{7,6},{8,9},{9,8},{10,11... | collective-permute-start | bytes 2654216 | tf_op jit(solution)/shard_map/ppermute | solution.py:22
  95.0 4.5 %collective-permute-start.13 = (bf16[256,768]{0,1:T(8,128)(2,1)S(1)}, bf16[256,768]{0,1:T(8,128)(2,1)S(1)}, u32[]{:S(2)}, u32[]{:S(2)}) collective-permute-start(bf16[256,768]{0,1:T(8,128)(2,1)S(1)} %add_convert_fusion.1), channel_id=1, source_target_pairs={{0,64},{1,65},{2,66},{3,67},{4,68},{5,69},{6,70},{7,71},{8,72},{9,... | collective-permute-start | bytes 1179656 | tf_op jit(solution)/shard_map/ppermute | solution.py:22
  99.5 1.5 collective-permute-start.12
  101.0 14.9 %collective-permute-done.13 = bf16[256,768]{0,1:T(8,128)(2,1)S(1)} collective-permute-done((bf16[256,768]{0,1:T(8,128)(2,1)S(1)}, bf16[256,768]{0,1:T(8,128)(2,1)S(1)}, u32[]{:S(2)}, u32[]{:S(2)}) %collective-permute-start.13) | collective-permute-done | bytes 393248 | tf_op jit(solution)/shard_map/ppermute | solution.py:22
  118.6 1.7 multiply_reduce_fusion.1
  122.4 19.6 %all-to-all-start = ((f32[32,18,128]{2,1,0:T(8,128)}), f32[32,18,128]{2,1,0:T(8,128)S(1)}, u32[]{:S(2)}, u32[]{:S(2)}) async-start(f32[32,18,128]{2,1,0:T(8,128)} %broadcast_in_dim.19), calls=%async_computation | async-start | bytes 786432 | tf_op jit(solution)/shard_map/all_to_all | solution.py:48
  143.2 9.1 %all-to-all-done = f32[32,18,128]{2,1,0:T(8,128)S(1)} async-done(((f32[32,18,128]{2,1,0:T(8,128)}), f32[32,18,128]{2,1,0:T(8,128)S(1)}, u32[]{:S(2)}, u32[]{:S(2)}) %all-to-all-start) | async-done | bytes 294944 | tf_op jit(solution)/shard_map/all_to_all | solution.py:48
  152.9 1.4 broadcast_in_dim.40
  154.3 14.9 %all-to-all-start.1 = ((f32[16,18,128]{2,1,0:T(8,128)}), f32[16,18,128]{2,1,0:T(8,128)S(1)}, u32[]{:S(2)}, u32[]{:S(2)}) async-start(f32[16,18,128]{2,1,0:T(8,128)} %broadcast_in_dim.40), calls=%async_computation.1 | async-start | bytes 393216 | tf_op jit(solution)/shard_map/all_to_all | solution.py:48
  169.2 2.2 %add_convert_fusion = bf16[2,128,1536]{2,1,0:T(8,128)(2,1)} fusion(bf16[2,128,1536]{2,1,0:T(8,128)(2,1)S(1)} %copy-done.5, f32[2,128]{1,0:T(2,128)} %negate_multiply_fusion, f32[2,128]{1,0:T(2,128)} %copy-done.8, f32[2,128]{1,0:T(2,128)S(1)} %get-tuple-element.28, bf16[2,128,1536]{2,1,0:T(8,128)(2,1)S(1)} %copy-done, f32[2,128]{1,0:T(2,128)S(1)} %get-tuple-element.30, ...), kind=kLoop, calls=%fused_computation.33 | loop fusion | flops 4325376 | bytes 3942400 | tf_op jit(solution)/shard_map/convert_element_type | solution.py:111
  171.4 11.0 %all-to-all-done.1 = f32[16,18,128]{2,1,0:T(8,128)S(1)} async-done(((f32[16,18,128]{2,1,0:T(8,128)}), f32[16,18,128]{2,1,0:T(8,128)S(1)}, u32[]{:S(2)}, u32[]{:S(2)}) %all-to-all-start.1) | async-done | bytes 147488 | tf_op jit(solution)/shard_map/all_to_all | solution.py:48
  (76 shorter events, 22.3 us)
Async XLA Ops:
  0.6 13.8 %copy-start.2 = (bf16[192,1536]{1,0:T(8,128)(2,1)S(1)}, bf16[192,1536]{1,0:T(8,128)(2,1)}, u32[]{:S(2)}) copy-start(bf16[192,1536]{1,0:T(8,128)(2,1)} %param.8) | copy-start | bytes 1769476
  0.6 23.4 %copy-start = (bf16[2,128,1536]{2,1,0:T(8,128)(2,1)S(1)}, bf16[2,128,1536]{2,1,0:T(8,128)(2,1)}, u32[]{:S(2)}) copy-start(bf16[2,128,1536]{2,1,0:T(8,128)(2,1)} %param.6) | copy-start | bytes 2359300
  0.6 87.9 %collective-permute-start.6 = (bf16[3,384,768]{2,1,0:T(8,128)(2,1)}, bf16[3,384,768]{2,1,0:T(8,128)(2,1)S(1)}, u32[]{:S(2)}, u32[]{:S(2)}) collective-permute-start(bf16[3,384,768]{2,1,0:T(8,128)(2,1)} %param.7), channel_id=1, source_target_pairs={{0,1},{1,0},{2,3},{3,2},{4,5},{5,4},{6,7},{7,6},{8,9},{9,8},{10,11... | collective-permute-start | bytes 5308424 | tf_op jit(solution)/shard_map/ppermute | solution.py:22
  12.4 12.3 %copy-start.6 = (f32[1536]{0:T(1024)S(1)}, f32[1536]{0:T(1024)}, u32[]{:S(2)}) copy-start(f32[1536]{0:T(1024)} %param.9) | copy-start | bytes 18436
  12.4 46.9 %collective-permute-start.7 = (bf16[3,192,768]{2,1,0:T(8,128)(2,1)}, bf16[3,192,768]{2,1,0:T(8,128)(2,1)}, u32[]{:S(2)}, u32[]{:S(2)}) collective-permute-start(bf16[3,192,768]{2,1,0:T(8,128)(2,1)} %get-tuple-element.12), channel_id=1, source_target_pairs={{0,2},{1,3},{2,64},{3,65},{4,6},{5,7},{6,68},{7,69},{8,10},{9,11},... | collective-permute-start | bytes 2654216 | tf_op jit(solution)/shard_map/ppermute | solution.py:22
  14.4 33.8 %collective-permute-start = (bf16[192,1536]{1,0:T(8,128)(2,1)S(1)}, bf16[192,1536]{1,0:T(8,128)(2,1)}, u32[]{:S(2)}, u32[]{:S(2)}) collective-permute-start(bf16[192,1536]{1,0:T(8,128)(2,1)S(1)} %copy-done.2), channel_id=1, source_target_pairs={{0,1},{1,0},{2,3},{3,2},{4,5},{5,4},{6,7},{7,6},{8,9},{9,8},{10,11... | collective-permute-start | bytes 1769480 | tf_op jit(solution)/shard_map/ppermute | solution.py:22
  17.2 26.3 %collective-permute-start.1 = (bf16[96,1536]{1,0:T(8,128)(2,1)}, bf16[96,1536]{1,0:T(8,128)(2,1)}, u32[]{:S(2)}, u32[]{:S(2)}) collective-permute-start(bf16[96,1536]{1,0:T(8,128)(2,1)} %get-tuple-element.26), channel_id=1, source_target_pairs={{0,2},{1,3},{2,64},{3,65},{4,6},{5,7},{6,68},{7,69},{8,10},{9,11},... | collective-permute-start | bytes 884744 | tf_op jit(solution)/shard_map/ppermute | solution.py:22
  19.1 26.4 %collective-permute-start.2 = (bf16[96,1536]{1,0:T(8,128)(2,1)}, bf16[96,1536]{1,0:T(8,128)(2,1)S(1)}, u32[]{:S(2)}, u32[]{:S(2)}) collective-permute-start(bf16[96,1536]{1,0:T(8,128)(2,1)} %get-tuple-element.25), channel_id=1, source_target_pairs={{0,66},{1,67},{2,0},{3,1},{4,70},{5,71},{6,4},{7,5},{8,74},{9,75},... | collective-permute-start | bytes 884744 | tf_op jit(solution)/shard_map/ppermute | solution.py:22
  25.5 1.5 copy-start.1
  27.0 16.5 %copy-start.3 = (bf16[3,192,768]{2,1,0:T(8,128)(2,1)S(1)}, bf16[3,192,768]{2,1,0:T(8,128)(2,1)}, u32[]{:S(2)}) copy-start(bf16[3,192,768]{2,1,0:T(8,128)(2,1)} %get-tuple-element.11) | copy-start | bytes 2654212
  43.5 44.1 %copy-start.4 = (bf16[2,128,1536]{2,1,0:T(8,128)(2,1)S(1)}, bf16[2,128,1536]{2,1,0:T(8,128)(2,1)}, u32[]{:S(2)}) copy-start(bf16[2,128,1536]{2,1,0:T(8,128)(2,1)} %param.11) | copy-start | bytes 2359300
  43.5 39.2 %collective-permute-start.8 = (bf16[3,192,768]{2,1,0:T(8,128)(2,1)S(1)}, bf16[3,192,768]{2,1,0:T(8,128)(2,1)S(1)}, u32[]{:S(2)}, u32[]{:S(2)}) collective-permute-start(bf16[3,192,768]{2,1,0:T(8,128)(2,1)S(1)} %copy-done.3), channel_id=1, source_target_pairs={{0,66},{1,67},{2,0},{3,1},{4,70},{5,71},{6,4},{7,5},{8,74},{9,75},... | collective-permute-start | bytes 2654216 | tf_op jit(solution)/shard_map/ppermute | solution.py:22
  45.5 6.8 %collective-permute-start.3 = (bf16[96,1536]{1,0:T(8,128)(2,1)}, bf16[96,1536]{1,0:T(8,128)(2,1)S(1)}, u32[]{:S(2)}, u32[]{:S(2)}) collective-permute-start(bf16[96,1536]{1,0:T(8,128)(2,1)} %collective-permute-done.1), channel_id=1, source_target_pairs={{0,1},{1,0},{2,3},{3,2},{4,5},{5,4},{6,7},{7,6},{8,9},{9,8},{10,11... | collective-permute-start | bytes 884744 | tf_op jit(solution)/shard_map/ppermute | solution.py:22
  48.3 5.4 %collective-permute-start.4 = (bf16[96,1536]{1,0:T(8,128)(2,1)S(1)}, bf16[96,1536]{1,0:T(8,128)(2,1)S(1)}, u32[]{:S(2)}, u32[]{:S(2)}) collective-permute-start(bf16[96,1536]{1,0:T(8,128)(2,1)S(1)} %collective-permute-done.2), channel_id=1, source_target_pairs={{0,1},{1,0},{2,3},{3,2},{4,5},{5,4},{6,7},{7,6},{8,9},{9,8},{10,11... | collective-permute-start | bytes 884744 | tf_op jit(solution)/shard_map/ppermute | solution.py:22
  52.3 37.8 %collective-permute-start.11 = (bf16[256,1536]{1,0:T(8,128)(2,1)S(1)}, bf16[256,1536]{1,0:T(8,128)(2,1)S(1)}, u32[]{:S(2)}, u32[]{:S(2)}) collective-permute-start(bf16[256,1536]{1,0:T(8,128)(2,1)S(1)} %pad_maximum_fusion.2), channel_id=1, source_target_pairs={{64,0},{65,1},{66,2},{67,3},{68,4},{69,5},{70,6},{71,7},{72,8},{73... | collective-permute-start | bytes 2359304 | tf_op jit(solution)/shard_map/ppermute | solution.py:22
  53.7 37.5 %collective-permute-start.5 = (bf16[256,1536]{1,0:T(8,128)(2,1)S(1)}, bf16[256,1536]{1,0:T(8,128)(2,1)S(1)}, u32[]{:S(2)}, u32[]{:S(2)}) collective-permute-start(bf16[256,1536]{1,0:T(8,128)(2,1)S(1)} %pad_maximum_fusion.2), channel_id=1, source_target_pairs={{0,64},{1,65},{2,66},{3,67},{4,68},{5,69},{6,70},{7,71},{8,72},{9,... | collective-permute-start | bytes 2359304 | tf_op jit(solution)/shard_map/ppermute | solution.py:22
  59.2 30.7 %collective-permute-start.9 = (bf16[3,192,768]{2,1,0:T(8,128)(2,1)}, bf16[3,192,768]{2,1,0:T(8,128)(2,1)S(1)}, u32[]{:S(2)}, u32[]{:S(2)}) collective-permute-start(bf16[3,192,768]{2,1,0:T(8,128)(2,1)} %collective-permute-done.7), channel_id=1, source_target_pairs={{0,1},{1,0},{2,3},{3,2},{4,5},{5,4},{6,7},{7,6},{8,9},{9,8},{10,11... | collective-permute-start | bytes 2654216 | tf_op jit(solution)/shard_map/ppermute | solution.py:22
  82.7 7.3 %collective-permute-start.10 = (bf16[3,192,768]{2,1,0:T(8,128)(2,1)S(1)}, bf16[3,192,768]{2,1,0:T(8,128)(2,1)S(1)}, u32[]{:S(2)}, u32[]{:S(2)}) collective-permute-start(bf16[3,192,768]{2,1,0:T(8,128)(2,1)S(1)} %collective-permute-done.8), channel_id=1, source_target_pairs={{0,1},{1,0},{2,3},{3,2},{4,5},{5,4},{6,7},{7,6},{8,9},{9,8},{10,11... | collective-permute-start | bytes 2654216 | tf_op jit(solution)/shard_map/ppermute | solution.py:22
  95.0 20.9 %collective-permute-start.13 = (bf16[256,768]{0,1:T(8,128)(2,1)S(1)}, bf16[256,768]{0,1:T(8,128)(2,1)S(1)}, u32[]{:S(2)}, u32[]{:S(2)}) collective-permute-start(bf16[256,768]{0,1:T(8,128)(2,1)S(1)} %add_convert_fusion.1), channel_id=1, source_target_pairs={{0,64},{1,65},{2,66},{3,67},{4,68},{5,69},{6,70},{7,71},{8,72},{9,... | collective-permute-start | bytes 1179656 | tf_op jit(solution)/shard_map/ppermute | solution.py:22
  99.5 17.2 %collective-permute-start.12 = (bf16[256,768]{0,1:T(8,128)(2,1)S(1)}, bf16[256,768]{0,1:T(8,128)(2,1)S(1)}, u32[]{:S(2)}, u32[]{:S(2)}) collective-permute-start(bf16[256,768]{0,1:T(8,128)(2,1)S(1)} %add_convert_fusion.1), channel_id=1, source_target_pairs={{64,0},{65,1},{66,2},{67,3},{68,4},{69,5},{70,6},{71,7},{72,8},{73... | collective-permute-start | bytes 1179656 | tf_op jit(solution)/shard_map/ppermute | solution.py:22
  120.3 1.3 copy-start.8
  121.6 47.7 %copy-start.5 = (bf16[2,128,1536]{2,1,0:T(8,128)(2,1)S(1)}, bf16[2,128,1536]{2,1,0:T(8,128)(2,1)}, u32[]{:S(2)}) copy-start(bf16[2,128,1536]{2,1,0:T(8,128)(2,1)} %param.11) | copy-start | bytes 2359300
  122.4 29.9 %all-to-all-start = ((f32[32,18,128]{2,1,0:T(8,128)}), f32[32,18,128]{2,1,0:T(8,128)S(1)}, u32[]{:S(2)}, u32[]{:S(2)}) async-start(f32[32,18,128]{2,1,0:T(8,128)} %broadcast_in_dim.19), calls=%async_computation | async-start | bytes 786432 | tf_op jit(solution)/shard_map/all_to_all | solution.py:48
  154.3 28.2 %all-to-all-start.1 = ((f32[16,18,128]{2,1,0:T(8,128)}), f32[16,18,128]{2,1,0:T(8,128)S(1)}, u32[]{:S(2)}, u32[]{:S(2)}) async-start(f32[16,18,128]{2,1,0:T(8,128)} %broadcast_in_dim.40), calls=%async_computation.1 | async-start | bytes 393216 | tf_op jit(solution)/shard_map/all_to_all | solution.py:48
  (1 other events, 1.3 us)

commit v2 on v1

v2 whole, which is shorter than its diff:
```python
import jax
import jax.numpy as jnp
import numpy as np
from jax import lax
from jax.sharding import Mesh
from jax.sharding import PartitionSpec as P

AXES = ("x", "yh", "z", "yl", "c")
SIZES = (4, 2, 16, 2, 2)
SEQ = ("x", "yh", "z")
FSDP = ("yl", "c")
HALF = 0.7978845608028654


def permute(value, target):
    pairs = []
    for place in np.ndindex(*SIZES):
        to = target(*place)
        if to is not None:
            pairs.append(
                (int(np.ravel_multi_index(place, SIZES)), int(np.ravel_multi_index(to, SIZES)))
            )
    return lax.ppermute(value, AXES, pairs)


def along_y(steps):
    def target(x, yh, z, yl, c):
        y = (2 * yh + yl + steps) % 4
        return (x, y // 2, z, y % 2, c)

    return target


def along_z(steps):
    def target(x, yh, z, yl, c):
        return (x, yh, (z + steps) % 16, yl, c)

    return target


def sister(x, yh, z, yl, c):
    return (x, yh, z, yl, 1 - c)


def along_bins(steps):
    def target(x, yh, z, yl, c):
        k = 2 * x + yh + steps
        return (k // 2, k % 2, z, yl, c) if 0 <= k < 8 else None

    return target


def total(value, axes):
    count = lax.axis_size(axes)
    copies = lax.optimization_barrier(jnp.broadcast_to(value[None], (count,) + value.shape))
    return jnp.sum(lax.all_to_all(copies, axes, 0, 0), axis=0)


def normed(values):
    centre = values - jnp.mean(values, axis=-1, keepdims=True)
    spread = jnp.mean(centre * centre, axis=-1, keepdims=True)
    scale = lax.rsqrt(spread + 1e-05)
    return centre * scale, scale


def act(a):
    return 0.5 * a * (1.0 + jnp.tanh(HALF * (a + 0.044715 * a * a * a)))


def slope(a):
    t = jnp.tanh(HALF * (a + 0.044715 * a * a * a))
    return 0.5 * (1.0 + t) + 0.5 * a * (1.0 - t * t) * (HALF * (1.0 + 0.134145 * a * a))


def norm_back(grad, scale, unit):
    return scale * (
        grad
        - jnp.mean(grad, axis=-1, keepdims=True)
        - unit * jnp.mean(grad * unit, axis=-1, keepdims=True)
    )


def dot(a, b):
    return lax.dot_general(a, b, (((1,), (0,)), ((), ())), preferred_element_type=jnp.float32)


def dot_t(a, b):
    return lax.dot_general(a, b, (((1,), (1,)), ((), ())), preferred_element_type=jnp.float32)


def body(block_input, weight, project, gain_first, gain_second, grad_output):
    samples, bins, channels = block_input.shape
    rows = samples * bins
    width = weight.shape[2]
    part = weight.shape[1]
    part_h = project.shape[0]
    inputs = block_input.reshape(rows, channels)
    cotangent = grad_output.reshape(rows, channels)

    own = lax.axis_index(FSDP)
    odd = lax.axis_index("z") % 2

    slabs = jnp.concatenate(
        [weight, jnp.concatenate([project[:, :width], project[:, width:]], axis=0)[None]], axis=0
    )
    up = permute(lax.dynamic_index_in_dim(slabs, 2 * odd, 0, False), along_y(1))
    down = permute(lax.dynamic_index_in_dim(slabs, 2 * odd + 1, 0, False), along_y(-1))
    lagging = permute(inputs, along_bins(1))
    leading = permute(inputs, along_bins(-1))
    slabs_s = permute(slabs, sister)
    up_z = permute(up, along_z(1))
    down_z = permute(down, along_z(-1))
    first = [up, down, up_z, down_z]
    second = [permute(piece, sister) for piece in first]

    def far(pieces, k):
        return jnp.where(odd == 0, pieces[k], pieces[k ^ 2])

    def full(k):
        whole = jnp.zeros((4 * part, width), jnp.bfloat16)
        for piece, f in (
            (slabs[k], own),
            (slabs_s[k], own ^ 1),
            (far(first, k), own ^ 2),
            (far(second, k), own ^ 3),
        ):
            whole = lax.dynamic_update_slice(whole, piece, (f * part, 0))
        return whole

    taps = [full(k) for k in range(3)]
    proj = full(3).reshape(4, 2, part_h, width)
    proj = [proj[:, j].reshape(4 * part_h, width) for j in range(2)]

    grad_hidden2 = dot_t(cotangent[:, :width], proj[0]) + dot_t(cotangent[:, width:], proj[1])

    units, scales, hiddens, weighs, slopes = [], [], [], [], []
    for block in (lagging, inputs, leading):
        unit, scale = normed(block.astype(jnp.float32))
        a = unit * gain_first
        units.append(unit)
        scales.append(scale)
        hiddens.append(act(a).astype(jnp.bfloat16))
        slopes.append(slope(a))
        weighs.append(slopes[-1] * unit)

    mixed = dot(hiddens[1], taps[1]) + dot(hiddens[0], taps[0]) + dot(hiddens[2], taps[2])
    mixed = mixed.astype(jnp.bfloat16).astype(jnp.float32)
    unit2, scale2 = normed(mixed)
    grad_a = grad_hidden2 * slope(unit2 * gain_second)
    second_sum = jnp.sum(grad_a * unit2, axis=0)
    grad_mixed = norm_back(grad_a * gain_second, scale2, unit2).astype(jnp.bfloat16)

    ahead = permute(grad_mixed, along_bins(-1))
    behind = permute(grad_mixed, along_bins(1))

    terms = [dot_t(grad_mixed, tap) for tap in taps]
    first_sum = jnp.sum(terms[0] * weighs[0] + terms[1] * weighs[1] + terms[2] * weighs[2], axis=0)
    sums = jnp.concatenate([first_sum, second_sum]).reshape(-1, 128)
    sums = total(sums, ("x", "yh", "yl", "c"))
    ahead, behind, sums = lax.optimization_barrier((ahead, behind, sums))
    sums = total(sums, "z").reshape(-1)

    grad_hidden = terms[1] + dot_t(ahead, taps[0]) + dot_t(behind, taps[2])
    grad_branch = norm_back(grad_hidden * slopes[1] * gain_first, scales[1], units[1])
    grad_input = (cotangent.astype(jnp.float32) + grad_branch).astype(jnp.bfloat16)
    return (grad_input.reshape(block_input.shape), sums[:channels], sums[channels:])


def solution(mesh):
    fine = Mesh(mesh.devices.reshape(SIZES), AXES)
    in_specs = (
        P(FSDP, SEQ, None),
        P(None, FSDP, None),
        P(FSDP, None),
        P(),
        P(),
        P(FSDP, SEQ, None),
    )
    out_specs = (P(FSDP, SEQ, None), P(), P())
    return jax.shard_map(body, mesh=fine, in_specs=in_specs, out_specs=out_specs, check_vma=False)
```

time: 187 us -> 168 us (0.90)
  waiting for transfers between devices: 71.9 us -> 40.1 us
  starting transfers between devices: 81.5 us -> 55.7 us
  blocking collectives: 0 us -> 17.5 us
  matrix products: 6.47 us -> 21.3 us
  other arithmetic: 10.1 us -> 16.7 us
    all_to_all x2 -> x1, starting transfers between devices: 34.5 us -> 5.53 us  [total(): return jnp.sum(lax.all_to_all(copies, axes, 0, 0), axis=0)]
    ppermute x14 -> x13, waiting for transfers between devices: 51.8 us -> 28.4 us  [permute(): return lax.ppermute(value, AXES, pairs)]
    all_to_all x0 -> x1, blocking collectives: none -> 17.5 us  [total(): return jnp.sum(lax.all_to_all(copies, axes, 0, 0), axis=0)]
    dot_general x4 -> x7, matrix products: 3.27 us -> 14.4 us  [dot_t(): lax.dot_general(a, b, (((1,), (1,)), ((), ())), preferred_element_type=jn...]
    all_to_all x2 -> x1, waiting for transfers between devices: 20.1 us -> 11.7 us  [total(): return jnp.sum(lax.all_to_all(copies, axes, 0, 0), axis=0)]
    dot_general x3, matrix products: 3.2 us -> 6.89 us  [dot(): lax.dot_general(a, b, (((1,), (0,)), ((), ())), preferred_element_type=jn...]
    dynamic_update_slice x0 -> x4, other arithmetic: none -> 3.37 us  [full(): whole = lax.dynamic_update_slice(whole, piece, (f * part, 0))]
    ppermute x14 -> x13, starting transfers between devices: 47 us -> 50.1 us  [permute(): return lax.ppermute(value, AXES, pairs)]
  transfers between devices with their start and end apart: 16 -> 14, of which waited for: 5 -> 3; matrix products, arithmetic and copies ran while one was open for 8% -> 16% of each run, Pallas kernels for 0% -> 0%
where the time goes in v2:
time: 168 us; the launch traced here: 165 us
  starting transfers between devices  55.7 us (33%)
  waiting for transfers between devices  40.1 us (24%)
  matrix products  21.3 us (13%)
  blocking collectives  17.5 us (10%)
  other arithmetic  16.7 us (10%)
  local copies, waits for them, and re-layouts  12.3 us (7%)
    ppermute x13, starting transfers between devices, permute(): return lax.ppermute(value, AXES, pairs)  50.1 us
    ppermute x13, waiting for transfers between devices, permute(): return lax.ppermute(value, AXES, pairs)  28.4 us
    all_to_all x1, blocking collectives, total(): return jnp.sum(lax.all_to_all(copies, axes, 0, 0), axis=0)  17.5 us
    dot_general x7, matrix products, dot_t(): lax.dot_general(a, b, (((1,), (1,)), ((), ())), preferred_element_type=jn...  14.4 us
    all_to_all x1, waiting for transfers between devices, total(): return jnp.sum(lax.all_to_all(copies, axes, 0, 0), axis=0)  11.7 us
    dot_general x3, matrix products, dot(): lax.dot_general(a, b, (((1,), (0,)), ((), ())), preferred_element_type=jn...  6.89 us
    unnamed x44, local copies, waits for them, and re-layouts  5.71 us
    all_to_all x1, starting transfers between devices, total(): return jnp.sum(lax.all_to_all(copies, axes, 0, 0), axis=0)  5.53 us
  transfers between devices with their start and end apart: 14, of which 3 were waited for; matrix products, arithmetic and copies ran while one was open for 16% of the time, Pallas kernels for 0%

profile of v2, /device:TPU:1, one launch (start us, length us, event | category | flops | bytes accessed | tf_op | source)
XLA Modules:
  0.0 165.0 jit_solution(3756639816159021720)
XLA Ops:
  0.6 6.5 %collective-permute-start.5 = (bf16[256,1536]{1,0:T(8,128)(2,1)}, bf16[256,1536]{1,0:T(8,128)(2,1)}, u32[]{:S(2)}, u32[]{:S(2)}) collective-permute-start(bf16[256,1536]{1,0:T(8,128)(2,1)} %bitcast.67), channel_id=1, source_target_pairs={{0,64},{1,65},{2,66},{3,67},{4,68},{5,69},{6,70},{7,71},{8,72},{9,... | collective-permute-start | bytes 2359304 | tf_op jit(solution)/shard_map/ppermute | solution.py:23
  12.5 5.4 %collective-permute-start.1 = (bf16[384,768]{1,0:T(8,128)(2,1)}, bf16[384,768]{1,0:T(8,128)(2,1)}, u32[]{:S(2)}, u32[]{:S(2)}) collective-permute-start(bf16[384,768]{1,0:T(8,128)(2,1)} %get-tuple-element.19), channel_id=1, source_target_pairs={{0,66},{1,67},{2,0},{3,1},{4,70},{5,71},{6,4},{7,5},{8,74},{9,75},... | collective-permute-start | bytes 1769480 | tf_op jit(solution)/shard_map/ppermute | solution.py:23
  19.6 3.4 %collective-permute-start = (bf16[4,384,768]{2,1,0:T(8,128)(2,1)}, bf16[4,384,768]{2,1,0:T(8,128)(2,1)}, u32[]{:S(2)}, u32[]{:S(2)}) collective-permute-start(bf16[4,384,768]{2,1,0:T(8,128)(2,1)} %pad_maximum_fusion), channel_id=1, source_target_pairs={{0,1},{1,0},{2,3},{3,2},{4,5},{5,4},{6,7},{7,6},{8,9},{9,8},{10,11... | collective-permute-start | bytes 7077896 | tf_op jit(solution)/shard_map/ppermute | solution.py:23
  23.0 1.9 %collective-permute-start.6 = (bf16[384,768]{1,0:T(8,128)(2,1)}, bf16[384,768]{1,0:T(8,128)(2,1)}, u32[]{:S(2)}, u32[]{:S(2)}) collective-permute-start(bf16[384,768]{1,0:T(8,128)(2,1)} %get-tuple-element.18), channel_id=1, source_target_pairs={{0,2},{1,3},{2,64},{3,65},{4,6},{5,7},{6,68},{7,69},{8,10},{9,11},... | collective-permute-start | bytes 1769480 | tf_op jit(solution)/shard_map/ppermute | solution.py:23
  31.3 22.1 %collective-permute-done.1 = bf16[384,768]{1,0:T(8,128)(2,1)} collective-permute-done((bf16[384,768]{1,0:T(8,128)(2,1)}, bf16[384,768]{1,0:T(8,128)(2,1)}, u32[]{:S(2)}, u32[]{:S(2)}) %collective-permute-start.1) | collective-permute-done | bytes 589856 | tf_op jit(solution)/shard_map/ppermute | solution.py:23
  53.5 11.1 %collective-permute-start.2 = (bf16[384,768]{1,0:T(8,128)(2,1)}, bf16[384,768]{1,0:T(8,128)(2,1)S(1)}, u32[]{:S(2)}, u32[]{:S(2)}) collective-permute-start(bf16[384,768]{1,0:T(8,128)(2,1)} %collective-permute-done.1), channel_id=1, source_target_pairs={{0,60},{1,61},{2,62},{3,63},{4,0},{5,1},{6,2},{7,3},{8,4},{9,5},{1... | collective-permute-start | bytes 1769480 | tf_op jit(solution)/shard_map/ppermute | solution.py:23
  64.6 3.7 %collective-permute-start.3 = (bf16[384,768]{1,0:T(8,128)(2,1)}, bf16[384,768]{1,0:T(8,128)(2,1)S(1)}, u32[]{:S(2)}, u32[]{:S(2)}) collective-permute-start(bf16[384,768]{1,0:T(8,128)(2,1)} %collective-permute-done.1), channel_id=1, source_target_pairs={{0,1},{1,0},{2,3},{3,2},{4,5},{5,4},{6,7},{7,6},{8,9},{9,8},{10,11... | collective-permute-start | bytes 1769480 | tf_op jit(solution)/shard_map/ppermute | solution.py:23
  68.3 1.9 %collective-permute-start.7 = (bf16[384,768]{1,0:T(8,128)(2,1)}, bf16[384,768]{1,0:T(8,128)(2,1)S(1)}, u32[]{:S(2)}, u32[]{:S(2)}) collective-permute-start(bf16[384,768]{1,0:T(8,128)(2,1)} %collective-permute-done.6), channel_id=1, source_target_pairs={{0,4},{1,5},{2,6},{3,7},{4,8},{5,9},{6,10},{7,11},{8,12},{9,13},{1... | collective-permute-start | bytes 1769480 | tf_op jit(solution)/shard_map/ppermute | solution.py:23
  71.6 1.9 %collective-permute-start.8 = (bf16[384,768]{1,0:T(8,128)(2,1)}, bf16[384,768]{1,0:T(8,128)(2,1)S(1)}, u32[]{:S(2)}, u32[]{:S(2)}) collective-permute-start(bf16[384,768]{1,0:T(8,128)(2,1)} %collective-permute-done.6), channel_id=1, source_target_pairs={{0,1},{1,0},{2,3},{3,2},{4,5},{5,4},{6,7},{7,6},{8,9},{9,8},{10,11... | collective-permute-start | bytes 1769480 | tf_op jit(solution)/shard_map/ppermute | solution.py:23
  77.9 2.4 %collective-permute-start.4 = (bf16[384,768]{1,0:T(8,128)(2,1)S(1)}, bf16[384,768]{1,0:T(8,128)(2,1)S(1)}, u32[]{:S(2)}, u32[]{:S(2)}) collective-permute-start(bf16[384,768]{1,0:T(8,128)(2,1)S(1)} %collective-permute-done.2), channel_id=1, source_target_pairs={{0,1},{1,0},{2,3},{3,2},{4,5},{5,4},{6,7},{7,6},{8,9},{9,8},{10,11... | collective-permute-start | bytes 1769480 | tf_op jit(solution)/shard_map/ppermute | solution.py:23
  80.3 6.3 %collective-permute-done.7 = bf16[384,768]{1,0:T(8,128)(2,1)S(1)} collective-permute-done((bf16[384,768]{1,0:T(8,128)(2,1)}, bf16[384,768]{1,0:T(8,128)(2,1)S(1)}, u32[]{:S(2)}, u32[]{:S(2)}) %collective-permute-start.7) | collective-permute-done | bytes 589856 | tf_op jit(solution)/shard_map/ppermute | solution.py:23
  86.6 2.9 %collective-permute-start.9 = (bf16[384,768]{1,0:T(8,128)(2,1)S(1)}, bf16[384,768]{1,0:T(8,128)(2,1)S(1)}, u32[]{:S(2)}, u32[]{:S(2)}) collective-permute-start(bf16[384,768]{1,0:T(8,128)(2,1)S(1)} %collective-permute-done.7), channel_id=1, source_target_pairs={{0,1},{1,0},{2,3},{3,2},{4,5},{5,4},{6,7},{7,6},{8,9},{9,8},{10,11... | collective-permute-start | bytes 1769480 | tf_op jit(solution)/shard_map/ppermute | solution.py:23
  89.5 2.6 %fusion.90 = (bf16[1536,768]{1,0:T(8,128)(2,1)S(1)}, bf16[1536,768]{1,0:T(8,128)(2,1)S(1)}, bf16[1536,768]{1,0:T(8,128)(2,1)S(1)}, bf16[1536,768]{1,0:T(8,128)(2,1)}) fusion(bf16[1536,768]{1,0:T(8,128)(2,1)S(1)} %copy-done.3, s32[]{:T(128)S(6)} %select_n.75, bf16[4,384,768]{2,1,0:T(8,128)(2,1)} %collective-permute-done, ...), kind=kLoop, calls=%fused_computation.126 | loop fusion | bytes 4718596 | tf_op jit(solution)/shard_map/dynamic_update_slice | solution.py:127
  96.1 3.0 %fusion.52 = f32[256,768]{1,0:T(8,128)S(1)} fusion(bf16[1536,768]{1,0:T(8,128)(2,1)S(1)} %get-tuple-element.26, bf16[256,1536]{1,0:T(8,128)(2,1)} %collective-permute-done.5, f32[256]{0:T(256)S(1)} %add_rsqrt_fusion.2, f32[256]{0:T(256)S(1)} %broadcast_multiply_fusion.6, f32[1536]{0:T(1024)S(1)} %copy-done.17), kind=kOutput, calls=%fused_computation.80 | convolution fusion | flops 609091584 | bytes 3940352 | tf_op jit(solution)/shard_map/dot_general | solution.py:84
  99.1 2.4 %fusion.54 = f32[256,768]{1,0:T(8,128)S(1)} fusion(bf16[1536,768]{1,0:T(8,128)(2,1)S(1)} %get-tuple-element.27, bf16[256,1536]{1,0:T(8,128)(2,1)} %collective-permute-done.10, f32[256]{0:T(256)S(1)} %add_rsqrt_fusion.1, f32[256]{0:T(256)S(1)} %broadcast_multiply_fusion.5, f32[1536]{0:T(1024)S(1)} %copy-done.17), kind=kOutput, calls=%fused_computation.81 | convolution fusion | flops 609091584 | bytes 3940352 | tf_op jit(solution)/shard_map/dot_general | solution.py:84
  106.0 1.8 %fusion.113 = f32[256,1536]{1,0:T(8,128)S(1)} fusion(bf16[256,768]{1,0:T(8,128)(2,1)} %multiply_convert_fusion.2, bf16[1536,768]{1,0:T(8,128)(2,1)S(1)} %get-tuple-element.22), kind=kOutput, calls=%fused_computation.176 | convolution fusion | flops 603979776 | bytes 4325376 | tf_op jit(solution)/shard_map/dot_general | solution.py:88
  109.1 6.3 %collective-permute-start.12 = (bf16[256,768]{1,0:T(8,128)(2,1)}, bf16[256,768]{1,0:T(8,128)(2,1)}, u32[]{:S(2)}, u32[]{:S(2)}) collective-permute-start(bf16[256,768]{1,0:T(8,128)(2,1)} %multiply_convert_fusion.2), channel_id=1, source_target_pairs={{0,64},{1,65},{2,66},{3,67},{4,68},{5,69},{6,70},{7,71},{8,72},{9,... | collective-permute-start | bytes 1179656 | tf_op jit(solution)/shard_map/ppermute | solution.py:23
  115.4 2.8 %convolution_multiply_fusion = f32[256,1536]{1,0:T(8,128)S(1)} fusion(bf16[256,768]{1,0:T(8,128)(2,1)} %multiply_convert_fusion.2, bf16[1536,768]{1,0:T(8,128)(2,1)S(1)} %get-tuple-element.27, bf16[256,1536]{1,0:T(8,128)(2,1)} %collective-permute-done.10, f32[256]{0:T(256)S(1)} %add_rsqrt_fusion.1, f32[256]{0:T(256)S(1)} %broadcast_multiply_fusion.5, ...), kind=kOutput, calls=%fused_computation.7 | convolution fusion | flops 613023744 | bytes 5120000 | tf_op jit(solution)/shard_map/dot_general | solution.py:88
  118.2 3.4 %fusion.46 = f32[1536]{0:T(1024)S(1)} fusion(f32[256,1536]{1,0:T(8,128)S(1)} %convolution_multiply_fusion, f32[256,1536]{1,0:T(8,128)S(1)} %fusion.113, f32[256,1536]{1,0:T(8,128)S(1)} %fusion.40, bf16[256,1536]{1,0:T(8,128)(2,1)S(1)} %bitcast.70, bf16[256,1536]{1,0:T(8,128)(2,1)} %collective-permute-done.5, bf16[256,768]{1,0:T(8,128)(2,1)} %multiply_convert_fusion.2, ...), kind=kOutput, calls=%fused_computation.70 | convolution fusion | flops 616167936 | bytes 9060352 | tf_op jit(solution)/shard_map/dot_general | solution.py:88
  121.7 17.5 %all_to_all.10 = f32[32,18,128]{2,1,0:T(8,128)S(1)} all-to-all(f32[32,18,128]{2,1,0:T(8,128)S(1)} %broadcast_in_dim.10), channel_id=1, replica_groups=mesh['x'=4,'yh'=2,'z'=16,'yl'=2,'c'=2] {'x','yh','yl','c'}, dimensions={0} | all-to-all | bytes 589824 | tf_op jit(solution)/shard_map/all_to_all | solution.py:56
  139.3 1.9 %fusion.114 = f32[256,1536]{1,0:T(8,128)S(1)} fusion(bf16[256,768]{1,0:T(8,128)(2,1)} %collective-permute-done.12, bf16[1536,768]{1,0:T(8,128)(2,1)S(1)} %copy-done.7), kind=kOutput, calls=%fused_computation.177 | convolution fusion | flops 603979776 | bytes 4325376 | tf_op jit(solution)/shard_map/dot_general | solution.py:88
  141.5 2.8 %fusion.109 = (f32[256]{0:T(256)S(1)}, f32[256]{0:T(256)S(1)}, f32[256,1536]{1,0:T(8,128)S(1)}) fusion(f32[256]{0:T(256)S(1)} %copy-done.20, f32[256]{0:T(256)S(1)} %get-tuple-element.35, bf16[2,128,1536]{2,1,0:T(8,128)(2,1)S(1)} %copy-done, f32[1536]{0:T(1024)S(1)} %copy-done.18, f32[256,1536]{1,0:T(8,128)} %copy-done.14, f32[256,1536]{1,0:T(8,128)S(1)} %fusion.114, ...), kind=kOutput, calls=%fused_computation.172 | convolution fusion | flops 607911424 | bytes 9840640 | tf_op jit(solution)/shard_map/dot_general | solution.py:88
  145.0 5.5 %all-to-all-start.1 = ((f32[16,18,128]{2,1,0:T(8,128)}), f32[16,18,128]{2,1,0:T(8,128)S(1)}, u32[]{:S(2)}, u32[]{:S(2)}) async-start(f32[16,18,128]{2,1,0:T(8,128)} %broadcast_in_dim.11), calls=%async_computation.1 | async-start | bytes 393216 | tf_op jit(solution)/shard_map/all_to_all | solution.py:56
  152.0 11.7 %all-to-all-done.1 = f32[16,18,128]{2,1,0:T(8,128)S(1)} async-done(((f32[16,18,128]{2,1,0:T(8,128)}), f32[16,18,128]{2,1,0:T(8,128)S(1)}, u32[]{:S(2)}, u32[]{:S(2)}) %all-to-all-start.1) | async-done | bytes 147488 | tf_op jit(solution)/shard_map/all_to_all | solution.py:56
  (104 shorter events, 32.0 us)
Async XLA Ops:
  0.6 67.7 %collective-permute-start.5 = (bf16[256,1536]{1,0:T(8,128)(2,1)}, bf16[256,1536]{1,0:T(8,128)(2,1)}, u32[]{:S(2)}, u32[]{:S(2)}) collective-permute-start(bf16[256,1536]{1,0:T(8,128)(2,1)} %bitcast.67), channel_id=1, source_target_pairs={{0,64},{1,65},{2,66},{3,67},{4,68},{5,69},{6,70},{7,71},{8,72},{9,... | collective-permute-start | bytes 2359304 | tf_op jit(solution)/shard_map/ppermute | solution.py:23
  7.2 64.4 %collective-permute-start.10 = (bf16[256,1536]{1,0:T(8,128)(2,1)}, bf16[256,1536]{1,0:T(8,128)(2,1)}, u32[]{:S(2)}, u32[]{:S(2)}) collective-permute-start(bf16[256,1536]{1,0:T(8,128)(2,1)} %bitcast.68), channel_id=1, source_target_pairs={{64,0},{65,1},{66,2},{67,3},{68,4},{69,5},{70,6},{71,7},{72,8},{73... | collective-permute-start | bytes 2359304 | tf_op jit(solution)/shard_map/ppermute | solution.py:23
  12.5 12.5 %copy-start = (bf16[2,128,1536]{2,1,0:T(8,128)(2,1)S(1)}, bf16[2,128,1536]{2,1,0:T(8,128)(2,1)}, u32[]{:S(2)}) copy-start(bf16[2,128,1536]{2,1,0:T(8,128)(2,1)} %param.6) | copy-start | bytes 2359300
  12.5 40.9 %collective-permute-start.1 = (bf16[384,768]{1,0:T(8,128)(2,1)}, bf16[384,768]{1,0:T(8,128)(2,1)}, u32[]{:S(2)}, u32[]{:S(2)}) collective-permute-start(bf16[384,768]{1,0:T(8,128)(2,1)} %get-tuple-element.19), channel_id=1, source_target_pairs={{0,66},{1,67},{2,0},{3,1},{4,70},{5,71},{6,4},{7,5},{8,74},{9,75},... | collective-permute-start | bytes 1769480 | tf_op jit(solution)/shard_map/ppermute | solution.py:23
  19.6 69.9 %collective-permute-start = (bf16[4,384,768]{2,1,0:T(8,128)(2,1)}, bf16[4,384,768]{2,1,0:T(8,128)(2,1)}, u32[]{:S(2)}, u32[]{:S(2)}) collective-permute-start(bf16[4,384,768]{2,1,0:T(8,128)(2,1)} %pad_maximum_fusion), channel_id=1, source_target_pairs={{0,1},{1,0},{2,3},{3,2},{4,5},{5,4},{6,7},{7,6},{8,9},{9,8},{10,11... | collective-permute-start | bytes 7077896 | tf_op jit(solution)/shard_map/ppermute | solution.py:23
  23.0 41.5 %collective-permute-start.6 = (bf16[384,768]{1,0:T(8,128)(2,1)}, bf16[384,768]{1,0:T(8,128)(2,1)}, u32[]{:S(2)}, u32[]{:S(2)}) collective-permute-start(bf16[384,768]{1,0:T(8,128)(2,1)} %get-tuple-element.18), channel_id=1, source_target_pairs={{0,2},{1,3},{2,64},{3,65},{4,6},{5,7},{6,68},{7,69},{8,10},{9,11},... | collective-permute-start | bytes 1769480 | tf_op jit(solution)/shard_map/ppermute | solution.py:23
  30.1 88.1 %copy-start.19 = (f32[256]{0:T(256)}, f32[256]{0:T(256)S(1)}, u32[]{:S(2)}) copy-start(f32[256]{0:T(256)S(1)} %rsqrt_bitcast_fusion) | copy-start | bytes 3076
  30.1 59.4 %copy-start.5 = (bf16[1536,768]{1,0:T(8,128)(2,1)S(1)}, bf16[1536,768]{1,0:T(8,128)(2,1)}, u32[]{:S(2)}) copy-start(bf16[1536,768]{1,0:T(8,128)(2,1)} %copy-done.4) | copy-start | bytes 7077892
  31.3 86.9 %copy-start.14 = (f32[256,1536]{1,0:T(8,128)}, f32[256,1536]{1,0:T(8,128)S(1)}, u32[]{:S(2)}) copy-start(f32[256,1536]{1,0:T(8,128)S(1)} %fusion.40) | copy-start | bytes 4718596
  31.3 58.2 %copy-start.3 = (bf16[1536,768]{1,0:T(8,128)(2,1)S(1)}, bf16[1536,768]{1,0:T(8,128)(2,1)}, u32[]{:S(2)}) copy-start(bf16[1536,768]{1,0:T(8,128)(2,1)} %copy-done.2) | copy-start | bytes 7077892
  53.5 24.4 %collective-permute-start.2 = (bf16[384,768]{1,0:T(8,128)(2,1)}, bf16[384,768]{1,0:T(8,128)(2,1)S(1)}, u32[]{:S(2)}, u32[]{:S(2)}) collective-permute-start(bf16[384,768]{1,0:T(8,128)(2,1)} %collective-permute-done.1), channel_id=1, source_target_pairs={{0,60},{1,61},{2,62},{3,63},{4,0},{5,1},{6,2},{7,3},{8,4},{9,5},{1... | collective-permute-start | bytes 1769480 | tf_op jit(solution)/shard_map/ppermute | solution.py:23
  64.6 30.7 %collective-permute-start.3 = (bf16[384,768]{1,0:T(8,128)(2,1)}, bf16[384,768]{1,0:T(8,128)(2,1)S(1)}, u32[]{:S(2)}, u32[]{:S(2)}) collective-permute-start(bf16[384,768]{1,0:T(8,128)(2,1)} %collective-permute-done.1), channel_id=1, source_target_pairs={{0,1},{1,0},{2,3},{3,2},{4,5},{5,4},{6,7},{7,6},{8,9},{9,8},{10,11... | collective-permute-start | bytes 1769480 | tf_op jit(solution)/shard_map/ppermute | solution.py:23
  68.3 18.3 %collective-permute-start.7 = (bf16[384,768]{1,0:T(8,128)(2,1)}, bf16[384,768]{1,0:T(8,128)(2,1)S(1)}, u32[]{:S(2)}, u32[]{:S(2)}) collective-permute-start(bf16[384,768]{1,0:T(8,128)(2,1)} %collective-permute-done.6), channel_id=1, source_target_pairs={{0,4},{1,5},{2,6},{3,7},{4,8},{5,9},{6,10},{7,11},{8,12},{9,13},{1... | collective-permute-start | bytes 1769480 | tf_op jit(solution)/shard_map/ppermute | solution.py:23
  71.6 24.2 %collective-permute-start.8 = (bf16[384,768]{1,0:T(8,128)(2,1)}, bf16[384,768]{1,0:T(8,128)(2,1)S(1)}, u32[]{:S(2)}, u32[]{:S(2)}) collective-permute-start(bf16[384,768]{1,0:T(8,128)(2,1)} %collective-permute-done.6), channel_id=1, source_target_pairs={{0,1},{1,0},{2,3},{3,2},{4,5},{5,4},{6,7},{7,6},{8,9},{9,8},{10,11... | collective-permute-start | bytes 1769480 | tf_op jit(solution)/shard_map/ppermute | solution.py:23
  77.9 17.5 %collective-permute-start.4 = (bf16[384,768]{1,0:T(8,128)(2,1)S(1)}, bf16[384,768]{1,0:T(8,128)(2,1)S(1)}, u32[]{:S(2)}, u32[]{:S(2)}) collective-permute-start(bf16[384,768]{1,0:T(8,128)(2,1)S(1)} %collective-permute-done.2), channel_id=1, source_target_pairs={{0,1},{1,0},{2,3},{3,2},{4,5},{5,4},{6,7},{7,6},{8,9},{9,8},{10,11... | collective-permute-start | bytes 1769480 | tf_op jit(solution)/shard_map/ppermute | solution.py:23
  86.6 9.2 %collective-permute-start.9 = (bf16[384,768]{1,0:T(8,128)(2,1)S(1)}, bf16[384,768]{1,0:T(8,128)(2,1)S(1)}, u32[]{:S(2)}, u32[]{:S(2)}) collective-permute-start(bf16[384,768]{1,0:T(8,128)(2,1)S(1)} %collective-permute-done.7), channel_id=1, source_target_pairs={{0,1},{1,0},{2,3},{3,2},{4,5},{5,4},{6,7},{7,6},{8,9},{9,8},{10,11... | collective-permute-start | bytes 1769480 | tf_op jit(solution)/shard_map/ppermute | solution.py:23
  96.1 19.3 %copy-start.6 = (bf16[1536,768]{1,0:T(8,128)(2,1)}, bf16[1536,768]{1,0:T(8,128)(2,1)S(1)}, u32[]{:S(2)}) copy-start(bf16[1536,768]{1,0:T(8,128)(2,1)S(1)} %get-tuple-element.27) | copy-start | bytes 7077892
  96.1 22.1 %copy-start.10 = (bf16[1536,768]{1,0:T(8,128)(2,1)}, bf16[1536,768]{1,0:T(8,128)(2,1)S(1)}, u32[]{:S(2)}) copy-start(bf16[1536,768]{1,0:T(8,128)(2,1)S(1)} %get-tuple-element.26) | copy-start | bytes 7077892
  107.8 10.4 %copy-start.12 = (f32[256,1536]{1,0:T(8,128)}, f32[256,1536]{1,0:T(8,128)S(1)}, u32[]{:S(2)}) copy-start(f32[256,1536]{1,0:T(8,128)S(1)} %fusion.113) | copy-start | bytes 4718596
  107.8 31.5 %collective-permute-start.11 = (bf16[256,768]{1,0:T(8,128)(2,1)}, bf16[256,768]{1,0:T(8,128)(2,1)}, u32[]{:S(2)}, u32[]{:S(2)}) collective-permute-start(bf16[256,768]{1,0:T(8,128)(2,1)} %multiply_convert_fusion.2), channel_id=1, source_target_pairs={{64,0},{65,1},{66,2},{67,3},{68,4},{69,5},{70,6},{71,7},{72,8},{73... | collective-permute-start | bytes 1179656 | tf_op jit(solution)/shard_map/ppermute | solution.py:23
  109.1 30.2 %collective-permute-start.12 = (bf16[256,768]{1,0:T(8,128)(2,1)}, bf16[256,768]{1,0:T(8,128)(2,1)}, u32[]{:S(2)}, u32[]{:S(2)}) collective-permute-start(bf16[256,768]{1,0:T(8,128)(2,1)} %multiply_convert_fusion.2), channel_id=1, source_target_pairs={{0,64},{1,65},{2,66},{3,67},{4,68},{5,69},{6,70},{7,71},{8,72},{9,... | collective-permute-start | bytes 1179656 | tf_op jit(solution)/shard_map/ppermute | solution.py:23
  118.2 21.1 %copy-start.7 = (bf16[1536,768]{1,0:T(8,128)(2,1)S(1)}, bf16[1536,768]{1,0:T(8,128)(2,1)}, u32[]{:S(2)}) copy-start(bf16[1536,768]{1,0:T(8,128)(2,1)} %copy-done.6) | copy-start | bytes 7077892
  141.5 9.1 %copy-start.16 = (bf16[2,128,1536]{2,1,0:T(8,128)(2,1)S(1)}, bf16[2,128,1536]{2,1,0:T(8,128)(2,1)}, u32[]{:S(2)}) copy-start(bf16[2,128,1536]{2,1,0:T(8,128)(2,1)} %param.11) | copy-start | bytes 2359300
  145.0 18.8 %all-to-all-start.1 = ((f32[16,18,128]{2,1,0:T(8,128)}), f32[16,18,128]{2,1,0:T(8,128)S(1)}, u32[]{:S(2)}, u32[]{:S(2)}) async-start(f32[16,18,128]{2,1,0:T(8,128)} %broadcast_in_dim.11), calls=%async_computation.1 | async-start | bytes 393216 | tf_op jit(solution)/shard_map/all_to_all | solution.py:56
  (12 other events, 21.8 us)

commit v3 on v2

--- a/solution.py
+++ b/solution.py
@@ -2,6 +2,8 @@
 import jax.numpy as jnp
 import numpy as np
 from jax import lax
+from jax.experimental import pallas as pl
+from jax.experimental.pallas import tpu as pltpu
 from jax.sharding import Mesh
 from jax.sharding import PartitionSpec as P
 
@@ -10,6 +12,7 @@
 SEQ = ("x", "yh", "z")
 FSDP = ("yl", "c")
 HALF = 0.7978845608028654
+VMEM_LIMIT = 32 * 1024 * 1024
 
 
 def permute(value, target):
@@ -56,6 +59,9 @@
     return jnp.sum(lax.all_to_all(copies, axes, 0, 0), axis=0)
 
 
+CHUNK = 16
+
+
 def normed(values):
     centre = values - jnp.mean(values, axis=-1, keepdims=True)
     spread = jnp.mean(centre * centre, axis=-1, keepdims=True)
@@ -63,13 +69,10 @@
     return centre * scale, scale
 
 
-def act(a):
-    return 0.5 * a * (1.0 + jnp.tanh(HALF * (a + 0.044715 * a * a * a)))
-
-
-def slope(a):
-    t = jnp.tanh(HALF * (a + 0.044715 * a * a * a))
-    return 0.5 * (1.0 + t) + 0.5 * a * (1.0 - t * t) * (HALF * (1.0 + 0.134145 * a * a))
+def bend(a):
+    square = a * a
+    t = jnp.tanh(HALF * a * (1.0 + 0.044715 * square))
+    return t, 0.5 * (1.0 + t) + (0.5 * HALF) * a * (1.0 - t * t) * (1.0 + 0.134145 * square)
 
 
 def norm_back(grad, scale, unit):
@@ -78,6 +81,88 @@
         - jnp.mean(grad, axis=-1, keepdims=True)
         - unit * jnp.mean(grad * unit, axis=-1, keepdims=True)
     )
+
+
+def over_rows(count, step):
+    def run(i, carry):
+        step(pl.ds(pl.multiple_of(i * CHUNK, CHUNK), CHUNK))
+        return carry
+
+    lax.fori_loop(0, count // CHUNK, run, 0, unroll=True)
+
+
+def prepare_kernel(block, gain, hidden, weigh):
+    def step(rows):
+        unit, scale = normed(block[rows, :].astype(jnp.float32))
+        a = unit * gain[...]
+        t, slope = bend(a)
+        hidden[rows, :] = (0.5 * a * (1.0 + t)).astype(jnp.bfloat16)
+        weigh[rows, :] = slope * unit
+
+    over_rows(block.shape[0], step)
+
+
+def middle_kernel(
+    h0, h1, h2, e0, e1, e2, t0, t1, t2, grad2, gain, grad_mixed, first, second, mixed, partial
+):
+    rows, width = mixed.shape
+    channels = e0.shape[1]
+    for n in range(0, width, 256):
+        cols = slice(n, n + 256)
+        mixed[:, cols] = (
+            dot(h1[...], t1[:, cols]) + dot(h0[...], t0[:, cols]) + dot(h2[...], t2[:, cols])
+        )
+    partial[...] = jnp.zeros_like(partial)
+
+    def step(at):
+        unit, scale = normed(mixed[at, :].astype(jnp.bfloat16).astype(jnp.float32))
+        unused, slope = bend(unit * gain[...])
+        grad_a = grad2[at, :] * slope
+        terms = grad_a * unit
+        partial[...] += jnp.sum(terms.reshape(-1, 8, width), axis=0)
+        grad_mixed[at, :] = norm_back(grad_a * gain[...], scale, unit).astype(jnp.bfloat16)
+
+    over_rows(rows, step)
+    second[...] = jnp.sum(partial[...], axis=0, keepdims=True)
+    for n in range(0, channels, 256):
+        cols = slice(n, n + 256)
+        terms = dot_t(grad_mixed[...], t0[cols, :]) * e0[:, cols]
+        terms += dot_t(grad_mixed[...], t1[cols, :]) * e1[:, cols]
+        terms += dot_t(grad_mixed[...], t2[cols, :]) * e2[:, cols]
+        first[:, cols] = jnp.sum(terms, axis=0, keepdims=True)
+
+
+def last_kernel(block, cotangent, ahead, here, behind, t0, t1, t2, gain, result, grads):
+    rows, channels = block.shape
+    for n in range(0, channels, 256):
+        cols = slice(n, n + 256)
+        grads[:, cols] = (
+            dot_t(here[...], t1[cols, :])
+            + dot_t(ahead[...], t0[cols, :])
+            + dot_t(behind[...], t2[cols, :])
+        )
+
+    def step(at):
+        unit, scale = normed(block[at, :].astype(jnp.float32))
+        unused, slope = bend(unit * gain[...])
+        branch = norm_back(grads[at, :] * slope * gain[...], scale, unit)
+        result[at, :] = (cotangent[at, :].astype(jnp.float32) + branch).astype(jnp.bfloat16)
+
+    over_rows(rows, step)
+
+
+def call(kernel, name, out_shape, scratch, flops, *operands):
+    moved = sum(v.size * v.dtype.itemsize for v in operands)
+    return pl.pallas_call(
+        kernel,
+        name=name,
+        out_shape=out_shape,
+        in_specs=[pl.BlockSpec(memory_space=pltpu.VMEM)] * len(operands),
+        out_specs=jax.tree.map(lambda _: pl.BlockSpec(memory_space=pltpu.VMEM), out_shape),
+        scratch_shapes=scratch,
+        cost_estimate=pl.CostEstimate(flops=flops, bytes_accessed=moved, transcendentals=0),
+        compiler_params=pltpu.CompilerParams(vmem_limit_bytes=VMEM_LIMIT),
+    )(*operands)
 
 
 def dot(a, b):
@@ -100,14 +185,14 @@
     own = lax.axis_index(FSDP)
     odd = lax.axis_index("z") % 2
 
-    slabs = jnp.concatenate(
-        [weight, jnp.concatenate([project[:, :width], project[:, width:]], axis=0)[None]], axis=0
-    )
-    up = permute(lax.dynamic_index_in_dim(slabs, 2 * odd, 0, False), along_y(1))
-    down = permute(lax.dynamic_index_in_dim(slabs, 2 * odd + 1, 0, False), along_y(-1))
-    lagging = permute(inputs, along_bins(1))
-    leading = permute(inputs, along_bins(-1))
-    slabs_s = permute(slabs, sister)
+    folded = jnp.concatenate([project[:, :width], project[:, width:]], axis=0)
+    slabs = [weight[0], weight[1], weight[2], folded]
+    near_u = jnp.where(odd == 0, slabs[0], slabs[2])
+    near_d = jnp.where(odd == 0, slabs[1], slabs[3])
+    weight_s = permute(weight, sister)
+    up = permute(near_u, along_y(1))
+    down = permute(near_d, along_y(-1))
+    slabs_s = [weight_s[0], weight_s[1], weight_s[2], permute(folded, sister)]
     up_z = permute(up, along_z(1))
     down_z = permute(down, along_z(-1))
     first = [up, down, up_z, down_z]
@@ -133,36 +218,68 @@
 
     grad_hidden2 = dot_t(cotangent[:, :width], proj[0]) + dot_t(cotangent[:, width:], proj[1])
 
-    units, scales, hiddens, weighs, slopes = [], [], [], [], []
-    for block in (lagging, inputs, leading):
-        unit, scale = normed(block.astype(jnp.float32))
-        a = unit * gain_first
-        units.append(unit)
-        scales.append(scale)
-        hiddens.append(act(a).astype(jnp.bfloat16))
-        slopes.append(slope(a))
-        weighs.append(slopes[-1] * unit)
-
-    mixed = dot(hiddens[1], taps[1]) + dot(hiddens[0], taps[0]) + dot(hiddens[2], taps[2])
-    mixed = mixed.astype(jnp.bfloat16).astype(jnp.float32)
-    unit2, scale2 = normed(mixed)
-    grad_a = grad_hidden2 * slope(unit2 * gain_second)
-    second_sum = jnp.sum(grad_a * unit2, axis=0)
-    grad_mixed = norm_back(grad_a * gain_second, scale2, unit2).astype(jnp.bfloat16)
-
+    f32, bf16 = jnp.float32, jnp.bfloat16
+    gain1, gain2 = gain_first[None], gain_second[None]
+
+    def prepare(block):
+        return call(
+            prepare_kernel,
+            "prepare",
+            [jax.ShapeDtypeStruct(block.shape, bf16), jax.ShapeDtypeStruct(block.shape, f32)],
+            [],
+            40 * block.size,
+            block,
+            gain1,
+        )
+
+    own_pair = prepare(inputs)
+    halo, own_pair = lax.optimization_barrier((inputs, own_pair))
+    lagging = permute(halo, along_bins(1))
+    leading = permute(halo, along_bins(-1))
+    pairs = [prepare(lagging), own_pair, prepare(leading)]
+    hiddens = [pair[0] for pair in pairs]
+    weighs = [pair[1] for pair in pairs]
+
+    work = 2 * rows * channels * width
+    grad_mixed, first_sum, second_sum = call(
+        middle_kernel,
+        "middle",
+        [
+            jax.ShapeDtypeStruct((rows, width), bf16),
+            jax.ShapeDtypeStruct((1, channels), f32),
+            jax.ShapeDtypeStruct((1, width), f32),
+        ],
+        [pltpu.VMEM((rows, width), f32), pltpu.VMEM((8, width), f32)],
+        6 * work,
+        *hiddens,
+        *weighs,
+        *taps,
+        grad_hidden2,
+        gain2,
+    )
+    first_sum, second_sum = first_sum[0], second_sum[0]
     ahead = permute(grad_mixed, along_bins(-1))
     behind = permute(grad_mixed, along_bins(1))
 
-    terms = [dot_t(grad_mixed, tap) for tap in taps]
-    first_sum = jnp.sum(terms[0] * weighs[0] + terms[1] * weighs[1] + terms[2] * weighs[2], axis=0)
     sums = jnp.concatenate([first_sum, second_sum]).reshape(-1, 128)
     sums = total(sums, ("x", "yh", "yl", "c"))
     ahead, behind, sums = lax.optimization_barrier((ahead, behind, sums))
     sums = total(sums, "z").reshape(-1)
 
-    grad_hidden = terms[1] + dot_t(ahead, taps[0]) + dot_t(behind, taps[2])
-    grad_branch = norm_back(grad_hidden * slopes[1] * gain_first, scales[1], units[1])
-    grad_input = (cotangent.astype(jnp.float32) + grad_branch).astype(jnp.bfloat16)
+    grad_input = call(
+        last_kernel,
+        "last",
+        jax.ShapeDtypeStruct(inputs.shape, bf16),
+        [pltpu.VMEM(inputs.shape, f32)],
+        3 * work,
+        inputs,
+        cotangent,
+        ahead,
+        grad_mixed,
+        behind,
+        *taps,
+        gain1,
+    )
     return (grad_input.reshape(block_input.shape), sums[:channels], sums[channels:])
 
 

time: 168 us -> 173 us (1.030)
  the two profiles are of different devices: /device:TPU:1 before, /device:TPU:24 now
where the time goes in v3:
time: 173 us; the launch traced here: 172 us
  starting transfers between devices  74.3 us (43%)
  waiting for transfers between devices  30.3 us (18%)
  Pallas kernels  18.7 us (11%)
  local copies, waits for them, and re-layouts  18.6 us (11%)
  blocking collectives  18.3 us (11%)
  other arithmetic  9.41 us (5%)
    ppermute x14, starting transfers between devices, permute(): return lax.ppermute(value, AXES, pairs)  66.2 us
    ppermute x14, waiting for transfers between devices, permute(): return lax.ppermute(value, AXES, pairs)  23.2 us
    pallas_call x5, Pallas kernels, call(): pl.pallas_call(kernel, name=name, out_shape=out_shape, in_specs=[pl.Block...  18.7 us
    all_to_all x1, blocking collectives, total(): return jnp.sum(lax.all_to_all(copies, axes, 0, 0), axis=0)  18.3 us
    unnamed x40, local copies, waits for them, and re-layouts  11.6 us
    all_to_all x1, starting transfers between devices, total(): return jnp.sum(lax.all_to_all(copies, axes, 0, 0), axis=0)  8.13 us
    all_to_all x1, waiting for transfers between devices, total(): return jnp.sum(lax.all_to_all(copies, axes, 0, 0), axis=0)  7.12 us
    dynamic_update_slice x6, other arithmetic, full(): whole = lax.dynamic_update_slice(whole, piece, (f * part, 0))  4.79 us
  transfers between devices with their start and end apart: 15, of which 3 were waited for; matrix products, arithmetic and copies ran while one was open for 8% of the time, Pallas kernels for 7%

profile of v3, /device:TPU:24, one launch (start us, length us, event | category | flops | bytes accessed | tf_op | source)
XLA Modules:
  0.0 171.8 jit_solution(18375249716023784533)
XLA Ops:
  0.6 1.9 %collective-permute-start.2 = (bf16[3,384,768]{2,1,0:T(8,128)(2,1)}, bf16[3,384,768]{2,1,0:T(8,128)(2,1)}, u32[]{:S(2)}, u32[]{:S(2)}) collective-permute-start(bf16[3,384,768]{2,1,0:T(8,128)(2,1)} %param.7), channel_id=1, source_target_pairs={{0,1},{1,0},{2,3},{3,2},{4,5},{5,4},{6,7},{7,6},{8,9},{9,8},{10,11... | collective-permute-start | bytes 5308424 | tf_op jit(solution)/shard_map/ppermute | solution.py:26
  2.6 1.8 %fusion.8 = (bf16[192,768]{1,0:T(8,128)(2,1)S(1)}, bf16[192,768]{1,0:T(8,128)(2,1)}) fusion(bf16[192,1536]{1,0:T(8,128)(2,1)} %param.8), kind=kLoop, calls=%fused_computation.31 | loop fusion | bytes 1179648 | tf_op jit(solution)/shard_map/slice | solution.py:188
  7.4 2.4 %collective-permute-start.11 = (bf16[384,768]{1,0:T(8,128)(2,1)S(1)}, bf16[384,768]{1,0:T(8,128)(2,1)S(1)}, u32[]{:S(2)}, u32[]{:S(2)}) collective-permute-start(bf16[384,768]{1,0:T(8,128)(2,1)S(1)} %get-tuple-element.49), channel_id=1, source_target_pairs={{0,1},{1,0},{2,3},{3,2},{4,5},{5,4},{6,7},{7,6},{8,9},{9,8},{10,11... | collective-permute-start | bytes 1769480 | tf_op jit(solution)/shard_map/ppermute | solution.py:26
  9.8 2.7 %collective-permute-start.7 = (bf16[384,768]{1,0:T(8,128)(2,1)}, bf16[384,768]{1,0:T(8,128)(2,1)}, u32[]{:S(2)}, u32[]{:S(2)}) collective-permute-start(bf16[384,768]{1,0:T(8,128)(2,1)} %get-tuple-element.39), channel_id=1, source_target_pairs={{0,66},{1,67},{2,0},{3,1},{4,70},{5,71},{6,4},{7,5},{8,74},{9,75},... | collective-permute-start | bytes 1769480 | tf_op jit(solution)/shard_map/ppermute | solution.py:26
  12.4 6.8 %collective-permute-start.3 = (bf16[384,768]{1,0:T(8,128)(2,1)}, bf16[384,768]{1,0:T(8,128)(2,1)}, u32[]{:S(2)}, u32[]{:S(2)}) collective-permute-start(bf16[384,768]{1,0:T(8,128)(2,1)} %get-tuple-element.40), channel_id=1, source_target_pairs={{0,2},{1,3},{2,64},{3,65},{4,6},{5,7},{6,68},{7,69},{8,10},{9,11},... | collective-permute-start | bytes 1769480 | tf_op jit(solution)/shard_map/ppermute | solution.py:26
  23.1 3.4 %collective-permute-start.1 = (bf16[256,1536]{1,0:T(8,128)(2,1)S(1)}, bf16[256,1536]{1,0:T(8,128)(2,1)}, u32[]{:S(2)}, u32[]{:S(2)}) collective-permute-start(bf16[256,1536]{1,0:T(8,128)(2,1)S(1)} %bitcast.41), channel_id=1, source_target_pairs={{64,0},{65,1},{66,2},{67,3},{68,4},{69,5},{70,6},{71,7},{72,8},{73... | collective-permute-start | bytes 2359304 | tf_op jit(solution)/shard_map/ppermute | solution.py:26
  27.4 4.9 %collective-permute-start = (bf16[256,1536]{1,0:T(8,128)(2,1)S(1)}, bf16[256,1536]{1,0:T(8,128)(2,1)}, u32[]{:S(2)}, u32[]{:S(2)}) collective-permute-start(bf16[256,1536]{1,0:T(8,128)(2,1)S(1)} %bitcast.42), channel_id=1, source_target_pairs={{0,64},{1,65},{2,66},{3,67},{4,68},{5,69},{6,70},{7,71},{8,72},{9,... | collective-permute-start | bytes 2359304 | tf_op jit(solution)/shard_map/ppermute | solution.py:26
  32.3 15.6 %collective-permute-done.7 = bf16[384,768]{1,0:T(8,128)(2,1)} collective-permute-done((bf16[384,768]{1,0:T(8,128)(2,1)}, bf16[384,768]{1,0:T(8,128)(2,1)}, u32[]{:S(2)}, u32[]{:S(2)}) %collective-permute-start.7) | collective-permute-done | bytes 589856 | tf_op jit(solution)/shard_map/ppermute | solution.py:26
  47.9 25.6 %collective-permute-start.8 = (bf16[384,768]{1,0:T(8,128)(2,1)}, bf16[384,768]{1,0:T(8,128)(2,1)S(1)}, u32[]{:S(2)}, u32[]{:S(2)}) collective-permute-start(bf16[384,768]{1,0:T(8,128)(2,1)} %collective-permute-done.7), channel_id=1, source_target_pairs={{0,60},{1,61},{2,62},{3,63},{4,0},{5,1},{6,2},{7,3},{8,4},{9,5},{1... | collective-permute-start | bytes 1769480 | tf_op jit(solution)/shard_map/ppermute | solution.py:26
  73.8 2.1 %collective-permute-start.4 = (bf16[384,768]{1,0:T(8,128)(2,1)}, bf16[384,768]{1,0:T(8,128)(2,1)S(1)}, u32[]{:S(2)}, u32[]{:S(2)}) collective-permute-start(bf16[384,768]{1,0:T(8,128)(2,1)} %collective-permute-done.3), channel_id=1, source_target_pairs={{0,4},{1,5},{2,6},{3,7},{4,8},{5,9},{6,10},{7,11},{8,12},{9,13},{1... | collective-permute-start | bytes 1769480 | tf_op jit(solution)/shard_map/ppermute | solution.py:26
  76.3 1.9 %collective-permute-start.9 = (bf16[384,768]{1,0:T(8,128)(2,1)}, bf16[384,768]{1,0:T(8,128)(2,1)S(1)}, u32[]{:S(2)}, u32[]{:S(2)}) collective-permute-start(bf16[384,768]{1,0:T(8,128)(2,1)} %collective-permute-done.7), channel_id=1, source_target_pairs={{0,1},{1,0},{2,3},{3,2},{4,5},{5,4},{6,7},{7,6},{8,9},{9,8},{10,11... | collective-permute-start | bytes 1769480 | tf_op jit(solution)/shard_map/ppermute | solution.py:26
  78.2 7.5 %collective-permute-done.8 = bf16[384,768]{1,0:T(8,128)(2,1)S(1)} collective-permute-done((bf16[384,768]{1,0:T(8,128)(2,1)}, bf16[384,768]{1,0:T(8,128)(2,1)S(1)}, u32[]{:S(2)}, u32[]{:S(2)}) %collective-permute-start.8) | collective-permute-done | bytes 589856 | tf_op jit(solution)/shard_map/ppermute | solution.py:26
  85.7 1.9 %collective-permute-start.10 = (bf16[384,768]{1,0:T(8,128)(2,1)S(1)}, bf16[384,768]{1,0:T(8,128)(2,1)S(1)}, u32[]{:S(2)}, u32[]{:S(2)}) collective-permute-start(bf16[384,768]{1,0:T(8,128)(2,1)S(1)} %collective-permute-done.8), channel_id=1, source_target_pairs={{0,1},{1,0},{2,3},{3,2},{4,5},{5,4},{6,7},{7,6},{8,9},{9,8},{10,11... | collective-permute-start | bytes 1769480 | tf_op jit(solution)/shard_map/ppermute | solution.py:26
  87.7 2.9 %prepare.5 = (bf16[256,1536]{1,0:T(8,128)(2,1)S(1)}, f32[256,1536]{1,0:T(8,128)S(1)}) custom-call(bf16[256,1536]{1,0:T(8,128)(2,1)} %collective-permute-done.1.block, f32[1,1536]{1,0:T(1,128)S(1)} %broadcast_in_dim.19.gain), custom_call_target="tpu_custom_call" | custom-call | flops 15728640 | bytes 792576 | tf_op jit(solution)/shard_map/prepare/pallas_call | solution.py:156
  90.6 2.4 %collective-permute-start.5 = (bf16[384,768]{1,0:T(8,128)(2,1)}, bf16[384,768]{1,0:T(8,128)(2,1)S(1)}, u32[]{:S(2)}, u32[]{:S(2)}) collective-permute-start(bf16[384,768]{1,0:T(8,128)(2,1)} %collective-permute-done.3), channel_id=1, source_target_pairs={{0,1},{1,0},{2,3},{3,2},{4,5},{5,4},{6,7},{7,6},{8,9},{9,8},{10,11... | collective-permute-start | bytes 1769480 | tf_op jit(solution)/shard_map/ppermute | solution.py:26
  93.0 2.9 %prepare.4 = (bf16[256,1536]{1,0:T(8,128)(2,1)S(1)}, f32[256,1536]{1,0:T(8,128)S(1)}) custom-call(bf16[256,1536]{1,0:T(8,128)(2,1)} %collective-permute-done.block, f32[1,1536]{1,0:T(1,128)S(1)} %broadcast_in_dim.19.gain), custom_call_target="tpu_custom_call" | custom-call | flops 15728640 | bytes 792576 | tf_op jit(solution)/shard_map/prepare/pallas_call | solution.py:156
  95.9 2.1 %collective-permute-start.6 = (bf16[384,768]{1,0:T(8,128)(2,1)S(1)}, bf16[384,768]{1,0:T(8,128)(2,1)S(1)}, u32[]{:S(2)}, u32[]{:S(2)}) collective-permute-start(bf16[384,768]{1,0:T(8,128)(2,1)S(1)} %collective-permute-done.4), channel_id=1, source_target_pairs={{0,1},{1,0},{2,3},{3,2},{4,5},{5,4},{6,7},{7,6},{8,9},{9,8},{10,11... | collective-permute-start | bytes 1769480 | tf_op jit(solution)/shard_map/ppermute | solution.py:26
  106.5 6.1 %middle.1 = (bf16[256,768]{1,0:T(8,128)(2,1)S(1)}, f32[1,1536]{1,0:T(1,128)S(1)}, f32[1,768]{1,0:T(1,128)S(1)}) custom-call(bf16[256,1536]{1,0:T(8,128)(2,1)S(1)} %get-tuple-element.21.h0, bf16[256,1536]{1,0:T(8,128)(2,1)S(1)} %copy-done.10, bf16[256,1536]{1,0:T(8,128)(2,1)S(1)} %get-tuple-element.23.h2, f32[256,1536]{1,0:T(8,128)S(1)} %get-tuple-element.24.e0, ...), custom_call_target="tpu_custom_call" | custom-call | flops 3623878656 | bytes 14945280 | tf_op jit(solution)/shard_map/middle/pallas_call | solution.py:156
  113.3 1.9 %collective-permute-start.12 = (bf16[256,768]{1,0:T(8,128)(2,1)S(1)}, bf16[256,768]{1,0:T(8,128)(2,1)}, u32[]{:S(2)}, u32[]{:S(2)}) collective-permute-start(bf16[256,768]{1,0:T(8,128)(2,1)S(1)} %get-tuple-element.27.here), channel_id=1, source_target_pairs={{64,0},{65,1},{66,2},{67,3},{68,4},{69,5},{70,6},{71,7},{72,8},{73... | collective-permute-start | bytes 1179656 | tf_op jit(solution)/shard_map/ppermute | solution.py:26
  115.2 6.3 %collective-permute-start.13 = (bf16[256,768]{1,0:T(8,128)(2,1)S(1)}, bf16[256,768]{1,0:T(8,128)(2,1)}, u32[]{:S(2)}, u32[]{:S(2)}) collective-permute-start(bf16[256,768]{1,0:T(8,128)(2,1)S(1)} %get-tuple-element.27.here), channel_id=1, source_target_pairs={{0,64},{1,65},{2,66},{3,67},{4,68},{5,69},{6,70},{7,71},{8,72},{9,... | collective-permute-start | bytes 1179656 | tf_op jit(solution)/shard_map/ppermute | solution.py:26
  123.6 18.3 %all_to_all.10 = f32[32,18,128]{2,1,0:T(8,128)} all-to-all(f32[32,18,128]{2,1,0:T(8,128)S(1)} %broadcast_in_dim.22), channel_id=1, replica_groups=mesh['x'=4,'yh'=2,'z'=16,'yl'=2,'c'=2] {'x','yh','yl','c'}, dimensions={0} | all-to-all | bytes 589824 | tf_op jit(solution)/shard_map/all_to_all | solution.py:59
  145.0 8.1 %all-to-all-start.1 = ((f32[16,18,128]{2,1,0:T(8,128)}), f32[16,18,128]{2,1,0:T(8,128)}, u32[]{:S(2)}, u32[]{:S(2)}) async-start(f32[16,18,128]{2,1,0:T(8,128)} %broadcast_in_dim.23), calls=%async_computation.1 | async-start | bytes 393216 | tf_op jit(solution)/shard_map/all_to_all | solution.py:59
  157.6 5.0 %last.1 = bf16[256,1536]{1,0:T(8,128)(2,1)} custom-call(bf16[256,1536]{1,0:T(8,128)(2,1)S(1)} %bitcast.43, bf16[256,1536]{1,0:T(8,128)(2,1)S(1)} %bitcast.39, bf16[256,768]{1,0:T(8,128)(2,1)} %collective-permute-done.12.ahead, bf16[256,768]{1,0:T(8,128)(2,1)S(1)} %get-tuple-element.27.here, bf16[256,768]{1,0:T(8,128)(2,1)} %collective-permute-done.13.behind, ...), custom_call_target="tpu_custom_call" | custom-call | flops 1811939328 | bytes 9836544 | tf_op jit(solution)/shard_map/last/pallas_call | solution.py:156
  162.6 7.1 %all-to-all-done.1 = f32[16,18,128]{2,1,0:T(8,128)} async-done(((f32[16,18,128]{2,1,0:T(8,128)}), f32[16,18,128]{2,1,0:T(8,128)}, u32[]{:S(2)}, u32[]{:S(2)}) %all-to-all-start.1) | async-done | bytes 147488 | tf_op jit(solution)/shard_map/all_to_all | solution.py:59
  (81 shorter events, 29.0 us)
Async XLA Ops:
  0.6 97.4 %collective-permute-start.2 = (bf16[3,384,768]{2,1,0:T(8,128)(2,1)}, bf16[3,384,768]{2,1,0:T(8,128)(2,1)}, u32[]{:S(2)}, u32[]{:S(2)}) collective-permute-start(bf16[3,384,768]{2,1,0:T(8,128)(2,1)} %param.7), channel_id=1, source_target_pairs={{0,1},{1,0},{2,3},{3,2},{4,5},{5,4},{6,7},{7,6},{8,9},{9,8},{10,11... | collective-permute-start | bytes 5308424 | tf_op jit(solution)/shard_map/ppermute | solution.py:26
  5.9 13.3 %copy-start.18 = (f32[1536]{0:T(1024)S(1)}, f32[1536]{0:T(1024)}, u32[]{:S(2)}) copy-start(f32[1536]{0:T(1024)} %param.9) | copy-start | bytes 18436
  5.9 13.4 %copy-start.5 = (bf16[2,128,1536]{2,1,0:T(8,128)(2,1)S(1)}, bf16[2,128,1536]{2,1,0:T(8,128)(2,1)}, u32[]{:S(2)}) copy-start(bf16[2,128,1536]{2,1,0:T(8,128)(2,1)} %param.6) | copy-start | bytes 2359300
  5.9 26.4 %copy-start.19 = (f32[768]{0:T(1024)S(1)}, f32[768]{0:T(1024)}, u32[]{:S(2)}) copy-start(f32[768]{0:T(1024)} %param.10) | copy-start | bytes 9220
  7.4 19.1 %collective-permute-start.11 = (bf16[384,768]{1,0:T(8,128)(2,1)S(1)}, bf16[384,768]{1,0:T(8,128)(2,1)S(1)}, u32[]{:S(2)}, u32[]{:S(2)}) collective-permute-start(bf16[384,768]{1,0:T(8,128)(2,1)S(1)} %get-tuple-element.49), channel_id=1, source_target_pairs={{0,1},{1,0},{2,3},{3,2},{4,5},{5,4},{6,7},{7,6},{8,9},{9,8},{10,11... | collective-permute-start | bytes 1769480 | tf_op jit(solution)/shard_map/ppermute | solution.py:26
  9.8 38.2 %collective-permute-start.7 = (bf16[384,768]{1,0:T(8,128)(2,1)}, bf16[384,768]{1,0:T(8,128)(2,1)}, u32[]{:S(2)}, u32[]{:S(2)}) collective-permute-start(bf16[384,768]{1,0:T(8,128)(2,1)} %get-tuple-element.39), channel_id=1, source_target_pairs={{0,66},{1,67},{2,0},{3,1},{4,70},{5,71},{6,4},{7,5},{8,74},{9,75},... | collective-permute-start | bytes 1769480 | tf_op jit(solution)/shard_map/ppermute | solution.py:26
  12.4 61.4 %collective-permute-start.3 = (bf16[384,768]{1,0:T(8,128)(2,1)}, bf16[384,768]{1,0:T(8,128)(2,1)}, u32[]{:S(2)}, u32[]{:S(2)}) collective-permute-start(bf16[384,768]{1,0:T(8,128)(2,1)} %get-tuple-element.40), channel_id=1, source_target_pairs={{0,2},{1,3},{2,64},{3,65},{4,6},{5,7},{6,68},{7,69},{8,10},{9,11},... | collective-permute-start | bytes 1769480 | tf_op jit(solution)/shard_map/ppermute | solution.py:26
  23.1 53.2 %collective-permute-start.1 = (bf16[256,1536]{1,0:T(8,128)(2,1)S(1)}, bf16[256,1536]{1,0:T(8,128)(2,1)}, u32[]{:S(2)}, u32[]{:S(2)}) collective-permute-start(bf16[256,1536]{1,0:T(8,128)(2,1)S(1)} %bitcast.41), channel_id=1, source_target_pairs={{64,0},{65,1},{66,2},{67,3},{68,4},{69,5},{70,6},{71,7},{72,8},{73... | collective-permute-start | bytes 2359304 | tf_op jit(solution)/shard_map/ppermute | solution.py:26
  27.4 63.3 %collective-permute-start = (bf16[256,1536]{1,0:T(8,128)(2,1)S(1)}, bf16[256,1536]{1,0:T(8,128)(2,1)}, u32[]{:S(2)}, u32[]{:S(2)}) collective-permute-start(bf16[256,1536]{1,0:T(8,128)(2,1)S(1)} %bitcast.42), channel_id=1, source_target_pairs={{0,64},{1,65},{2,66},{3,67},{4,68},{5,69},{6,70},{7,71},{8,72},{9,... | collective-permute-start | bytes 2359304 | tf_op jit(solution)/shard_map/ppermute | solution.py:26
  32.3 41.4 %copy-start.15 = (bf16[192,768]{1,0:T(8,128)(2,1)S(1)}, bf16[192,768]{1,0:T(8,128)(2,1)}, u32[]{:S(2)}) copy-start(bf16[192,768]{1,0:T(8,128)(2,1)} %get-tuple-element.51) | copy-start | bytes 884740
  47.9 37.8 %collective-permute-start.8 = (bf16[384,768]{1,0:T(8,128)(2,1)}, bf16[384,768]{1,0:T(8,128)(2,1)S(1)}, u32[]{:S(2)}, u32[]{:S(2)}) collective-permute-start(bf16[384,768]{1,0:T(8,128)(2,1)} %collective-permute-done.7), channel_id=1, source_target_pairs={{0,60},{1,61},{2,62},{3,63},{4,0},{5,1},{6,2},{7,3},{8,4},{9,5},{1... | collective-permute-start | bytes 1769480 | tf_op jit(solution)/shard_map/ppermute | solution.py:26
  73.7 2.3 %copy-start.13 = (bf16[3,384,768]{2,1,0:T(8,128)(2,1)S(1)}, bf16[3,384,768]{2,1,0:T(8,128)(2,1)}, u32[]{:S(2)}) copy-start(bf16[3,384,768]{2,1,0:T(8,128)(2,1)} %param.7) | copy-start | bytes 5308420
  73.8 22.2 %collective-permute-start.4 = (bf16[384,768]{1,0:T(8,128)(2,1)}, bf16[384,768]{1,0:T(8,128)(2,1)S(1)}, u32[]{:S(2)}, u32[]{:S(2)}) collective-permute-start(bf16[384,768]{1,0:T(8,128)(2,1)} %collective-permute-done.3), channel_id=1, source_target_pairs={{0,4},{1,5},{2,6},{3,7},{4,8},{5,9},{6,10},{7,11},{8,12},{9,13},{1... | collective-permute-start | bytes 1769480 | tf_op jit(solution)/shard_map/ppermute | solution.py:26
  76.0 11.6 %copy-start.17 = (bf16[384,768]{1,0:T(8,128)(2,1)S(1)}, bf16[384,768]{1,0:T(8,128)(2,1)}, u32[]{:S(2)}) copy-start(bf16[384,768]{1,0:T(8,128)(2,1)} %copy-done.16) | copy-start | bytes 1769476
  76.3 24.7 %collective-permute-start.9 = (bf16[384,768]{1,0:T(8,128)(2,1)}, bf16[384,768]{1,0:T(8,128)(2,1)S(1)}, u32[]{:S(2)}, u32[]{:S(2)}) collective-permute-start(bf16[384,768]{1,0:T(8,128)(2,1)} %collective-permute-done.7), channel_id=1, source_target_pairs={{0,1},{1,0},{2,3},{3,2},{4,5},{5,4},{6,7},{7,6},{8,9},{9,8},{10,11... | collective-permute-start | bytes 1769480 | tf_op jit(solution)/shard_map/ppermute | solution.py:26
  85.7 15.3 %collective-permute-start.10 = (bf16[384,768]{1,0:T(8,128)(2,1)S(1)}, bf16[384,768]{1,0:T(8,128)(2,1)S(1)}, u32[]{:S(2)}, u32[]{:S(2)}) collective-permute-start(bf16[384,768]{1,0:T(8,128)(2,1)S(1)} %collective-permute-done.8), channel_id=1, source_target_pairs={{0,1},{1,0},{2,3},{3,2},{4,5},{5,4},{6,7},{7,6},{8,9},{9,8},{10,11... | collective-permute-start | bytes 1769480 | tf_op jit(solution)/shard_map/ppermute | solution.py:26
  90.6 14.8 %collective-permute-start.5 = (bf16[384,768]{1,0:T(8,128)(2,1)}, bf16[384,768]{1,0:T(8,128)(2,1)S(1)}, u32[]{:S(2)}, u32[]{:S(2)}) collective-permute-start(bf16[384,768]{1,0:T(8,128)(2,1)} %collective-permute-done.3), channel_id=1, source_target_pairs={{0,1},{1,0},{2,3},{3,2},{4,5},{5,4},{6,7},{7,6},{8,9},{9,8},{10,11... | collective-permute-start | bytes 1769480 | tf_op jit(solution)/shard_map/ppermute | solution.py:26
  95.9 9.5 %collective-permute-start.6 = (bf16[384,768]{1,0:T(8,128)(2,1)S(1)}, bf16[384,768]{1,0:T(8,128)(2,1)S(1)}, u32[]{:S(2)}, u32[]{:S(2)}) collective-permute-start(bf16[384,768]{1,0:T(8,128)(2,1)S(1)} %collective-permute-done.4), channel_id=1, source_target_pairs={{0,1},{1,0},{2,3},{3,2},{4,5},{5,4},{6,7},{7,6},{8,9},{9,8},{10,11... | collective-permute-start | bytes 1769480 | tf_op jit(solution)/shard_map/ppermute | solution.py:26
  101.3 4.5 %copy-start.2 = (bf16[1536,768]{1,0:T(8,128)(2,1)}, bf16[1536,768]{1,0:T(8,128)(2,1)S(1)}, u32[]{:S(2)}) copy-start(bf16[1536,768]{1,0:T(8,128)(2,1)S(1)} %get-tuple-element.42.t1) | copy-start | bytes 7077892
  101.4 1.7 copy-start.4
  105.8 6.9 %copy-start = (bf16[1536,768]{1,0:T(8,128)(2,1)}, bf16[1536,768]{1,0:T(8,128)(2,1)S(1)}, u32[]{:S(2)}) copy-start(bf16[1536,768]{1,0:T(8,128)(2,1)S(1)} %get-tuple-element.46.t0) | copy-start | bytes 7077892
  113.3 30.3 %collective-permute-start.12 = (bf16[256,768]{1,0:T(8,128)(2,1)S(1)}, bf16[256,768]{1,0:T(8,128)(2,1)}, u32[]{:S(2)}, u32[]{:S(2)}) collective-permute-start(bf16[256,768]{1,0:T(8,128)(2,1)S(1)} %get-tuple-element.27.here), channel_id=1, source_target_pairs={{64,0},{65,1},{66,2},{67,3},{68,4},{69,5},{70,6},{71,7},{72,8},{73... | collective-permute-start | bytes 1179656 | tf_op jit(solution)/shard_map/ppermute | solution.py:26
  115.2 28.4 %collective-permute-start.13 = (bf16[256,768]{1,0:T(8,128)(2,1)S(1)}, bf16[256,768]{1,0:T(8,128)(2,1)}, u32[]{:S(2)}, u32[]{:S(2)}) collective-permute-start(bf16[256,768]{1,0:T(8,128)(2,1)S(1)} %get-tuple-element.27.here), channel_id=1, source_target_pairs={{0,64},{1,65},{2,66},{3,67},{4,68},{5,69},{6,70},{7,71},{8,72},{9,... | collective-permute-start | bytes 1179656 | tf_op jit(solution)/shard_map/ppermute | solution.py:26
  145.0 24.7 %all-to-all-start.1 = ((f32[16,18,128]{2,1,0:T(8,128)}), f32[16,18,128]{2,1,0:T(8,128)}, u32[]{:S(2)}, u32[]{:S(2)}) async-start(f32[16,18,128]{2,1,0:T(8,128)} %broadcast_in_dim.23), calls=%async_computation.1 | async-start | bytes 393216 | tf_op jit(solution)/shard_map/all_to_all | solution.py:59
  (11 other events, 14.0 us)

commit v4 on v3

--- a/solution.py
+++ b/solution.py
@@ -34,13 +34,6 @@
     return target
 
 
-def along_z(steps):
-    def target(x, yh, z, yl, c):
-        return (x, yh, (z + steps) % 16, yl, c)
-
-    return target
-
-
 def sister(x, yh, z, yl, c):
     return (x, yh, z, yl, 1 - c)
 
@@ -51,12 +44,6 @@
         return (k // 2, k % 2, z, yl, c) if 0 <= k < 8 else None
 
     return target
-
-
-def total(value, axes):
-    count = lax.axis_size(axes)
-    copies = lax.optimization_barrier(jnp.broadcast_to(value[None], (count,) + value.shape))
-    return jnp.sum(lax.all_to_all(copies, axes, 0, 0), axis=0)
 
 
 CHUNK = 16
@@ -102,16 +89,57 @@
     over_rows(block.shape[0], step)
 
 
-def middle_kernel(
-    h0, h1, h2, e0, e1, e2, t0, t1, t2, grad2, gain, grad_mixed, first, second, mixed, partial
-):
+def gather(where, pieces, whole, semaphores, slabs):
+    copies = {}
+    for k in slabs:
+        for r in range(4):
+            ref, slab = pieces[r][k]
+            part = ref.shape[-2]
+            place = pl.ds(pl.multiple_of(where[r], 128), part)
+            copies[k, r] = pltpu.make_async_copy(
+                ref.at[slab] if slab is not None else ref,
+                whole.at[k, place],
+                semaphores.at[k, r],
+            )
+            copies[k, r].start()
+
+    def ready(k):
+        for r in range(4):
+            copies[k, r].wait()
+
+    return ready
+
+
+def pieces_of(weight, folded, weight_s, folded_s, up, down, up_s, down_s):
+    return [
+        [(weight, 0), (weight, 1), (weight, 2), (folded, None)],
+        [(weight_s, 0), (weight_s, 1), (weight_s, 2), (folded_s, None)],
+        [(up, 0), (up, 1), (down, 0), (down, 1)],
+        [(up_s, 0), (up_s, 1), (down_s, 0), (down_s, 1)],
+    ]
+
+
+def middle_kernel(*refs):
+    where, h0, h1, h2, e0, e1, e2, cotangent, gain = refs[:9]
+    grad_mixed, sums, whole, mixed, grad2, partial, semaphores = refs[17:]
+    ready = gather(where, pieces_of(*refs[9:17]), whole, semaphores, (3, 1, 0, 2))
     rows, width = mixed.shape
     channels = e0.shape[1]
-    for n in range(0, width, 256):
-        cols = slice(n, n + 256)
-        mixed[:, cols] = (
-            dot(h1[...], t1[:, cols]) + dot(h0[...], t0[:, cols]) + dot(h2[...], t2[:, cols])
+    half = whole.shape[1] // 8
+
+    ready(3)
+    for j in range(2):
+        held = jnp.concatenate(
+            [whole[3, (2 * f + j) * half : (2 * f + j + 1) * half, :] for f in range(4)], axis=0
         )
+        product = dot_t(cotangent[:, j * width : (j + 1) * width], held)
+        grad2[...] = product if j == 0 else grad2[...] + product
+    ready(1)
+    mixed[...] = dot(h1[...], whole[1])
+    ready(0)
+    mixed[...] += dot(h0[...], whole[0])
+    ready(2)
+    mixed[...] += dot(h2[...], whole[2])
     partial[...] = jnp.zeros_like(partial)
 
     def step(at):
@@ -123,24 +151,40 @@
         grad_mixed[at, :] = norm_back(grad_a * gain[...], scale, unit).astype(jnp.bfloat16)
 
     over_rows(rows, step)
-    second[...] = jnp.sum(partial[...], axis=0, keepdims=True)
+
+    def put(start, row):
+        for i in range(0, row.shape[1], 128):
+            j = (start + i) // 128
+            sums[:, j : j + 1, :] = jnp.broadcast_to(
+                row[:, i : i + 128][None], (sums.shape[0], 1, 128)
+            )
+
+    put(channels, jnp.sum(partial[...], axis=0, keepdims=True))
     for n in range(0, channels, 256):
         cols = slice(n, n + 256)
-        terms = dot_t(grad_mixed[...], t0[cols, :]) * e0[:, cols]
-        terms += dot_t(grad_mixed[...], t1[cols, :]) * e1[:, cols]
-        terms += dot_t(grad_mixed[...], t2[cols, :]) * e2[:, cols]
-        first[:, cols] = jnp.sum(terms, axis=0, keepdims=True)
-
-
-def last_kernel(block, cotangent, ahead, here, behind, t0, t1, t2, gain, result, grads):
+        terms = dot_t(grad_mixed[...], whole[0, cols, :]) * e0[:, cols]
+        terms += dot_t(grad_mixed[...], whole[1, cols, :]) * e1[:, cols]
+        terms += dot_t(grad_mixed[...], whole[2, cols, :]) * e2[:, cols]
+        put(n, jnp.sum(terms, axis=0, keepdims=True))
+
+
+def spread_kernel(arrived, sums):
+    total = jnp.sum(arrived[...], axis=0, keepdims=True)
+    sums[...] = jnp.broadcast_to(total, sums.shape)
+
+
+def last_kernel(*refs):
+    where, block, cotangent, ahead, here, behind, gain = refs[:7]
+    result, whole, grads, semaphores = refs[15:]
+    ready = gather(where, pieces_of(*refs[7:15]), whole, semaphores, (1, 0, 2))
+    grads_of = ((1, here), (0, ahead), (2, behind))
     rows, channels = block.shape
-    for n in range(0, channels, 256):
-        cols = slice(n, n + 256)
-        grads[:, cols] = (
-            dot_t(here[...], t1[cols, :])
-            + dot_t(ahead[...], t0[cols, :])
-            + dot_t(behind[...], t2[cols, :])
-        )
+    for k, grad in grads_of:
+        ready(k)
+        for n in range(0, channels, 256):
+            cols = slice(n, n + 256)
+            product = dot_t(grad[...], whole[k, cols, :])
+            grads[:, cols] = product if k == 1 else grads[:, cols] + product
 
     def step(at):
         unit, scale = normed(block[at, :].astype(jnp.float32))
@@ -151,14 +195,19 @@
     over_rows(rows, step)
 
 
-def call(kernel, name, out_shape, scratch, flops, *operands):
+VMEM_SPEC = pl.BlockSpec(memory_space=pltpu.VMEM)
+SMEM_SPEC = pl.BlockSpec(memory_space=pltpu.SMEM)
+ANY_SPEC = pl.BlockSpec(memory_space=pl.ANY)
+
+
+def call(kernel, name, out_shape, scratch, flops, *operands, specs=None):
     moved = sum(v.size * v.dtype.itemsize for v in operands)
     return pl.pallas_call(
         kernel,
         name=name,
         out_shape=out_shape,
-        in_specs=[pl.BlockSpec(memory_space=pltpu.VMEM)] * len(operands),
-        out_specs=jax.tree.map(lambda _: pl.BlockSpec(memory_space=pltpu.VMEM), out_shape),
+        in_specs=specs or [VMEM_SPEC] * len(operands),
+        out_specs=jax.tree.map(lambda _: VMEM_SPEC, out_shape),
         scratch_shapes=scratch,
         cost_estimate=pl.CostEstimate(flops=flops, bytes_accessed=moved, transcendentals=0),
         compiler_params=pltpu.CompilerParams(vmem_limit_bytes=VMEM_LIMIT),
@@ -183,40 +232,14 @@
     cotangent = grad_output.reshape(rows, channels)
 
     own = lax.axis_index(FSDP)
-    odd = lax.axis_index("z") % 2
+    where = jnp.stack([(own ^ r) * part for r in range(4)])
 
     folded = jnp.concatenate([project[:, :width], project[:, width:]], axis=0)
-    slabs = [weight[0], weight[1], weight[2], folded]
-    near_u = jnp.where(odd == 0, slabs[0], slabs[2])
-    near_d = jnp.where(odd == 0, slabs[1], slabs[3])
-    weight_s = permute(weight, sister)
-    up = permute(near_u, along_y(1))
-    down = permute(near_d, along_y(-1))
-    slabs_s = [weight_s[0], weight_s[1], weight_s[2], permute(folded, sister)]
-    up_z = permute(up, along_z(1))
-    down_z = permute(down, along_z(-1))
-    first = [up, down, up_z, down_z]
-    second = [permute(piece, sister) for piece in first]
-
-    def far(pieces, k):
-        return jnp.where(odd == 0, pieces[k], pieces[k ^ 2])
-
-    def full(k):
-        whole = jnp.zeros((4 * part, width), jnp.bfloat16)
-        for piece, f in (
-            (slabs[k], own),
-            (slabs_s[k], own ^ 1),
-            (far(first, k), own ^ 2),
-            (far(second, k), own ^ 3),
-        ):
-            whole = lax.dynamic_update_slice(whole, piece, (f * part, 0))
-        return whole
-
-    taps = [full(k) for k in range(3)]
-    proj = full(3).reshape(4, 2, part_h, width)
-    proj = [proj[:, j].reshape(4 * part_h, width) for j in range(2)]
-
-    grad_hidden2 = dot_t(cotangent[:, :width], proj[0]) + dot_t(cotangent[:, width:], proj[1])
+    up = permute(weight[:2], along_y(1))
+    down = permute(jnp.stack([weight[2], folded]), along_y(-1))
+    weight_s, folded_s = permute(weight, sister), permute(folded, sister)
+    up_s, down_s = permute(up, sister), permute(down, sister)
+    pieces = (weight, folded, weight_s, folded_s, up, down, up_s, down_s)
 
     f32, bf16 = jnp.float32, jnp.bfloat16
     gain1, gain2 = gain_first[None], gain_second[None]
@@ -241,44 +264,58 @@
     weighs = [pair[1] for pair in pairs]
 
     work = 2 * rows * channels * width
-    grad_mixed, first_sum, second_sum = call(
+    grad_mixed, sums = call(
         middle_kernel,
         "middle",
         [
             jax.ShapeDtypeStruct((rows, width), bf16),
-            jax.ShapeDtypeStruct((1, channels), f32),
-            jax.ShapeDtypeStruct((1, width), f32),
+            jax.ShapeDtypeStruct((32, (channels + width) // 128, 128), f32),
         ],
-        [pltpu.VMEM((rows, width), f32), pltpu.VMEM((8, width), f32)],
-        6 * work,
+        [
+            pltpu.VMEM((4, channels, width), bf16),
+            pltpu.VMEM((rows, width), f32),
+            pltpu.VMEM((rows, width), f32),
+            pltpu.VMEM((8, width), f32),
+            pltpu.SemaphoreType.DMA((4, 4)),
+        ],
+        8 * work,
+        where,
         *hiddens,
         *weighs,
-        *taps,
-        grad_hidden2,
+        cotangent,
         gain2,
-    )
-    first_sum, second_sum = first_sum[0], second_sum[0]
+        *pieces,
+        specs=[SMEM_SPEC] + [VMEM_SPEC] * 8 + [ANY_SPEC] * 8,
+    )
     ahead = permute(grad_mixed, along_bins(-1))
     behind = permute(grad_mixed, along_bins(1))
 
-    sums = jnp.concatenate([first_sum, second_sum]).reshape(-1, 128)
-    sums = total(sums, ("x", "yh", "yl", "c"))
+    sums = lax.all_to_all(sums, ("x", "yh", "yl", "c"), 0, 0)
+    sums = call(
+        spread_kernel, "spread", jax.ShapeDtypeStruct((16,) + sums.shape[1:], f32), [], 1, sums
+    )
     ahead, behind, sums = lax.optimization_barrier((ahead, behind, sums))
-    sums = total(sums, "z").reshape(-1)
+    sums = jnp.sum(lax.all_to_all(sums, "z", 0, 0), axis=0).reshape(-1)
 
     grad_input = call(
         last_kernel,
         "last",
         jax.ShapeDtypeStruct(inputs.shape, bf16),
-        [pltpu.VMEM(inputs.shape, f32)],
+        [
+            pltpu.VMEM((3, channels, width), bf16),
+            pltpu.VMEM(inputs.shape, f32),
+            pltpu.SemaphoreType.DMA((3, 4)),
+        ],
         3 * work,
+        where,
         inputs,
         cotangent,
         ahead,
         grad_mixed,
         behind,
-        *taps,
         gain1,
+        *pieces,
+        specs=[SMEM_SPEC] + [VMEM_SPEC] * 6 + [ANY_SPEC] * 8,
     )
     return (grad_input.reshape(block_input.shape), sums[:channels], sums[channels:])
 

time: 173 us -> 158 us (0.913)
  the two profiles are of different devices: /device:TPU:24 before, /device:TPU:34 now
where the time goes in v4:
time: 158 us; the launch traced here: 157 us
  waiting for transfers between devices  50.5 us (32%)
  starting transfers between devices  46.8 us (30%)
  Pallas kernels  23.1 us (15%)
  blocking collectives  19.9 us (13%)
  local copies, waits for them, and re-layouts  13.9 us (9%)
  other arithmetic  2.05 us (1%)
    ppermute x10, waiting for transfers between devices, permute(): return lax.ppermute(value, AXES, pairs)  43.8 us
    ppermute x10, starting transfers between devices, permute(): return lax.ppermute(value, AXES, pairs)  31.6 us
    pallas_call x6, Pallas kernels, call(): pl.pallas_call(kernel, name=name, out_shape=out_shape, in_specs=specs or...  23.1 us
    all_to_all x1, blocking collectives, body(): sums = lax.all_to_all(sums, ('x', 'yh', 'yl', 'c'), 0, 0)  19.9 us
    all_to_all x1, starting transfers between devices, body(): sums = jnp.sum(lax.all_to_all(sums, 'z', 0, 0), axis=0).reshape(-1)  15.2 us
    unnamed x34, local copies, waits for them, and re-layouts  11 us
    all_to_all x1, waiting for transfers between devices, body(): sums = jnp.sum(lax.all_to_all(sums, 'z', 0, 0), axis=0).reshape(-1)  6.7 us
  transfers between devices with their start and end apart: 11, of which 3 were waited for; matrix products, arithmetic and copies ran while one was open for 1% of the time, Pallas kernels for 9%

profile of v4, /device:TPU:34, one launch (start us, length us, event | category | flops | bytes accessed | tf_op | source)
XLA Modules:
  0.0 157.3 jit_solution(8705260256525915997)
XLA Ops:
  0.6 1.3 slice.26
  2.0 3.6 %collective-permute-start.4 = (bf16[2,384,768]{2,1,0:T(8,128)(2,1)S(1)}, bf16[2,384,768]{2,1,0:T(8,128)(2,1)}, u32[]{:S(2)}, u32[]{:S(2)}) collective-permute-start(bf16[2,384,768]{2,1,0:T(8,128)(2,1)S(1)} %slice.26), channel_id=1, source_target_pairs={{0,2},{1,3},{2,64},{3,65},{4,6},{5,7},{6,68},{7,69},{8,10},{9,11},... | collective-permute-start | bytes 3538952 | tf_op jit(solution)/shard_map/ppermute | solution.py:26
  7.0 3.7 %collective-permute-start.5 = (bf16[2,384,768]{2,1,0:T(8,128)(2,1)S(1)}, bf16[2,384,768]{2,1,0:T(8,128)(2,1)}, u32[]{:S(2)}, u32[]{:S(2)}) collective-permute-start(bf16[2,384,768]{2,1,0:T(8,128)(2,1)S(1)} %pad_maximum_fusion), channel_id=1, source_target_pairs={{0,66},{1,67},{2,0},{3,1},{4,70},{5,71},{6,4},{7,5},{8,74},{9,75},... | collective-permute-start | bytes 3538952 | tf_op jit(solution)/shard_map/ppermute | solution.py:26
  10.7 1.9 %collective-permute-start.2 = (bf16[3,384,768]{2,1,0:T(8,128)(2,1)S(1)}, bf16[3,384,768]{2,1,0:T(8,128)(2,1)}, u32[]{:S(2)}, u32[]{:S(2)}) collective-permute-start(bf16[3,384,768]{2,1,0:T(8,128)(2,1)S(1)} %copy-done), channel_id=1, source_target_pairs={{0,1},{1,0},{2,3},{3,2},{4,5},{5,4},{6,7},{7,6},{8,9},{9,8},{10,11... | collective-permute-start | bytes 5308424 | tf_op jit(solution)/shard_map/ppermute | solution.py:26
  12.7 1.8 %prepare.3 = (bf16[256,1536]{1,0:T(8,128)(2,1)S(1)}, f32[256,1536]{1,0:T(8,128)S(1)}) custom-call(bf16[256,1536]{1,0:T(8,128)(2,1)S(1)} %bitcast.13, f32[1,1536]{1,0:T(1,128)S(1)} %broadcast_in_dim.6.gain.refs_6_), custom_call_target="tpu_custom_call" | custom-call | flops 15728640 | bytes 792576 | tf_op jit(solution)/shard_map/prepare/pallas_call | solution.py:205
  14.5 1.2 copy-done.10
  16.6 3.9 %collective-permute-start = (bf16[256,1536]{1,0:T(8,128)(2,1)S(1)}, bf16[256,1536]{1,0:T(8,128)(2,1)S(1)}, u32[]{:S(2)}, u32[]{:S(2)}) collective-permute-start(bf16[256,1536]{1,0:T(8,128)(2,1)S(1)} %bitcast.14), channel_id=1, source_target_pairs={{0,64},{1,65},{2,66},{3,67},{4,68},{5,69},{6,70},{7,71},{8,72},{9,... | collective-permute-start | bytes 2359304 | tf_op jit(solution)/shard_map/ppermute | solution.py:26
  20.5 29.5 %collective-permute-done.4.refs_13_.refs_11_ = bf16[2,384,768]{2,1,0:T(8,128)(2,1)} collective-permute-done((bf16[2,384,768]{2,1,0:T(8,128)(2,1)S(1)}, bf16[2,384,768]{2,1,0:T(8,128)(2,1)}, u32[]{:S(2)}, u32[]{:S(2)}) %collective-permute-start.4) | collective-permute-done | bytes 1179680 | tf_op jit(solution)/shard_map/ppermute | solution.py:26
  50.0 1.9 %collective-permute-start.6 = (bf16[2,384,768]{2,1,0:T(8,128)(2,1)}, bf16[2,384,768]{2,1,0:T(8,128)(2,1)}, u32[]{:S(2)}, u32[]{:S(2)}) collective-permute-start(bf16[2,384,768]{2,1,0:T(8,128)(2,1)} %collective-permute-done.4.refs_13_.refs_11_), channel_id=1, source_target_pairs={{0,1},{1,0},{2,3},{3,2},{4,5},{5,4},{6,7},{7,6},{8,9},{9,8},{10,11... | collective-permute-start | bytes 3538952 | tf_op jit(solution)/shard_map/ppermute | solution.py:26
  51.9 2.4 %collective-permute-start.7 = (bf16[2,384,768]{2,1,0:T(8,128)(2,1)}, bf16[2,384,768]{2,1,0:T(8,128)(2,1)}, u32[]{:S(2)}, u32[]{:S(2)}) collective-permute-start(bf16[2,384,768]{2,1,0:T(8,128)(2,1)} %collective-permute-done.5.refs_14_.refs_12_), channel_id=1, source_target_pairs={{0,1},{1,0},{2,3},{3,2},{4,5},{5,4},{6,7},{7,6},{8,9},{9,8},{10,11... | collective-permute-start | bytes 3538952 | tf_op jit(solution)/shard_map/ppermute | solution.py:26
  54.3 3.8 %collective-permute-start.1 = (bf16[256,1536]{1,0:T(8,128)(2,1)S(1)}, bf16[256,1536]{1,0:T(8,128)(2,1)}, u32[]{:S(2)}, u32[]{:S(2)}) collective-permute-start(bf16[256,1536]{1,0:T(8,128)(2,1)S(1)} %bitcast.15), channel_id=1, source_target_pairs={{64,0},{65,1},{66,2},{67,3},{68,4},{69,5},{70,6},{71,7},{72,8},{73... | collective-permute-start | bytes 2359304 | tf_op jit(solution)/shard_map/ppermute | solution.py:26
  59.0 2.1 %collective-permute-start.3 = (bf16[384,768]{1,0:T(8,128)(2,1)}, bf16[384,768]{1,0:T(8,128)(2,1)S(1)}, u32[]{:S(2)}, u32[]{:S(2)}) collective-permute-start(bf16[384,768]{1,0:T(8,128)(2,1)} %get-tuple-element.32.refs_10_.refs_8_), channel_id=1, source_target_pairs={{0,1},{1,0},{2,3},{3,2},{4,5},{5,4},{6,7},{7,6},{8,9},{9,8},{10,11... | collective-permute-start | bytes 1769480 | tf_op jit(solution)/shard_map/ppermute | solution.py:26
  61.2 1.1 copy-done.3
  62.4 1.8 %prepare.4 = (bf16[256,1536]{1,0:T(8,128)(2,1)S(1)}, f32[256,1536]{1,0:T(8,128)S(1)}) custom-call(bf16[256,1536]{1,0:T(8,128)(2,1)S(1)} %copy-done.3, f32[1,1536]{1,0:T(1,128)S(1)} %broadcast_in_dim.6.gain.refs_6_), custom_call_target="tpu_custom_call" | custom-call | flops 15728640 | bytes 792576 | tf_op jit(solution)/shard_map/prepare/pallas_call | solution.py:205
  64.1 14.3 %collective-permute-done.1.block = bf16[256,1536]{1,0:T(8,128)(2,1)} collective-permute-done((bf16[256,1536]{1,0:T(8,128)(2,1)S(1)}, bf16[256,1536]{1,0:T(8,128)(2,1)}, u32[]{:S(2)}, u32[]{:S(2)}) %collective-permute-start.1) | collective-permute-done | bytes 786464 | tf_op jit(solution)/shard_map/ppermute | solution.py:26
  78.5 2.9 %prepare.5 = (bf16[256,1536]{1,0:T(8,128)(2,1)S(1)}, f32[256,1536]{1,0:T(8,128)S(1)}) custom-call(bf16[256,1536]{1,0:T(8,128)(2,1)} %collective-permute-done.1.block, f32[1,1536]{1,0:T(1,128)S(1)} %broadcast_in_dim.6.gain.refs_6_), custom_call_target="tpu_custom_call" | custom-call | flops 15728640 | bytes 792576 | tf_op jit(solution)/shard_map/prepare/pallas_call | solution.py:205
  82.5 1.1 copy-done.13
  83.7 9.4 %middle.1 = (bf16[256,768]{1,0:T(8,128)(2,1)S(1)}, f32[32,18,128]{2,1,0:T(8,128)S(1)}) custom-call(s32[4]{0:T(128)S(1)} %pad_add_fusion.refs_0_, bf16[256,1536]{1,0:T(8,128)(2,1)S(1)} %get-tuple-element.20.refs_1_, bf16[256,1536]{1,0:T(8,128)(2,1)S(1)} %copy-done.13, bf16[256,1536]{1,0:T(8,128)(2,1)S(1)} %get-tuple-element.22.refs_3_, ...), custom_call_target="tpu_custom_call" | custom-call | flops 4831838208 | bytes 17304592 | tf_op jit(solution)/shard_map/middle/pallas_call | solution.py:205
  93.1 6.0 %collective-permute-start.9 = (bf16[256,768]{1,0:T(8,128)(2,1)S(1)}, bf16[256,768]{1,0:T(8,128)(2,1)S(1)}, u32[]{:S(2)}, u32[]{:S(2)}) collective-permute-start(bf16[256,768]{1,0:T(8,128)(2,1)S(1)} %get-tuple-element.26.refs_4_), channel_id=1, source_target_pairs={{0,64},{1,65},{2,66},{3,67},{4,68},{5,69},{6,70},{7,71},{8,72},{9,... | collective-permute-start | bytes 1179656 | tf_op jit(solution)/shard_map/ppermute | solution.py:26
  99.1 2.2 %collective-permute-start.8 = (bf16[256,768]{1,0:T(8,128)(2,1)S(1)}, bf16[256,768]{1,0:T(8,128)(2,1)S(1)}, u32[]{:S(2)}, u32[]{:S(2)}) collective-permute-start(bf16[256,768]{1,0:T(8,128)(2,1)S(1)} %get-tuple-element.26.refs_4_), channel_id=1, source_target_pairs={{64,0},{65,1},{66,2},{67,3},{68,4},{69,5},{70,6},{71,7},{72,8},{73... | collective-permute-start | bytes 1179656 | tf_op jit(solution)/shard_map/ppermute | solution.py:26
  101.3 19.9 %all_to_all.10.arrived = f32[32,18,128]{2,1,0:T(8,128)S(1)} all-to-all(f32[32,18,128]{2,1,0:T(8,128)S(1)} %get-tuple-element.27), channel_id=1, replica_groups=mesh['x'=4,'yh'=2,'z'=16,'yl'=2,'c'=2] {'x','yh','yl','c'}, dimensions={0} | all-to-all | bytes 589824 | tf_op jit(solution)/shard_map/all_to_all | solution.py:293
  123.5 15.2 %all-to-all-start.1 = ((f32[16,18,128]{2,1,0:T(8,128)}), f32[16,18,128]{2,1,0:T(8,128)}, u32[]{:S(2)}, u32[]{:S(2)}) async-start(f32[16,18,128]{2,1,0:T(8,128)} %spread.1), calls=%async_computation.1 | async-start | bytes 393216 | tf_op jit(solution)/shard_map/all_to_all | solution.py:298
  141.9 6.5 %last.1 = bf16[256,1536]{1,0:T(8,128)(2,1)} custom-call(s32[4]{0:T(128)S(1)} %pad_add_fusion.refs_0_, bf16[256,1536]{1,0:T(8,128)(2,1)S(1)} %bitcast.16, bf16[256,1536]{1,0:T(8,128)(2,1)S(1)} %bitcast.18, bf16[256,768]{1,0:T(8,128)(2,1)S(1)} %copy-done.9, bf16[256,768]{1,0:T(8,128)(2,1)S(1)} %get-tuple-element.26.refs_4_, bf16[256,768]{1,0:T(8,128)(2,1)S(1)} %copy-done.7, ...), custom_call_target="tpu_custom_call" | custom-call | flops 1811939328 | bytes 12195856 | tf_op jit(solution)/shard_map/last/pallas_call | solution.py:205
  148.4 6.7 %all-to-all-done.1 = f32[16,18,128]{2,1,0:T(8,128)} async-done(((f32[16,18,128]{2,1,0:T(8,128)}), f32[16,18,128]{2,1,0:T(8,128)}, u32[]{:S(2)}, u32[]{:S(2)}) %all-to-all-start.1) | async-done | bytes 147488 | tf_op jit(solution)/shard_map/all_to_all | solution.py:298
  (51 shorter events, 12.0 us)
Async XLA Ops:
  2.0 3.6 %copy-start.14 = (bf16[192,1536]{1,0:T(8,128)(2,1)S(1)}, bf16[192,1536]{1,0:T(8,128)(2,1)}, u32[]{:S(2)}) copy-start(bf16[192,1536]{1,0:T(8,128)(2,1)} %param.8) | copy-start | bytes 1769476
  2.0 48.0 %collective-permute-start.4 = (bf16[2,384,768]{2,1,0:T(8,128)(2,1)S(1)}, bf16[2,384,768]{2,1,0:T(8,128)(2,1)}, u32[]{:S(2)}, u32[]{:S(2)}) collective-permute-start(bf16[2,384,768]{2,1,0:T(8,128)(2,1)S(1)} %slice.26), channel_id=1, source_target_pairs={{0,2},{1,3},{2,64},{3,65},{4,6},{5,7},{6,68},{7,69},{8,10},{9,11},... | collective-permute-start | bytes 3538952 | tf_op jit(solution)/shard_map/ppermute | solution.py:26
  5.7 1.2 slice-start
  5.7 7.0 %copy-start.1 = (bf16[2,128,1536]{2,1,0:T(8,128)(2,1)S(1)}, bf16[2,128,1536]{2,1,0:T(8,128)(2,1)}, u32[]{:S(2)}) copy-start(bf16[2,128,1536]{2,1,0:T(8,128)(2,1)} %param.6) | copy-start | bytes 2359300
  6.9 3.8 %copy-start = (bf16[3,384,768]{2,1,0:T(8,128)(2,1)S(1)}, bf16[3,384,768]{2,1,0:T(8,128)(2,1)}, u32[]{:S(2)}) copy-start(bf16[3,384,768]{2,1,0:T(8,128)(2,1)} %refs_7_.1) | copy-start | bytes 5308420
  6.9 5.8 %copy-start.15 = (f32[1536]{0:T(1024)S(1)}, f32[1536]{0:T(1024)}, u32[]{:S(2)}) copy-start(f32[1536]{0:T(1024)} %param.9) | copy-start | bytes 18436
  6.9 54.2 %copy-start.16 = (f32[768]{0:T(1024)S(1)}, f32[768]{0:T(1024)}, u32[]{:S(2)}) copy-start(f32[768]{0:T(1024)} %param.10) | copy-start | bytes 9220
  7.0 44.9 %collective-permute-start.5 = (bf16[2,384,768]{2,1,0:T(8,128)(2,1)S(1)}, bf16[2,384,768]{2,1,0:T(8,128)(2,1)}, u32[]{:S(2)}, u32[]{:S(2)}) collective-permute-start(bf16[2,384,768]{2,1,0:T(8,128)(2,1)S(1)} %pad_maximum_fusion), channel_id=1, source_target_pairs={{0,66},{1,67},{2,0},{3,1},{4,70},{5,71},{6,4},{7,5},{8,74},{9,75},... | collective-permute-start | bytes 3538952 | tf_op jit(solution)/shard_map/ppermute | solution.py:26
  10.7 70.6 %collective-permute-start.2 = (bf16[3,384,768]{2,1,0:T(8,128)(2,1)S(1)}, bf16[3,384,768]{2,1,0:T(8,128)(2,1)}, u32[]{:S(2)}, u32[]{:S(2)}) collective-permute-start(bf16[3,384,768]{2,1,0:T(8,128)(2,1)S(1)} %copy-done), channel_id=1, source_target_pairs={{0,1},{1,0},{2,3},{3,2},{4,5},{5,4},{6,7},{7,6},{8,9},{9,8},{10,11... | collective-permute-start | bytes 5308424 | tf_op jit(solution)/shard_map/ppermute | solution.py:26
  14.5 1.2 copy-start.10
  16.6 41.5 %collective-permute-start = (bf16[256,1536]{1,0:T(8,128)(2,1)S(1)}, bf16[256,1536]{1,0:T(8,128)(2,1)S(1)}, u32[]{:S(2)}, u32[]{:S(2)}) collective-permute-start(bf16[256,1536]{1,0:T(8,128)(2,1)S(1)} %bitcast.14), channel_id=1, source_target_pairs={{0,64},{1,65},{2,66},{3,67},{4,68},{5,69},{6,70},{7,71},{8,72},{9,... | collective-permute-start | bytes 2359304 | tf_op jit(solution)/shard_map/ppermute | solution.py:26
  50.0 31.4 %collective-permute-start.6 = (bf16[2,384,768]{2,1,0:T(8,128)(2,1)}, bf16[2,384,768]{2,1,0:T(8,128)(2,1)}, u32[]{:S(2)}, u32[]{:S(2)}) collective-permute-start(bf16[2,384,768]{2,1,0:T(8,128)(2,1)} %collective-permute-done.4.refs_13_.refs_11_), channel_id=1, source_target_pairs={{0,1},{1,0},{2,3},{3,2},{4,5},{5,4},{6,7},{7,6},{8,9},{9,8},{10,11... | collective-permute-start | bytes 3538952 | tf_op jit(solution)/shard_map/ppermute | solution.py:26
  51.9 29.5 %collective-permute-start.7 = (bf16[2,384,768]{2,1,0:T(8,128)(2,1)}, bf16[2,384,768]{2,1,0:T(8,128)(2,1)}, u32[]{:S(2)}, u32[]{:S(2)}) collective-permute-start(bf16[2,384,768]{2,1,0:T(8,128)(2,1)} %collective-permute-done.5.refs_14_.refs_12_), channel_id=1, source_target_pairs={{0,1},{1,0},{2,3},{3,2},{4,5},{5,4},{6,7},{7,6},{8,9},{9,8},{10,11... | collective-permute-start | bytes 3538952 | tf_op jit(solution)/shard_map/ppermute | solution.py:26
  54.3 24.1 %collective-permute-start.1 = (bf16[256,1536]{1,0:T(8,128)(2,1)S(1)}, bf16[256,1536]{1,0:T(8,128)(2,1)}, u32[]{:S(2)}, u32[]{:S(2)}) collective-permute-start(bf16[256,1536]{1,0:T(8,128)(2,1)S(1)} %bitcast.15), channel_id=1, source_target_pairs={{64,0},{65,1},{66,2},{67,3},{68,4},{69,5},{70,6},{71,7},{72,8},{73... | collective-permute-start | bytes 2359304 | tf_op jit(solution)/shard_map/ppermute | solution.py:26
  59.0 22.3 %collective-permute-start.3 = (bf16[384,768]{1,0:T(8,128)(2,1)}, bf16[384,768]{1,0:T(8,128)(2,1)S(1)}, u32[]{:S(2)}, u32[]{:S(2)}) collective-permute-start(bf16[384,768]{1,0:T(8,128)(2,1)} %get-tuple-element.32.refs_10_.refs_8_), channel_id=1, source_target_pairs={{0,1},{1,0},{2,3},{3,2},{4,5},{5,4},{6,7},{7,6},{8,9},{9,8},{10,11... | collective-permute-start | bytes 1769480 | tf_op jit(solution)/shard_map/ppermute | solution.py:26
  61.2 1.1 copy-start.3
  62.4 19.0 %copy-start.11 = (f32[256,1536]{1,0:T(8,128)S(1)}, f32[256,1536]{1,0:T(8,128)}, u32[]{:S(2)}) copy-start(f32[256,1536]{1,0:T(8,128)} %copy-done.10) | copy-start | bytes 4718596
  81.4 1.1 copy-start.4
  82.5 1.1 copy-start.13
  93.1 28.9 %collective-permute-start.9 = (bf16[256,768]{1,0:T(8,128)(2,1)S(1)}, bf16[256,768]{1,0:T(8,128)(2,1)S(1)}, u32[]{:S(2)}, u32[]{:S(2)}) collective-permute-start(bf16[256,768]{1,0:T(8,128)(2,1)S(1)} %get-tuple-element.26.refs_4_), channel_id=1, source_target_pairs={{0,64},{1,65},{2,66},{3,67},{4,68},{5,69},{6,70},{7,71},{8,72},{9,... | collective-permute-start | bytes 1179656 | tf_op jit(solution)/shard_map/ppermute | solution.py:26
  99.1 23.7 %collective-permute-start.8 = (bf16[256,768]{1,0:T(8,128)(2,1)S(1)}, bf16[256,768]{1,0:T(8,128)(2,1)S(1)}, u32[]{:S(2)}, u32[]{:S(2)}) collective-permute-start(bf16[256,768]{1,0:T(8,128)(2,1)S(1)} %get-tuple-element.26.refs_4_), channel_id=1, source_target_pairs={{64,0},{65,1},{66,2},{67,3},{68,4},{69,5},{70,6},{71,7},{72,8},{73... | collective-permute-start | bytes 1179656 | tf_op jit(solution)/shard_map/ppermute | solution.py:26
  123.5 31.6 %all-to-all-start.1 = ((f32[16,18,128]{2,1,0:T(8,128)}), f32[16,18,128]{2,1,0:T(8,128)}, u32[]{:S(2)}, u32[]{:S(2)}) async-start(f32[16,18,128]{2,1,0:T(8,128)} %spread.1), calls=%async_computation.1 | async-start | bytes 393216 | tf_op jit(solution)/shard_map/all_to_all | solution.py:298
  138.7 1.1 copy-start.5
  139.9 1.0 copy-start.7
  (5 other events, 4.3 us)

commit v5 on v4

--- a/solution.py
+++ b/solution.py
@@ -12,7 +12,7 @@
 SEQ = ("x", "yh", "z")
 FSDP = ("yl", "c")
 HALF = 0.7978845608028654
-VMEM_LIMIT = 32 * 1024 * 1024
+VMEM_LIMIT = 16 * 1024 * 1024
 
 
 def permute(value, target):
@@ -38,12 +38,18 @@
     return (x, yh, z, yl, 1 - c)
 
 
-def along_bins(steps):
-    def target(x, yh, z, yl, c):
-        k = 2 * x + yh + steps
-        return (k // 2, k % 2, z, yl, c) if 0 <= k < 8 else None
-
-    return target
+def antipode(x, yh, z, yl, c):
+    return (x, 1 - yh, z, yl, c)
+
+
+def hand_on(x, yh, z, yl, c):
+    to = x + 1 - 2 * yh
+    return (to, yh, z, yl, c) if 0 <= to < 4 else None
+
+
+def second_neighbour(x, yh, z, yl, c):
+    to = x + 1 - 2 * (1 - yh)
+    return (to, 1 - yh, z, yl, c) if 0 <= to < 4 else None
 
 
 CHUNK = 16
@@ -98,7 +104,7 @@
             place = pl.ds(pl.multiple_of(where[r], 128), part)
             copies[k, r] = pltpu.make_async_copy(
                 ref.at[slab] if slab is not None else ref,
-                whole.at[k, place],
+                whole.at[k ^ where[4] if k in (0, 2) else k, place],
                 semaphores.at[k, r],
             )
             copies[k, r].start()
@@ -119,15 +125,27 @@
     ]
 
 
-def middle_kernel(*refs):
-    where, h0, h1, h2, e0, e1, e2, cotangent, gain = refs[:9]
-    grad_mixed, sums, whole, mixed, grad2, partial, semaphores = refs[17:]
-    ready = gather(where, pieces_of(*refs[9:17]), whole, semaphores, (3, 1, 0, 2))
-    rows, width = mixed.shape
-    channels = e0.shape[1]
+def fetch(sources, places, semaphores):
+    copies = [
+        pltpu.make_async_copy(source, place, semaphores.at[i])
+        for i, (source, place) in enumerate(zip(sources, places))
+    ]
+    for copy in copies:
+        copy.start()
+    return lambda i: copies[i].wait()
+
+
+def early_kernel(*refs):
+    where = refs[0]
+    whole, mixed, grad2, semaphores, held_rows, row_semaphores = refs[11:]
+    hidden, cotangent = held_rows.at[0], held_rows.at[1]
+    fetched = fetch((refs[1], refs[2]), (hidden, cotangent), row_semaphores)
+    ready = gather(where, pieces_of(*refs[3:11]), whole, semaphores, (3, 1, 0, 2))
+    width = mixed.shape[1]
     half = whole.shape[1] // 8
 
     ready(3)
+    fetched(1)
     for j in range(2):
         held = jnp.concatenate(
             [whole[3, (2 * f + j) * half : (2 * f + j + 1) * half, :] for f in range(4)], axis=0
@@ -135,11 +153,26 @@
         product = dot_t(cotangent[:, j * width : (j + 1) * width], held)
         grad2[...] = product if j == 0 else grad2[...] + product
     ready(1)
-    mixed[...] = dot(h1[...], whole[1])
+    fetched(0)
+    mixed[...] = dot(hidden[...], whole[1])
     ready(0)
-    mixed[...] += dot(h0[...], whole[0])
     ready(2)
-    mixed[...] += dot(h2[...], whole[2])
+
+
+def middle_kernel(
+    h0_away, h2, e0_away, e1_away, e2_away, whole, centre, grad2, gain, grad_mixed, sums, mixed,
+    partial, h0, e0, e1, e2, semaphores,
+):
+    fetched = fetch((h0_away, e0_away, e1_away, e2_away), (h0, e0, e1, e2), semaphores)
+    rows, width = mixed.shape
+    channels = e0.shape[1]
+    for n in range(0, width, 256):
+        cols = slice(n, n + 256)
+        mixed[:, cols] = centre[:, cols] + dot(h2[...], whole[2, :, cols])
+    fetched(0)
+    for n in range(0, width, 256):
+        cols = slice(n, n + 256)
+        mixed[:, cols] += dot(h0[...], whole[0, :, cols])
     partial[...] = jnp.zeros_like(partial)
 
     def step(at):
@@ -159,6 +192,8 @@
                 row[:, i : i + 128][None], (sums.shape[0], 1, 128)
             )
 
+    for i in range(1, 4):
+        fetched(i)
     put(channels, jnp.sum(partial[...], axis=0, keepdims=True))
     for n in range(0, channels, 256):
         cols = slice(n, n + 256)
@@ -173,18 +208,15 @@
     sums[...] = jnp.broadcast_to(total, sums.shape)
 
 
-def last_kernel(*refs):
-    where, block, cotangent, ahead, here, behind, gain = refs[:7]
-    result, whole, grads, semaphores = refs[15:]
-    ready = gather(where, pieces_of(*refs[7:15]), whole, semaphores, (1, 0, 2))
-    grads_of = ((1, here), (0, ahead), (2, behind))
+def last_kernel(block, cotangent, near, here, far, whole, gain, result, grads):
     rows, channels = block.shape
-    for k, grad in grads_of:
-        ready(k)
-        for n in range(0, channels, 256):
-            cols = slice(n, n + 256)
-            product = dot_t(grad[...], whole[k, cols, :])
-            grads[:, cols] = product if k == 1 else grads[:, cols] + product
+    for n in range(0, channels, 256):
+        cols = slice(n, n + 256)
+        grads[:, cols] = (
+            dot_t(here[...], whole[1, cols, :])
+            + dot_t(near[...], whole[2, cols, :])
+            + dot_t(far[...], whole[0, cols, :])
+        )
 
     def step(at):
         unit, scale = normed(block[at, :].astype(jnp.float32))
@@ -232,14 +264,7 @@
     cotangent = grad_output.reshape(rows, channels)
 
     own = lax.axis_index(FSDP)
-    where = jnp.stack([(own ^ r) * part for r in range(4)])
-
-    folded = jnp.concatenate([project[:, :width], project[:, width:]], axis=0)
-    up = permute(weight[:2], along_y(1))
-    down = permute(jnp.stack([weight[2], folded]), along_y(-1))
-    weight_s, folded_s = permute(weight, sister), permute(folded, sister)
-    up_s, down_s = permute(up, sister), permute(down, sister)
-    pieces = (weight, folded, weight_s, folded_s, up, down, up_s, down_s)
+    where = jnp.stack([(own ^ r) * part for r in range(4)] + [2 - 2 * lax.axis_index("yh")])
 
     f32, bf16 = jnp.float32, jnp.bfloat16
     gain1, gain2 = gain_first[None], gain_second[None]
@@ -255,15 +280,43 @@
             gain1,
         )
 
-    own_pair = prepare(inputs)
-    halo, own_pair = lax.optimization_barrier((inputs, own_pair))
-    lagging = permute(halo, along_bins(1))
-    leading = permute(halo, along_bins(-1))
-    pairs = [prepare(lagging), own_pair, prepare(leading)]
-    hiddens = [pair[0] for pair in pairs]
-    weighs = [pair[1] for pair in pairs]
+    near = permute(inputs, antipode)
+    h1, e1 = prepare(inputs)
+    folded = jnp.concatenate([project[:, :width], project[:, width:]], axis=0)
+    sent_up, sent_down, sent, near = lax.optimization_barrier(
+        (weight[:2], jnp.stack([weight[2], folded]), weight, near)
+    )
+    far = permute(near, hand_on)
+    up, down = permute(sent_up, along_y(1)), permute(sent_down, along_y(-1))
+    weight_s, folded_s = permute(sent, sister), permute(sent_down[1], sister)
+    h0, e0 = prepare(near)
+    up, down, far, h0, h1 = lax.optimization_barrier((up, down, far, h0, h1))
+    up_s, down_s = permute(up, sister), permute(down, sister)
+    pieces = (weight, folded, weight_s, folded_s, up, down, up_s, down_s)
+
+    h2, e2 = prepare(far)
 
     work = 2 * rows * channels * width
+    whole, centre, grad2 = call(
+        early_kernel,
+        "early",
+        [
+            jax.ShapeDtypeStruct((4, channels, width), bf16),
+            jax.ShapeDtypeStruct((rows, width), f32),
+            jax.ShapeDtypeStruct((rows, width), f32),
+        ],
+        [
+            pltpu.SemaphoreType.DMA((4, 4)),
+            pltpu.VMEM((2, rows, channels), bf16),
+            pltpu.SemaphoreType.DMA((2,)),
+        ],
+        2 * work,
+        where,
+        h1,
+        cotangent,
+        *pieces,
+        specs=[SMEM_SPEC] + [ANY_SPEC] * 10,
+    )
     grad_mixed, sums = call(
         middle_kernel,
         "middle",
@@ -272,52 +325,53 @@
             jax.ShapeDtypeStruct((32, (channels + width) // 128, 128), f32),
         ],
         [
-            pltpu.VMEM((4, channels, width), bf16),
-            pltpu.VMEM((rows, width), f32),
             pltpu.VMEM((rows, width), f32),
             pltpu.VMEM((8, width), f32),
-            pltpu.SemaphoreType.DMA((4, 4)),
+            pltpu.VMEM((rows, channels), bf16),
+            pltpu.VMEM((rows, channels), f32),
+            pltpu.VMEM((rows, channels), f32),
+            pltpu.VMEM((rows, channels), f32),
+            pltpu.SemaphoreType.DMA((4,)),
         ],
-        8 * work,
-        where,
-        *hiddens,
-        *weighs,
-        cotangent,
+        5 * work,
+        h0,
+        h2,
+        e0,
+        e1,
+        e2,
+        whole,
+        centre,
+        grad2,
         gain2,
-        *pieces,
-        specs=[SMEM_SPEC] + [VMEM_SPEC] * 8 + [ANY_SPEC] * 8,
-    )
-    ahead = permute(grad_mixed, along_bins(-1))
-    behind = permute(grad_mixed, along_bins(1))
-
+        specs=[ANY_SPEC, VMEM_SPEC] + [ANY_SPEC] * 3 + [VMEM_SPEC] * 4,
+    )
     sums = lax.all_to_all(sums, ("x", "yh", "yl", "c"), 0, 0)
     sums = call(
         spread_kernel, "spread", jax.ShapeDtypeStruct((16,) + sums.shape[1:], f32), [], 1, sums
     )
-    ahead, behind, sums = lax.optimization_barrier((ahead, behind, sums))
-    sums = jnp.sum(lax.all_to_all(sums, "z", 0, 0), axis=0).reshape(-1)
+    grad_mixed, sums = lax.optimization_barrier((grad_mixed, sums))
+    near_grad = permute(grad_mixed, antipode)
+    far_grad = permute(grad_mixed, second_neighbour)
+    sums = lax.all_to_all(sums, "z", 0, 0)
 
     grad_input = call(
         last_kernel,
         "last",
         jax.ShapeDtypeStruct(inputs.shape, bf16),
-        [
-            pltpu.VMEM((3, channels, width), bf16),
-            pltpu.VMEM(inputs.shape, f32),
-            pltpu.SemaphoreType.DMA((3, 4)),
-        ],
+        [pltpu.VMEM(inputs.shape, f32)],
         3 * work,
-        where,
         inputs,
         cotangent,
-        ahead,
+        near_grad,
         grad_mixed,
-        behind,
+        far_grad,
+        whole,
         gain1,
-        *pieces,
-        specs=[SMEM_SPEC] + [VMEM_SPEC] * 6 + [ANY_SPEC] * 8,
-    )
-    return (grad_input.reshape(block_input.shape), sums[:channels], sums[channels:])
+    )
+    lines = channels // 128
+    first_sum = jnp.sum(sums[:, :lines], axis=0).reshape(-1)
+    second_sum = jnp.sum(sums[:, lines:], axis=0).reshape(-1)
+    return (grad_input.reshape(block_input.shape), first_sum, second_sum)
 
 
 def solution(mesh):

time: 158 us -> 136 us (0.86)
  the two profiles are of different devices: /device:TPU:34 before, /device:TPU:2 now
where the time goes in v5:
time: 136 us
  starting transfers between devices  47.1 us (35%)
  waiting for transfers between devices  37.4 us (28%)
  Pallas kernels  20.4 us (15%)
  blocking collectives  13.8 us (10%)
  local copies, waits for them, and re-layouts  13.7 us (10%)
  other arithmetic  2.28 us (2%)
    ppermute x10, starting transfers between devices, permute(): return lax.ppermute(value, AXES, pairs)  31.9 us
    ppermute x10, waiting for transfers between devices, permute(): return lax.ppermute(value, AXES, pairs)  28.9 us
    pallas_call x7, Pallas kernels, call(): pl.pallas_call(kernel, name=name, out_shape=out_shape, in_specs=specs or...  20.4 us
    all_to_all x1, starting transfers between devices, body(): sums = lax.all_to_all(sums, 'z', 0, 0)  15.2 us
    all_to_all x1, blocking collectives, body(): sums = lax.all_to_all(sums, ('x', 'yh', 'yl', 'c'), 0, 0)  13.8 us
    unnamed x40, local copies, waits for them, and re-layouts  11 us
    all_to_all x1, waiting for transfers between devices, body(): sums = lax.all_to_all(sums, 'z', 0, 0)  8.55 us
  transfers between devices with their start and end apart: 11, of which 5 were waited for; matrix products, arithmetic and copies ran while one was open for 3% of the time, Pallas kernels for 7%

profile of v5, /device:TPU:2, one launch (start us, length us, event | category | flops | bytes accessed | tf_op | source)
XLA Modules:
  0.0 135.7 jit_solution(16448517212680842984)
XLA Ops:
  0.6 5.1 %collective-permute-start = (bf16[256,1536]{1,0:T(8,128)(2,1)}, bf16[256,1536]{1,0:T(8,128)(2,1)S(1)}, u32[]{:S(2)}, u32[]{:S(2)}) collective-permute-start(bf16[256,1536]{1,0:T(8,128)(2,1)} %bitcast.14), channel_id=1, source_target_pairs={{0,64},{1,65},{2,66},{3,67},{4,68},{5,69},{6,70},{7,71},{8,72},{9,... | collective-permute-start | bytes 2359304 | tf_op jit(solution)/shard_map/ppermute | solution.py:26
  8.6 15.0 %collective-permute-done.block = bf16[256,1536]{1,0:T(8,128)(2,1)S(1)} collective-permute-done((bf16[256,1536]{1,0:T(8,128)(2,1)}, bf16[256,1536]{1,0:T(8,128)(2,1)S(1)}, u32[]{:S(2)}, u32[]{:S(2)}) %collective-permute-start) | collective-permute-done | bytes 786464 | tf_op jit(solution)/shard_map/ppermute | solution.py:26
  23.5 4.9 %collective-permute-start.2 = (bf16[2,384,768]{2,1,0:T(8,128)(2,1)S(1)}, bf16[2,384,768]{2,1,0:T(8,128)(2,1)}, u32[]{:S(2)}, u32[]{:S(2)}) collective-permute-start(bf16[2,384,768]{2,1,0:T(8,128)(2,1)S(1)} %pad_maximum_fusion), channel_id=1, source_target_pairs={{0,66},{1,67},{2,0},{3,1},{4,70},{5,71},{6,4},{7,5},{8,74},{9,75},... | collective-permute-start | bytes 3538952 | tf_op jit(solution)/shard_map/ppermute | solution.py:26
  28.4 1.9 %collective-permute-start.1 = (bf16[2,384,768]{2,1,0:T(8,128)(2,1)S(1)}, bf16[2,384,768]{2,1,0:T(8,128)(2,1)}, u32[]{:S(2)}, u32[]{:S(2)}) collective-permute-start(bf16[2,384,768]{2,1,0:T(8,128)(2,1)S(1)} %slice.21), channel_id=1, source_target_pairs={{0,2},{1,3},{2,64},{3,65},{4,6},{5,7},{6,68},{7,69},{8,10},{9,11},... | collective-permute-start | bytes 3538952 | tf_op jit(solution)/shard_map/ppermute | solution.py:26
  30.4 3.4 %collective-permute-start.3 = (bf16[256,1536]{1,0:T(8,128)(2,1)S(1)}, bf16[256,1536]{1,0:T(8,128)(2,1)S(1)}, u32[]{:S(2)}, u32[]{:S(2)}) collective-permute-start(bf16[256,1536]{1,0:T(8,128)(2,1)S(1)} %collective-permute-done.block), channel_id=1, source_target_pairs={{0,128},{1,129},{2,130},{3,131},{4,132},{5,133},{6,134},{7,135},{8... | collective-permute-start | bytes 2359304 | tf_op jit(solution)/shard_map/ppermute | solution.py:26
  33.8 1.9 %collective-permute-start.4 = (bf16[3,384,768]{2,1,0:T(8,128)(2,1)S(1)}, bf16[3,384,768]{2,1,0:T(8,128)(2,1)}, u32[]{:S(2)}, u32[]{:S(2)}) collective-permute-start(bf16[3,384,768]{2,1,0:T(8,128)(2,1)S(1)} %copy-done.2), channel_id=1, source_target_pairs={{0,1},{1,0},{2,3},{3,2},{4,5},{5,4},{6,7},{7,6},{8,9},{9,8},{10,11... | collective-permute-start | bytes 5308424 | tf_op jit(solution)/shard_map/ppermute | solution.py:26
  35.8 1.8 %prepare.4 = (bf16[256,1536]{1,0:T(8,128)(2,1)S(1)}, f32[256,1536]{1,0:T(8,128)S(1)}) custom-call(bf16[256,1536]{1,0:T(8,128)(2,1)S(1)} %bitcast.15, f32[1,1536]{1,0:T(1,128)S(1)} %broadcast_in_dim.6.gain), custom_call_target="tpu_custom_call" | custom-call | flops 15728640 | bytes 792576 | tf_op jit(solution)/shard_map/prepare/pallas_call | solution.py:237
  39.6 1.8 %prepare.3 = (bf16[256,1536]{1,0:T(8,128)(2,1)S(1)}, f32[256,1536]{1,0:T(8,128)S(1)}) custom-call(bf16[256,1536]{1,0:T(8,128)(2,1)S(1)} %collective-permute-done.block, f32[1,1536]{1,0:T(1,128)S(1)} %broadcast_in_dim.6.gain), custom_call_target="tpu_custom_call" | custom-call | flops 15728640 | bytes 792576 | tf_op jit(solution)/shard_map/prepare/pallas_call | solution.py:237
  43.4 7.0 %collective-permute-done.3.block = bf16[256,1536]{1,0:T(8,128)(2,1)S(1)} collective-permute-done((bf16[256,1536]{1,0:T(8,128)(2,1)S(1)}, bf16[256,1536]{1,0:T(8,128)(2,1)S(1)}, u32[]{:S(2)}, u32[]{:S(2)}) %collective-permute-start.3) | collective-permute-done | bytes 786464 | tf_op jit(solution)/shard_map/ppermute | solution.py:26
  51.3 1.5 %collective-permute-done.2.refs_8_ = bf16[2,384,768]{2,1,0:T(8,128)(2,1)} collective-permute-done((bf16[2,384,768]{2,1,0:T(8,128)(2,1)S(1)}, bf16[2,384,768]{2,1,0:T(8,128)(2,1)}, u32[]{:S(2)}, u32[]{:S(2)}) %collective-permute-start.2) | collective-permute-done | bytes 1179680 | tf_op jit(solution)/shard_map/ppermute | solution.py:26
  52.8 5.4 %collective-permute-done.1.refs_7_ = bf16[2,384,768]{2,1,0:T(8,128)(2,1)} collective-permute-done((bf16[2,384,768]{2,1,0:T(8,128)(2,1)S(1)}, bf16[2,384,768]{2,1,0:T(8,128)(2,1)}, u32[]{:S(2)}, u32[]{:S(2)}) %collective-permute-start.1) | collective-permute-done | bytes 1179680 | tf_op jit(solution)/shard_map/ppermute | solution.py:26
  58.2 1.9 %collective-permute-start.6 = (bf16[2,384,768]{2,1,0:T(8,128)(2,1)}, bf16[2,384,768]{2,1,0:T(8,128)(2,1)}, u32[]{:S(2)}, u32[]{:S(2)}) collective-permute-start(bf16[2,384,768]{2,1,0:T(8,128)(2,1)} %collective-permute-done.1.refs_7_), channel_id=1, source_target_pairs={{0,1},{1,0},{2,3},{3,2},{4,5},{5,4},{6,7},{7,6},{8,9},{9,8},{10,11... | collective-permute-start | bytes 3538952 | tf_op jit(solution)/shard_map/ppermute | solution.py:26
  60.1 2.4 %collective-permute-start.7 = (bf16[2,384,768]{2,1,0:T(8,128)(2,1)}, bf16[2,384,768]{2,1,0:T(8,128)(2,1)}, u32[]{:S(2)}, u32[]{:S(2)}) collective-permute-start(bf16[2,384,768]{2,1,0:T(8,128)(2,1)} %collective-permute-done.2.refs_8_), channel_id=1, source_target_pairs={{0,1},{1,0},{2,3},{3,2},{4,5},{5,4},{6,7},{7,6},{8,9},{9,8},{10,11... | collective-permute-start | bytes 3538952 | tf_op jit(solution)/shard_map/ppermute | solution.py:26
  63.5 2.1 %collective-permute-start.5 = (bf16[384,768]{1,0:T(8,128)(2,1)}, bf16[384,768]{1,0:T(8,128)(2,1)}, u32[]{:S(2)}, u32[]{:S(2)}) collective-permute-start(bf16[384,768]{1,0:T(8,128)(2,1)} %slice_bitcast_fusion), channel_id=1, source_target_pairs={{0,1},{1,0},{2,3},{3,2},{4,5},{5,4},{6,7},{7,6},{8,9},{9,8},{10,11... | collective-permute-start | bytes 1769480 | tf_op jit(solution)/shard_map/ppermute | solution.py:26
  66.8 1.8 %prepare.5 = (bf16[256,1536]{1,0:T(8,128)(2,1)S(1)}, f32[256,1536]{1,0:T(8,128)S(1)}) custom-call(bf16[256,1536]{1,0:T(8,128)(2,1)S(1)} %copy-done.14, f32[1,1536]{1,0:T(1,128)S(1)} %broadcast_in_dim.6.gain), custom_call_target="tpu_custom_call" | custom-call | flops 15728640 | bytes 792576 | tf_op jit(solution)/shard_map/prepare/pallas_call | solution.py:237
  69.8 4.8 %early.1 = (bf16[4,1536,768]{2,1,0:T(8,128)(2,1)S(1)}, f32[256,768]{1,0:T(8,128)S(1)}, f32[256,768]{1,0:T(8,128)S(1)}) custom-call(s32[5]{0:T(128)S(1)} %stack.31.refs_0_, bf16[256,1536]{1,0:T(8,128)(2,1)S(1)} %copy-done.16, bf16[256,1536]{1,0:T(8,128)(2,1)S(1)} %bitcast.17, bf16[3,384,768]{2,1,0:T(8,128)(2,1)S(1)} %copy-done.2, ...), custom_call_target="tpu_custom_call" | custom-call | flops 1207959552 | bytes 11010068 | tf_op jit(solution)/shard_map/early/pallas_call | solution.py:237
  74.6 5.8 %middle.1 = (bf16[256,768]{1,0:T(8,128)(2,1)S(1)}, f32[32,18,128]{2,1,0:T(8,128)S(1)}) custom-call(bf16[256,1536]{1,0:T(8,128)(2,1)S(1)} %copy-done.12, bf16[256,1536]{1,0:T(8,128)(2,1)S(1)} %get-tuple-element.32.h2, f32[256,1536]{1,0:T(8,128)S(1)} %copy-done.10, f32[256,1536]{1,0:T(8,128)S(1)} %copy-done.8, f32[256,1536]{1,0:T(8,128)S(1)} %get-tuple-element.35.e2_away, ...), custom_call_target="tpu_custom_call" | custom-call | flops 3019898880 | bytes 17304576 | tf_op jit(solution)/shard_map/middle/pallas_call | solution.py:237
  80.4 13.8 %all_to_all.10.arrived = f32[32,18,128]{2,1,0:T(8,128)S(1)} all-to-all(f32[32,18,128]{2,1,0:T(8,128)S(1)} %get-tuple-element.44), channel_id=1, replica_groups=mesh['x'=4,'yh'=2,'z'=16,'yl'=2,'c'=2] {'x','yh','yl','c'}, dimensions={0} | all-to-all | bytes 589824 | tf_op jit(solution)/shard_map/all_to_all | solution.py:348
  94.9 3.6 %collective-permute-start.8 = (bf16[256,768]{1,0:T(8,128)(2,1)S(1)}, bf16[256,768]{1,0:T(8,128)(2,1)S(1)}, u32[]{:S(2)}, u32[]{:S(2)}) collective-permute-start(bf16[256,768]{1,0:T(8,128)(2,1)S(1)} %get-tuple-element.45.here), channel_id=1, source_target_pairs={{0,64},{1,65},{2,66},{3,67},{4,68},{5,69},{6,70},{7,71},{8,72},{9,... | collective-permute-start | bytes 1179656 | tf_op jit(solution)/shard_map/ppermute | solution.py:26
  98.5 4.6 %collective-permute-start.9 = (bf16[256,768]{1,0:T(8,128)(2,1)S(1)}, bf16[256,768]{1,0:T(8,128)(2,1)S(1)}, u32[]{:S(2)}, u32[]{:S(2)}) collective-permute-start(bf16[256,768]{1,0:T(8,128)(2,1)S(1)} %get-tuple-element.45.here), channel_id=1, source_target_pairs={{64,128},{65,129},{66,130},{67,131},{68,132},{69,133},{70,134},{71... | collective-permute-start | bytes 1179656 | tf_op jit(solution)/shard_map/ppermute | solution.py:26
  103.1 15.2 %all-to-all-start.1 = ((f32[16,18,128]{2,1,0:T(8,128)}), f32[16,18,128]{2,1,0:T(8,128)S(1)}, u32[]{:S(2)}, u32[]{:S(2)}) async-start(f32[16,18,128]{2,1,0:T(8,128)} %spread.1), calls=%async_computation.1 | async-start | bytes 393216 | tf_op jit(solution)/shard_map/all_to_all | solution.py:355
  118.4 3.7 %copy-done.1 = bf16[4,1536,768]{2,1,0:T(8,128)(2,1)S(1)} copy-done((bf16[4,1536,768]{2,1,0:T(8,128)(2,1)S(1)}, bf16[4,1536,768]{2,1,0:T(8,128)(2,1)}, u32[]{:S(2)}) %copy-start.1) | copy-done | bytes 9437208
  122.1 3.9 %last.1 = bf16[256,1536]{1,0:T(8,128)(2,1)} custom-call(bf16[256,1536]{1,0:T(8,128)(2,1)S(1)} %bitcast.16, bf16[256,1536]{1,0:T(8,128)(2,1)S(1)} %bitcast.18, bf16[256,768]{1,0:T(8,128)(2,1)S(1)} %collective-permute-done.8.near, bf16[256,768]{1,0:T(8,128)(2,1)S(1)} %get-tuple-element.45.here, bf16[256,768]{1,0:T(8,128)(2,1)S(1)} %collective-permute-done.9.far, ...), custom_call_target="tpu_custom_call" | custom-call | flops 1811939328 | bytes 12195840 | tf_op jit(solution)/shard_map/last/pallas_call | solution.py:237
  125.9 8.5 %all-to-all-done.1 = f32[16,18,128]{2,1,0:T(8,128)S(1)} async-done(((f32[16,18,128]{2,1,0:T(8,128)}), f32[16,18,128]{2,1,0:T(8,128)S(1)}, u32[]{:S(2)}, u32[]{:S(2)}) %all-to-all-start.1) | async-done | bytes 147488 | tf_op jit(solution)/shard_map/all_to_all | solution.py:355
  (58 shorter events, 13.0 us)
Async XLA Ops:
  0.6 22.9 %collective-permute-start = (bf16[256,1536]{1,0:T(8,128)(2,1)}, bf16[256,1536]{1,0:T(8,128)(2,1)S(1)}, u32[]{:S(2)}, u32[]{:S(2)}) collective-permute-start(bf16[256,1536]{1,0:T(8,128)(2,1)} %bitcast.14), channel_id=1, source_target_pairs={{0,64},{1,65},{2,66},{3,67},{4,68},{5,69},{6,70},{7,71},{8,72},{9,... | collective-permute-start | bytes 2359304 | tf_op jit(solution)/shard_map/ppermute | solution.py:26
  5.7 1.4 %copy-start.17 = (bf16[192,1536]{1,0:T(8,128)(2,1)S(1)}, bf16[192,1536]{1,0:T(8,128)(2,1)}, u32[]{:S(2)}) copy-start(bf16[192,1536]{1,0:T(8,128)(2,1)} %param.8) | copy-start | bytes 1769476
  7.2 28.5 %copy-start.3 = (bf16[2,128,1536]{2,1,0:T(8,128)(2,1)S(1)}, bf16[2,128,1536]{2,1,0:T(8,128)(2,1)}, u32[]{:S(2)}) copy-start(bf16[2,128,1536]{2,1,0:T(8,128)(2,1)} %param.6) | copy-start | bytes 2359300
  8.4 25.3 %copy-start.2 = (bf16[3,384,768]{2,1,0:T(8,128)(2,1)S(1)}, bf16[3,384,768]{2,1,0:T(8,128)(2,1)}, u32[]{:S(2)}) copy-start(bf16[3,384,768]{2,1,0:T(8,128)(2,1)} %refs_3_.1) | copy-start | bytes 5308420
  8.4 27.3 %copy-start.18 = (f32[1536]{0:T(1024)S(1)}, f32[1536]{0:T(1024)}, u32[]{:S(2)}) copy-start(f32[1536]{0:T(1024)} %param.9) | copy-start | bytes 18436
  23.5 29.3 %collective-permute-start.2 = (bf16[2,384,768]{2,1,0:T(8,128)(2,1)S(1)}, bf16[2,384,768]{2,1,0:T(8,128)(2,1)}, u32[]{:S(2)}, u32[]{:S(2)}) collective-permute-start(bf16[2,384,768]{2,1,0:T(8,128)(2,1)S(1)} %pad_maximum_fusion), channel_id=1, source_target_pairs={{0,66},{1,67},{2,0},{3,1},{4,70},{5,71},{6,4},{7,5},{8,74},{9,75},... | collective-permute-start | bytes 3538952 | tf_op jit(solution)/shard_map/ppermute | solution.py:26
  28.4 29.8 %collective-permute-start.1 = (bf16[2,384,768]{2,1,0:T(8,128)(2,1)S(1)}, bf16[2,384,768]{2,1,0:T(8,128)(2,1)}, u32[]{:S(2)}, u32[]{:S(2)}) collective-permute-start(bf16[2,384,768]{2,1,0:T(8,128)(2,1)S(1)} %slice.21), channel_id=1, source_target_pairs={{0,2},{1,3},{2,64},{3,65},{4,6},{5,7},{6,68},{7,69},{8,10},{9,11},... | collective-permute-start | bytes 3538952 | tf_op jit(solution)/shard_map/ppermute | solution.py:26
  30.4 20.0 %collective-permute-start.3 = (bf16[256,1536]{1,0:T(8,128)(2,1)S(1)}, bf16[256,1536]{1,0:T(8,128)(2,1)S(1)}, u32[]{:S(2)}, u32[]{:S(2)}) collective-permute-start(bf16[256,1536]{1,0:T(8,128)(2,1)S(1)} %collective-permute-done.block), channel_id=1, source_target_pairs={{0,128},{1,129},{2,130},{3,131},{4,132},{5,133},{6,134},{7,135},{8... | collective-permute-start | bytes 2359304 | tf_op jit(solution)/shard_map/ppermute | solution.py:26
  33.8 34.8 %collective-permute-start.4 = (bf16[3,384,768]{2,1,0:T(8,128)(2,1)S(1)}, bf16[3,384,768]{2,1,0:T(8,128)(2,1)}, u32[]{:S(2)}, u32[]{:S(2)}) collective-permute-start(bf16[3,384,768]{2,1,0:T(8,128)(2,1)S(1)} %copy-done.2), channel_id=1, source_target_pairs={{0,1},{1,0},{2,3},{3,2},{4,5},{5,4},{6,7},{7,6},{8,9},{9,8},{10,11... | collective-permute-start | bytes 5308424 | tf_op jit(solution)/shard_map/ppermute | solution.py:26
  39.6 26.0 %copy-start.19 = (f32[768]{0:T(1024)S(1)}, f32[768]{0:T(1024)}, u32[]{:S(2)}) copy-start(f32[768]{0:T(1024)} %param.10) | copy-start | bytes 9220
  43.4 25.2 %copy-start.6 = (bf16[384,768]{1,0:T(8,128)(2,1)S(1)}, bf16[384,768]{1,0:T(8,128)(2,1)}, u32[]{:S(2)}) copy-start(bf16[384,768]{1,0:T(8,128)(2,1)} %get-tuple-element.47.refs_4_) | copy-start | bytes 1769476
  58.2 10.4 %collective-permute-start.6 = (bf16[2,384,768]{2,1,0:T(8,128)(2,1)}, bf16[2,384,768]{2,1,0:T(8,128)(2,1)}, u32[]{:S(2)}, u32[]{:S(2)}) collective-permute-start(bf16[2,384,768]{2,1,0:T(8,128)(2,1)} %collective-permute-done.1.refs_7_), channel_id=1, source_target_pairs={{0,1},{1,0},{2,3},{3,2},{4,5},{5,4},{6,7},{7,6},{8,9},{9,8},{10,11... | collective-permute-start | bytes 3538952 | tf_op jit(solution)/shard_map/ppermute | solution.py:26
  60.1 8.5 %collective-permute-start.7 = (bf16[2,384,768]{2,1,0:T(8,128)(2,1)}, bf16[2,384,768]{2,1,0:T(8,128)(2,1)}, u32[]{:S(2)}, u32[]{:S(2)}) collective-permute-start(bf16[2,384,768]{2,1,0:T(8,128)(2,1)} %collective-permute-done.2.refs_8_), channel_id=1, source_target_pairs={{0,1},{1,0},{2,3},{3,2},{4,5},{5,4},{6,7},{7,6},{8,9},{9,8},{10,11... | collective-permute-start | bytes 3538952 | tf_op jit(solution)/shard_map/ppermute | solution.py:26
  63.5 5.1 %collective-permute-start.5 = (bf16[384,768]{1,0:T(8,128)(2,1)}, bf16[384,768]{1,0:T(8,128)(2,1)}, u32[]{:S(2)}, u32[]{:S(2)}) collective-permute-start(bf16[384,768]{1,0:T(8,128)(2,1)} %slice_bitcast_fusion), channel_id=1, source_target_pairs={{0,1},{1,0},{2,3},{3,2},{4,5},{5,4},{6,7},{7,6},{8,9},{9,8},{10,11... | collective-permute-start | bytes 1769480 | tf_op jit(solution)/shard_map/ppermute | solution.py:26
  66.8 1.8 %copy-start.16 = (bf16[256,1536]{1,0:T(8,128)(2,1)S(1)}, bf16[256,1536]{1,0:T(8,128)(2,1)}, u32[]{:S(2)}) copy-start(bf16[256,1536]{1,0:T(8,128)(2,1)} %copy-done.15) | copy-start | bytes 2359300
  69.8 4.8 %copy-start.8 = (f32[256,1536]{1,0:T(8,128)S(1)}, f32[256,1536]{1,0:T(8,128)}, u32[]{:S(2)}) copy-start(f32[256,1536]{1,0:T(8,128)} %copy-done.7) | copy-start | bytes 4718596
  69.8 4.8 %copy-start.10 = (f32[256,1536]{1,0:T(8,128)S(1)}, f32[256,1536]{1,0:T(8,128)}, u32[]{:S(2)}) copy-start(f32[256,1536]{1,0:T(8,128)} %copy-done.9) | copy-start | bytes 4718596
  69.8 4.8 %copy-start.12 = (bf16[256,1536]{1,0:T(8,128)(2,1)S(1)}, bf16[256,1536]{1,0:T(8,128)(2,1)}, u32[]{:S(2)}) copy-start(bf16[256,1536]{1,0:T(8,128)(2,1)} %copy-done.11) | copy-start | bytes 2359300
  74.5 5.8 %copy-start = (bf16[4,1536,768]{2,1,0:T(8,128)(2,1)}, bf16[4,1536,768]{2,1,0:T(8,128)(2,1)S(1)}, u32[]{:S(2)}) copy-start(bf16[4,1536,768]{2,1,0:T(8,128)(2,1)S(1)} %get-tuple-element.40.whole) | copy-start | bytes 28311556
  80.4 38.0 %copy-start.5 = (bf16[2,128,1536]{2,1,0:T(8,128)(2,1)S(1)}, bf16[2,128,1536]{2,1,0:T(8,128)(2,1)}, u32[]{:S(2)}) copy-start(bf16[2,128,1536]{2,1,0:T(8,128)(2,1)} %param.11) | copy-start | bytes 2359300
  94.9 23.5 %collective-permute-start.8 = (bf16[256,768]{1,0:T(8,128)(2,1)S(1)}, bf16[256,768]{1,0:T(8,128)(2,1)S(1)}, u32[]{:S(2)}, u32[]{:S(2)}) collective-permute-start(bf16[256,768]{1,0:T(8,128)(2,1)S(1)} %get-tuple-element.45.here), channel_id=1, source_target_pairs={{0,64},{1,65},{2,66},{3,67},{4,68},{5,69},{6,70},{7,71},{8,72},{9,... | collective-permute-start | bytes 1179656 | tf_op jit(solution)/shard_map/ppermute | solution.py:26
  98.5 19.9 %collective-permute-start.9 = (bf16[256,768]{1,0:T(8,128)(2,1)S(1)}, bf16[256,768]{1,0:T(8,128)(2,1)S(1)}, u32[]{:S(2)}, u32[]{:S(2)}) collective-permute-start(bf16[256,768]{1,0:T(8,128)(2,1)S(1)} %get-tuple-element.45.here), channel_id=1, source_target_pairs={{64,128},{65,129},{66,130},{67,131},{68,132},{69,133},{70,134},{71... | collective-permute-start | bytes 1179656 | tf_op jit(solution)/shard_map/ppermute | solution.py:26
  103.1 31.4 %all-to-all-start.1 = ((f32[16,18,128]{2,1,0:T(8,128)}), f32[16,18,128]{2,1,0:T(8,128)S(1)}, u32[]{:S(2)}, u32[]{:S(2)}) async-start(f32[16,18,128]{2,1,0:T(8,128)} %spread.1), calls=%async_computation.1 | async-start | bytes 393216 | tf_op jit(solution)/shard_map/all_to_all | solution.py:355
  118.4 3.7 %copy-start.1 = (bf16[4,1536,768]{2,1,0:T(8,128)(2,1)S(1)}, bf16[4,1536,768]{2,1,0:T(8,128)(2,1)}, u32[]{:S(2)}) copy-start(bf16[4,1536,768]{2,1,0:T(8,128)(2,1)} %copy-done) | copy-start | bytes 28311556
  (8 other events, 8.5 us)

commit v6 on v5

--- a/solution.py
+++ b/solution.py
@@ -95,10 +95,10 @@
     over_rows(block.shape[0], step)
 
 
-def gather(where, pieces, whole, semaphores, slabs):
+def gather(where, pieces, whole, semaphores, slabs, shards):
     copies = {}
     for k in slabs:
-        for r in range(4):
+        for r in shards:
             ref, slab = pieces[r][k]
             part = ref.shape[-2]
             place = pl.ds(pl.multiple_of(where[r], 128), part)
@@ -110,19 +110,21 @@
             copies[k, r].start()
 
     def ready(k):
-        for r in range(4):
+        for r in shards:
             copies[k, r].wait()
 
     return ready
 
 
-def pieces_of(weight, folded, weight_s, folded_s, up, down, up_s, down_s):
-    return [
+def place_kernel(where, weight, folded, weight_s, folded_s, up, down, whole, semaphores):
+    pieces = [
         [(weight, 0), (weight, 1), (weight, 2), (folded, None)],
         [(weight_s, 0), (weight_s, 1), (weight_s, 2), (folded_s, None)],
         [(up, 0), (up, 1), (down, 0), (down, 1)],
-        [(up_s, 0), (up_s, 1), (down_s, 0), (down_s, 1)],
     ]
+    ready = gather(where, pieces, whole, semaphores, range(4), range(3))
+    for k in range(4):
+        ready(k)
 
 
 def fetch(sources, places, semaphores):
@@ -135,12 +137,14 @@
     return lambda i: copies[i].wait()
 
 
-def early_kernel(*refs):
-    where = refs[0]
-    whole, mixed, grad2, semaphores, held_rows, row_semaphores = refs[11:]
+def early_kernel(
+    where, hidden_away, cotangent_away, placed, up_s, down_s, whole, mixed, grad2, semaphores,
+    held_rows, row_semaphores,
+):
     hidden, cotangent = held_rows.at[0], held_rows.at[1]
-    fetched = fetch((refs[1], refs[2]), (hidden, cotangent), row_semaphores)
-    ready = gather(where, pieces_of(*refs[3:11]), whole, semaphores, (3, 1, 0, 2))
+    fetched = fetch((hidden_away, cotangent_away), (hidden, cotangent), row_semaphores)
+    fourth = [(up_s, 0), (up_s, 1), (down_s, 0), (down_s, 1)]
+    ready = gather(where, {3: fourth}, whole, semaphores, (3, 1, 0, 2), (3,))
     width = mixed.shape[1]
     half = whole.shape[1] // 8
 
@@ -232,7 +236,7 @@
 ANY_SPEC = pl.BlockSpec(memory_space=pl.ANY)
 
 
-def call(kernel, name, out_shape, scratch, flops, *operands, specs=None):
+def call(kernel, name, out_shape, scratch, flops, *operands, specs=None, aliases=None):
     moved = sum(v.size * v.dtype.itemsize for v in operands)
     return pl.pallas_call(
         kernel,
@@ -241,6 +245,7 @@
         in_specs=specs or [VMEM_SPEC] * len(operands),
         out_specs=jax.tree.map(lambda _: VMEM_SPEC, out_shape),
         scratch_shapes=scratch,
+        input_output_aliases=aliases or {},
         cost_estimate=pl.CostEstimate(flops=flops, bytes_accessed=moved, transcendentals=0),
         compiler_params=pltpu.CompilerParams(vmem_limit_bytes=VMEM_LIMIT),
     )(*operands)
@@ -290,18 +295,29 @@
     up, down = permute(sent_up, along_y(1)), permute(sent_down, along_y(-1))
     weight_s, folded_s = permute(sent, sister), permute(sent_down[1], sister)
     h0, e0 = prepare(near)
-    up, down, far, h0, h1 = lax.optimization_barrier((up, down, far, h0, h1))
+    h2, e2 = prepare(far)
+    up, down, h0, h1, h2, folded_s = lax.optimization_barrier((up, down, h0, h1, h2, folded_s))
     up_s, down_s = permute(up, sister), permute(down, sister)
     pieces = (weight, folded, weight_s, folded_s, up, down, up_s, down_s)
 
-    h2, e2 = prepare(far)
 
     work = 2 * rows * channels * width
+    kernels_whole = jax.ShapeDtypeStruct((4, channels, width), bf16)
+    placed = call(
+        place_kernel,
+        "place",
+        kernels_whole,
+        [pltpu.SemaphoreType.DMA((4, 4))],
+        work,
+        where,
+        *pieces[:6],
+        specs=[SMEM_SPEC] + [ANY_SPEC] * 6,
+    )
     whole, centre, grad2 = call(
         early_kernel,
         "early",
         [
-            jax.ShapeDtypeStruct((4, channels, width), bf16),
+            kernels_whole,
             jax.ShapeDtypeStruct((rows, width), f32),
             jax.ShapeDtypeStruct((rows, width), f32),
         ],
@@ -314,8 +330,10 @@
         where,
         h1,
         cotangent,
-        *pieces,
-        specs=[SMEM_SPEC] + [ANY_SPEC] * 10,
+        placed,
+        *pieces[6:],
+        specs=[SMEM_SPEC] + [ANY_SPEC] * 2 + [VMEM_SPEC] + [ANY_SPEC] * 2,
+        aliases={3: 0},
     )
     grad_mixed, sums = call(
         middle_kernel,

time: 136 us -> 133 us (0.978)
  waiting for transfers between devices: 37.4 us -> 28.3 us
  Pallas kernels: 20.4 us -> 23 us
  blocking collectives: 13.8 us -> 16 us
    ppermute x10, waiting for transfers between devices: 28.9 us -> 19.8 us  [permute(): return lax.ppermute(value, AXES, pairs)]
    pallas_call x7 -> x8, Pallas kernels: 20.4 us -> 23 us  [call(): pl.pallas_call(kernel, name=name, out_shape=out_shape, in_specs=specs or...]
    all_to_all x1, blocking collectives: 13.8 us -> 16 us  [body(): sums = lax.all_to_all(sums, ('x', 'yh', 'yl', 'c'), 0, 0)]
    unnamed x40 -> x48, local copies, waits for them, and re-layouts: 11 us -> 11.8 us
  transfers between devices with their start and end apart: 11 -> 11, of which waited for: 5 -> 4; matrix products, arithmetic and copies ran while one was open for 3% -> 2% of each run, Pallas kernels for 7% -> 9%
where the time goes in v6:
time: 133 us; the launch traced here: 132 us
  starting transfers between devices  47.9 us (36%)
  waiting for transfers between devices  28.3 us (21%)
  Pallas kernels  23 us (17%)
  blocking collectives  16 us (12%)
  local copies, waits for them, and re-layouts  13.6 us (10%)
  other arithmetic  2.28 us (2%)
    ppermute x10, starting transfers between devices, permute(): return lax.ppermute(value, AXES, pairs)  32.7 us
    pallas_call x8, Pallas kernels, call(): pl.pallas_call(kernel, name=name, out_shape=out_shape, in_specs=specs or...  23 us
    ppermute x10, waiting for transfers between devices, permute(): return lax.ppermute(value, AXES, pairs)  19.8 us
    all_to_all x1, blocking collectives, body(): sums = lax.all_to_all(sums, ('x', 'yh', 'yl', 'c'), 0, 0)  16 us
    all_to_all x1, starting transfers between devices, body(): sums = lax.all_to_all(sums, 'z', 0, 0)  15.2 us
    unnamed x48, local copies, waits for them, and re-layouts  11.8 us
    all_to_all x1, waiting for transfers between devices, body(): sums = lax.all_to_all(sums, 'z', 0, 0)  8.55 us
  transfers between devices with their start and end apart: 11, of which 4 were waited for; matrix products, arithmetic and copies ran while one was open for 2% of the time, Pallas kernels for 9%

profile of v6, /device:TPU:2, one launch (start us, length us, event | category | flops | bytes accessed | tf_op | source)
XLA Modules:
  0.0 132.3 jit_solution(16277029268411317309)
XLA Ops:
  0.6 5.2 %collective-permute-start = (bf16[256,1536]{1,0:T(8,128)(2,1)}, bf16[256,1536]{1,0:T(8,128)(2,1)S(1)}, u32[]{:S(2)}, u32[]{:S(2)}) collective-permute-start(bf16[256,1536]{1,0:T(8,128)(2,1)} %bitcast.14), channel_id=1, source_target_pairs={{0,64},{1,65},{2,66},{3,67},{4,68},{5,69},{6,70},{7,71},{8,72},{9,... | collective-permute-start | bytes 2359304 | tf_op jit(solution)/shard_map/ppermute | solution.py:26
  5.9 1.3 %slice.21 = bf16[2,384,768]{2,1,0:T(8,128)(2,1)S(1)} slice(bf16[3,384,768]{2,1,0:T(8,128)(2,1)} %weight.1), slice={[0:2], [0:384], [0:768]} | slice | bytes 2359296 | tf_op jit(solution)/shard_map/slice | solution.py:292
  8.7 15.0 %collective-permute-done.block = bf16[256,1536]{1,0:T(8,128)(2,1)S(1)} collective-permute-done((bf16[256,1536]{1,0:T(8,128)(2,1)}, bf16[256,1536]{1,0:T(8,128)(2,1)S(1)}, u32[]{:S(2)}, u32[]{:S(2)}) %collective-permute-start) | collective-permute-done | bytes 786464 | tf_op jit(solution)/shard_map/ppermute | solution.py:26
  23.7 3.5 %collective-permute-start.1 = (bf16[2,384,768]{2,1,0:T(8,128)(2,1)S(1)}, bf16[2,384,768]{2,1,0:T(8,128)(2,1)}, u32[]{:S(2)}, u32[]{:S(2)}) collective-permute-start(bf16[2,384,768]{2,1,0:T(8,128)(2,1)S(1)} %slice.21), channel_id=1, source_target_pairs={{0,2},{1,3},{2,64},{3,65},{4,6},{5,7},{6,68},{7,69},{8,10},{9,11},... | collective-permute-start | bytes 3538952 | tf_op jit(solution)/shard_map/ppermute | solution.py:26
  27.1 3.6 %collective-permute-start.2 = (bf16[2,384,768]{2,1,0:T(8,128)(2,1)S(1)}, bf16[2,384,768]{2,1,0:T(8,128)(2,1)}, u32[]{:S(2)}, u32[]{:S(2)}) collective-permute-start(bf16[2,384,768]{2,1,0:T(8,128)(2,1)S(1)} %pad_maximum_fusion), channel_id=1, source_target_pairs={{0,66},{1,67},{2,0},{3,1},{4,70},{5,71},{6,4},{7,5},{8,74},{9,75},... | collective-permute-start | bytes 3538952 | tf_op jit(solution)/shard_map/ppermute | solution.py:26
  30.7 3.4 %collective-permute-start.3 = (bf16[256,1536]{1,0:T(8,128)(2,1)S(1)}, bf16[256,1536]{1,0:T(8,128)(2,1)S(1)}, u32[]{:S(2)}, u32[]{:S(2)}) collective-permute-start(bf16[256,1536]{1,0:T(8,128)(2,1)S(1)} %collective-permute-done.block), channel_id=1, source_target_pairs={{0,128},{1,129},{2,130},{3,131},{4,132},{5,133},{6,134},{7,135},{8... | collective-permute-start | bytes 2359304 | tf_op jit(solution)/shard_map/ppermute | solution.py:26
  34.1 1.9 %collective-permute-start.5 = (bf16[3,384,768]{2,1,0:T(8,128)(2,1)S(1)}, bf16[3,384,768]{2,1,0:T(8,128)(2,1)}, u32[]{:S(2)}, u32[]{:S(2)}) collective-permute-start(bf16[3,384,768]{2,1,0:T(8,128)(2,1)S(1)} %copy-done.2), channel_id=1, source_target_pairs={{0,1},{1,0},{2,3},{3,2},{4,5},{5,4},{6,7},{7,6},{8,9},{9,8},{10,11... | collective-permute-start | bytes 5308424 | tf_op jit(solution)/shard_map/ppermute | solution.py:26
  36.1 2.4 %collective-permute-start.4 = (bf16[384,768]{1,0:T(8,128)(2,1)S(1)}, bf16[384,768]{1,0:T(8,128)(2,1)S(1)}, u32[]{:S(2)}, u32[]{:S(2)}) collective-permute-start(bf16[384,768]{1,0:T(8,128)(2,1)S(1)} %slice_bitcast_fusion), channel_id=1, source_target_pairs={{0,1},{1,0},{2,3},{3,2},{4,5},{5,4},{6,7},{7,6},{8,9},{9,8},{10,11... | collective-permute-start | bytes 1769480 | tf_op jit(solution)/shard_map/ppermute | solution.py:26
  38.6 1.8 %prepare.4 = (bf16[256,1536]{1,0:T(8,128)(2,1)S(1)}, f32[256,1536]{1,0:T(8,128)S(1)}) custom-call(bf16[256,1536]{1,0:T(8,128)(2,1)S(1)} %bitcast.15, f32[1,1536]{1,0:T(1,128)S(1)} %broadcast_in_dim.6.gain), custom_call_target="tpu_custom_call" | custom-call | flops 15728640 | bytes 792576 | tf_op jit(solution)/shard_map/prepare/pallas_call | solution.py:241
  42.4 1.8 %prepare.3 = (bf16[256,1536]{1,0:T(8,128)(2,1)S(1)}, f32[256,1536]{1,0:T(8,128)S(1)}) custom-call(bf16[256,1536]{1,0:T(8,128)(2,1)S(1)} %collective-permute-done.block, f32[1,1536]{1,0:T(1,128)S(1)} %broadcast_in_dim.6.gain), custom_call_target="tpu_custom_call" | custom-call | flops 15728640 | bytes 792576 | tf_op jit(solution)/shard_map/prepare/pallas_call | solution.py:241
  46.2 4.3 %collective-permute-done.3.block = bf16[256,1536]{1,0:T(8,128)(2,1)S(1)} collective-permute-done((bf16[256,1536]{1,0:T(8,128)(2,1)S(1)}, bf16[256,1536]{1,0:T(8,128)(2,1)S(1)}, u32[]{:S(2)}, u32[]{:S(2)}) %collective-permute-start.3) | collective-permute-done | bytes 786464 | tf_op jit(solution)/shard_map/ppermute | solution.py:26
  50.5 1.8 %prepare.5 = (bf16[256,1536]{1,0:T(8,128)(2,1)S(1)}, f32[256,1536]{1,0:T(8,128)S(1)}) custom-call(bf16[256,1536]{1,0:T(8,128)(2,1)S(1)} %collective-permute-done.3.block, f32[1,1536]{1,0:T(1,128)S(1)} %broadcast_in_dim.6.gain), custom_call_target="tpu_custom_call" | custom-call | flops 15728640 | bytes 792576 | tf_op jit(solution)/shard_map/prepare/pallas_call | solution.py:241
  55.7 1.9 %collective-permute-start.6 = (bf16[2,384,768]{2,1,0:T(8,128)(2,1)}, bf16[2,384,768]{2,1,0:T(8,128)(2,1)}, u32[]{:S(2)}, u32[]{:S(2)}) collective-permute-start(bf16[2,384,768]{2,1,0:T(8,128)(2,1)} %collective-permute-done.1.up), channel_id=1, source_target_pairs={{0,1},{1,0},{2,3},{3,2},{4,5},{5,4},{6,7},{7,6},{8,9},{9,8},{10,11... | collective-permute-start | bytes 3538952 | tf_op jit(solution)/shard_map/ppermute | solution.py:26
  57.6 2.6 %collective-permute-start.7 = (bf16[2,384,768]{2,1,0:T(8,128)(2,1)}, bf16[2,384,768]{2,1,0:T(8,128)(2,1)}, u32[]{:S(2)}, u32[]{:S(2)}) collective-permute-start(bf16[2,384,768]{2,1,0:T(8,128)(2,1)} %collective-permute-done.2.down), channel_id=1, source_target_pairs={{0,1},{1,0},{2,3},{3,2},{4,5},{5,4},{6,7},{7,6},{8,9},{9,8},{10,11... | collective-permute-start | bytes 3538952 | tf_op jit(solution)/shard_map/ppermute | solution.py:26
  61.4 3.1 %place.1.placed = bf16[4,1536,768]{2,1,0:T(8,128)(2,1)S(1)} custom-call(s32[5]{0:T(128)S(1)} %stack.31.where, bf16[3,384,768]{2,1,0:T(8,128)(2,1)S(1)} %copy-done.2, bf16[384,768]{1,0:T(8,128)(2,1)S(1)} %copy-done.6, bf16[3,384,768]{2,1,0:T(8,128)(2,1)} %collective-permute-done.5.weight_s, bf16[384,768]{1,0:T(8,128)(2,1)S(1)} %copy-done.20, ...), custom_call_target="tpu_custom_call" | custom-call | flops 603979776 | bytes 7077908 | tf_op jit(solution)/shard_map/place/pallas_call | solution.py:241
  64.6 4.2 %early.1 = (bf16[4,1536,768]{2,1,0:T(8,128)(2,1)S(1)}, f32[256,768]{1,0:T(8,128)S(1)}, f32[256,768]{1,0:T(8,128)S(1)}) custom-call(s32[5]{0:T(128)S(1)} %stack.31.where, bf16[256,1536]{1,0:T(8,128)(2,1)S(1)} %copy-done.18, bf16[256,1536]{1,0:T(8,128)(2,1)S(1)} %bitcast.17, bf16[4,1536,768]{2,1,0:T(8,128)(2,1)S(1)} %place.1.placed, ...), custom_call_target="tpu_custom_call", output_to_operand_aliasing={{0}: (3, {})} | custom-call | flops 1207959552 | bytes 13369364 | tf_op jit(solution)/shard_map/early/pallas_call | solution.py:241
  68.9 5.8 %middle.1 = (bf16[256,768]{1,0:T(8,128)(2,1)S(1)}, f32[32,18,128]{2,1,0:T(8,128)S(1)}) custom-call(bf16[256,1536]{1,0:T(8,128)(2,1)S(1)} %copy-done.14, bf16[256,1536]{1,0:T(8,128)(2,1)S(1)} %copy-done.16, f32[256,1536]{1,0:T(8,128)S(1)} %copy-done.10, f32[256,1536]{1,0:T(8,128)S(1)} %copy-done.8, f32[256,1536]{1,0:T(8,128)S(1)} %copy-done.12, ...), custom_call_target="tpu_custom_call" | custom-call | flops 3019898880 | bytes 17304576 | tf_op jit(solution)/shard_map/middle/pallas_call | solution.py:241
  74.7 16.0 %all_to_all.10.arrived = f32[32,18,128]{2,1,0:T(8,128)S(1)} all-to-all(f32[32,18,128]{2,1,0:T(8,128)S(1)} %get-tuple-element.46), channel_id=1, replica_groups=mesh['x'=4,'yh'=2,'z'=16,'yl'=2,'c'=2] {'x','yh','yl','c'}, dimensions={0} | all-to-all | bytes 589824 | tf_op jit(solution)/shard_map/all_to_all | solution.py:366
  91.4 3.6 %collective-permute-start.8 = (bf16[256,768]{1,0:T(8,128)(2,1)S(1)}, bf16[256,768]{1,0:T(8,128)(2,1)S(1)}, u32[]{:S(2)}, u32[]{:S(2)}) collective-permute-start(bf16[256,768]{1,0:T(8,128)(2,1)S(1)} %get-tuple-element.47.here), channel_id=1, source_target_pairs={{0,64},{1,65},{2,66},{3,67},{4,68},{5,69},{6,70},{7,71},{8,72},{9,... | collective-permute-start | bytes 1179656 | tf_op jit(solution)/shard_map/ppermute | solution.py:26
  95.0 4.6 %collective-permute-start.9 = (bf16[256,768]{1,0:T(8,128)(2,1)S(1)}, bf16[256,768]{1,0:T(8,128)(2,1)S(1)}, u32[]{:S(2)}, u32[]{:S(2)}) collective-permute-start(bf16[256,768]{1,0:T(8,128)(2,1)S(1)} %get-tuple-element.47.here), channel_id=1, source_target_pairs={{64,128},{65,129},{66,130},{67,131},{68,132},{69,133},{70,134},{71... | collective-permute-start | bytes 1179656 | tf_op jit(solution)/shard_map/ppermute | solution.py:26
  99.7 15.2 %all-to-all-start.1 = ((f32[16,18,128]{2,1,0:T(8,128)}), f32[16,18,128]{2,1,0:T(8,128)S(1)}, u32[]{:S(2)}, u32[]{:S(2)}) async-start(f32[16,18,128]{2,1,0:T(8,128)} %spread.1), calls=%async_computation.1 | async-start | bytes 393216 | tf_op jit(solution)/shard_map/all_to_all | solution.py:373
  114.9 3.7 %copy-done.1 = bf16[4,1536,768]{2,1,0:T(8,128)(2,1)S(1)} copy-done((bf16[4,1536,768]{2,1,0:T(8,128)(2,1)S(1)}, bf16[4,1536,768]{2,1,0:T(8,128)(2,1)}, u32[]{:S(2)}) %copy-start.1) | copy-done | bytes 9437208
  118.6 3.9 %last.1 = bf16[256,1536]{1,0:T(8,128)(2,1)} custom-call(bf16[256,1536]{1,0:T(8,128)(2,1)S(1)} %bitcast.16, bf16[256,1536]{1,0:T(8,128)(2,1)S(1)} %bitcast.18, bf16[256,768]{1,0:T(8,128)(2,1)S(1)} %collective-permute-done.8.near, bf16[256,768]{1,0:T(8,128)(2,1)S(1)} %get-tuple-element.47.here, bf16[256,768]{1,0:T(8,128)(2,1)S(1)} %collective-permute-done.9.far, ...), custom_call_target="tpu_custom_call" | custom-call | flops 1811939328 | bytes 12195840 | tf_op jit(solution)/shard_map/last/pallas_call | solution.py:241
  122.5 8.5 %all-to-all-done.1 = f32[16,18,128]{2,1,0:T(8,128)S(1)} async-done(((f32[16,18,128]{2,1,0:T(8,128)}), f32[16,18,128]{2,1,0:T(8,128)S(1)}, u32[]{:S(2)}, u32[]{:S(2)}) %all-to-all-start.1) | async-done | bytes 147488 | tf_op jit(solution)/shard_map/all_to_all | solution.py:373
  (67 shorter events, 12.1 us)
Async XLA Ops:
  0.6 6.6 %copy-start.21 = (bf16[192,1536]{1,0:T(8,128)(2,1)S(1)}, bf16[192,1536]{1,0:T(8,128)(2,1)}, u32[]{:S(2)}) copy-start(bf16[192,1536]{1,0:T(8,128)(2,1)} %param.8) | copy-start | bytes 1769476
  0.6 23.0 %collective-permute-start = (bf16[256,1536]{1,0:T(8,128)(2,1)}, bf16[256,1536]{1,0:T(8,128)(2,1)S(1)}, u32[]{:S(2)}, u32[]{:S(2)}) collective-permute-start(bf16[256,1536]{1,0:T(8,128)(2,1)} %bitcast.14), channel_id=1, source_target_pairs={{0,64},{1,65},{2,66},{3,67},{4,68},{5,69},{6,70},{7,71},{8,72},{9,... | collective-permute-start | bytes 2359304 | tf_op jit(solution)/shard_map/ppermute | solution.py:26
  8.6 25.6 %copy-start.2 = (bf16[3,384,768]{2,1,0:T(8,128)(2,1)S(1)}, bf16[3,384,768]{2,1,0:T(8,128)(2,1)}, u32[]{:S(2)}) copy-start(bf16[3,384,768]{2,1,0:T(8,128)(2,1)} %weight.1) | copy-start | bytes 5308420
  8.7 29.9 %copy-start.22 = (f32[1536]{0:T(1024)S(1)}, f32[1536]{0:T(1024)}, u32[]{:S(2)}) copy-start(f32[1536]{0:T(1024)} %param.9) | copy-start | bytes 18436
  8.7 29.9 %copy-start.3 = (bf16[2,128,1536]{2,1,0:T(8,128)(2,1)S(1)}, bf16[2,128,1536]{2,1,0:T(8,128)(2,1)}, u32[]{:S(2)}) copy-start(bf16[2,128,1536]{2,1,0:T(8,128)(2,1)} %param.6) | copy-start | bytes 2359300
  23.7 31.5 %collective-permute-start.1 = (bf16[2,384,768]{2,1,0:T(8,128)(2,1)S(1)}, bf16[2,384,768]{2,1,0:T(8,128)(2,1)}, u32[]{:S(2)}, u32[]{:S(2)}) collective-permute-start(bf16[2,384,768]{2,1,0:T(8,128)(2,1)S(1)} %slice.21), channel_id=1, source_target_pairs={{0,2},{1,3},{2,64},{3,65},{4,6},{5,7},{6,68},{7,69},{8,10},{9,11},... | collective-permute-start | bytes 3538952 | tf_op jit(solution)/shard_map/ppermute | solution.py:26
  27.1 28.6 %collective-permute-start.2 = (bf16[2,384,768]{2,1,0:T(8,128)(2,1)S(1)}, bf16[2,384,768]{2,1,0:T(8,128)(2,1)}, u32[]{:S(2)}, u32[]{:S(2)}) collective-permute-start(bf16[2,384,768]{2,1,0:T(8,128)(2,1)S(1)} %pad_maximum_fusion), channel_id=1, source_target_pairs={{0,66},{1,67},{2,0},{3,1},{4,70},{5,71},{6,4},{7,5},{8,74},{9,75},... | collective-permute-start | bytes 3538952 | tf_op jit(solution)/shard_map/ppermute | solution.py:26
  30.7 19.8 %collective-permute-start.3 = (bf16[256,1536]{1,0:T(8,128)(2,1)S(1)}, bf16[256,1536]{1,0:T(8,128)(2,1)S(1)}, u32[]{:S(2)}, u32[]{:S(2)}) collective-permute-start(bf16[256,1536]{1,0:T(8,128)(2,1)S(1)} %collective-permute-done.block), channel_id=1, source_target_pairs={{0,128},{1,129},{2,130},{3,131},{4,132},{5,133},{6,134},{7,135},{8... | collective-permute-start | bytes 2359304 | tf_op jit(solution)/shard_map/ppermute | solution.py:26
  34.1 26.2 %collective-permute-start.5 = (bf16[3,384,768]{2,1,0:T(8,128)(2,1)S(1)}, bf16[3,384,768]{2,1,0:T(8,128)(2,1)}, u32[]{:S(2)}, u32[]{:S(2)}) collective-permute-start(bf16[3,384,768]{2,1,0:T(8,128)(2,1)S(1)} %copy-done.2), channel_id=1, source_target_pairs={{0,1},{1,0},{2,3},{3,2},{4,5},{5,4},{6,7},{7,6},{8,9},{9,8},{10,11... | collective-permute-start | bytes 5308424 | tf_op jit(solution)/shard_map/ppermute | solution.py:26
  36.1 18.2 %collective-permute-start.4 = (bf16[384,768]{1,0:T(8,128)(2,1)S(1)}, bf16[384,768]{1,0:T(8,128)(2,1)S(1)}, u32[]{:S(2)}, u32[]{:S(2)}) collective-permute-start(bf16[384,768]{1,0:T(8,128)(2,1)S(1)} %slice_bitcast_fusion), channel_id=1, source_target_pairs={{0,1},{1,0},{2,3},{3,2},{4,5},{5,4},{6,7},{7,6},{8,9},{9,8},{10,11... | collective-permute-start | bytes 1769480 | tf_op jit(solution)/shard_map/ppermute | solution.py:26
  38.6 21.7 %copy-start.23 = (f32[768]{0:T(1024)S(1)}, f32[768]{0:T(1024)}, u32[]{:S(2)}) copy-start(f32[768]{0:T(1024)} %param.10) | copy-start | bytes 9220
  38.6 21.8 %copy-start.6 = (bf16[384,768]{1,0:T(8,128)(2,1)S(1)}, bf16[384,768]{1,0:T(8,128)(2,1)}, u32[]{:S(2)}) copy-start(bf16[384,768]{1,0:T(8,128)(2,1)} %get-tuple-element.49.folded) | copy-start | bytes 1769476
  55.7 8.8 %collective-permute-start.6 = (bf16[2,384,768]{2,1,0:T(8,128)(2,1)}, bf16[2,384,768]{2,1,0:T(8,128)(2,1)}, u32[]{:S(2)}, u32[]{:S(2)}) collective-permute-start(bf16[2,384,768]{2,1,0:T(8,128)(2,1)} %collective-permute-done.1.up), channel_id=1, source_target_pairs={{0,1},{1,0},{2,3},{3,2},{4,5},{5,4},{6,7},{7,6},{8,9},{9,8},{10,11... | collective-permute-start | bytes 3538952 | tf_op jit(solution)/shard_map/ppermute | solution.py:26
  57.6 6.9 %collective-permute-start.7 = (bf16[2,384,768]{2,1,0:T(8,128)(2,1)}, bf16[2,384,768]{2,1,0:T(8,128)(2,1)}, u32[]{:S(2)}, u32[]{:S(2)}) collective-permute-start(bf16[2,384,768]{2,1,0:T(8,128)(2,1)} %collective-permute-done.2.down), channel_id=1, source_target_pairs={{0,1},{1,0},{2,3},{3,2},{4,5},{5,4},{6,7},{7,6},{8,9},{9,8},{10,11... | collective-permute-start | bytes 3538952 | tf_op jit(solution)/shard_map/ppermute | solution.py:26
  64.5 4.3 %copy-start.8 = (f32[256,1536]{1,0:T(8,128)S(1)}, f32[256,1536]{1,0:T(8,128)}, u32[]{:S(2)}) copy-start(f32[256,1536]{1,0:T(8,128)} %copy-done.7) | copy-start | bytes 4718596
  64.5 4.3 %copy-start.10 = (f32[256,1536]{1,0:T(8,128)S(1)}, f32[256,1536]{1,0:T(8,128)}, u32[]{:S(2)}) copy-start(f32[256,1536]{1,0:T(8,128)} %copy-done.9) | copy-start | bytes 4718596
  64.5 4.3 %copy-start.12 = (f32[256,1536]{1,0:T(8,128)S(1)}, f32[256,1536]{1,0:T(8,128)}, u32[]{:S(2)}) copy-start(f32[256,1536]{1,0:T(8,128)} %copy-done.11) | copy-start | bytes 4718596
  64.6 4.3 %copy-start.14 = (bf16[256,1536]{1,0:T(8,128)(2,1)S(1)}, bf16[256,1536]{1,0:T(8,128)(2,1)}, u32[]{:S(2)}) copy-start(bf16[256,1536]{1,0:T(8,128)(2,1)} %copy-done.13) | copy-start | bytes 2359300
  64.6 4.3 %copy-start.16 = (bf16[256,1536]{1,0:T(8,128)(2,1)S(1)}, bf16[256,1536]{1,0:T(8,128)(2,1)}, u32[]{:S(2)}) copy-start(bf16[256,1536]{1,0:T(8,128)(2,1)} %copy-done.15) | copy-start | bytes 2359300
  68.8 5.9 %copy-start = (bf16[4,1536,768]{2,1,0:T(8,128)(2,1)}, bf16[4,1536,768]{2,1,0:T(8,128)(2,1)S(1)}, u32[]{:S(2)}) copy-start(bf16[4,1536,768]{2,1,0:T(8,128)(2,1)S(1)} %get-tuple-element.42.whole) | copy-start | bytes 28311556
  74.7 40.2 %copy-start.5 = (bf16[2,128,1536]{2,1,0:T(8,128)(2,1)S(1)}, bf16[2,128,1536]{2,1,0:T(8,128)(2,1)}, u32[]{:S(2)}) copy-start(bf16[2,128,1536]{2,1,0:T(8,128)(2,1)} %param.11) | copy-start | bytes 2359300
  91.4 23.5 %collective-permute-start.8 = (bf16[256,768]{1,0:T(8,128)(2,1)S(1)}, bf16[256,768]{1,0:T(8,128)(2,1)S(1)}, u32[]{:S(2)}, u32[]{:S(2)}) collective-permute-start(bf16[256,768]{1,0:T(8,128)(2,1)S(1)} %get-tuple-element.47.here), channel_id=1, source_target_pairs={{0,64},{1,65},{2,66},{3,67},{4,68},{5,69},{6,70},{7,71},{8,72},{9,... | collective-permute-start | bytes 1179656 | tf_op jit(solution)/shard_map/ppermute | solution.py:26
  95.0 19.9 %collective-permute-start.9 = (bf16[256,768]{1,0:T(8,128)(2,1)S(1)}, bf16[256,768]{1,0:T(8,128)(2,1)S(1)}, u32[]{:S(2)}, u32[]{:S(2)}) collective-permute-start(bf16[256,768]{1,0:T(8,128)(2,1)S(1)} %get-tuple-element.47.here), channel_id=1, source_target_pairs={{64,128},{65,129},{66,130},{67,131},{68,132},{69,133},{70,134},{71... | collective-permute-start | bytes 1179656 | tf_op jit(solution)/shard_map/ppermute | solution.py:26
  99.7 31.4 %all-to-all-start.1 = ((f32[16,18,128]{2,1,0:T(8,128)}), f32[16,18,128]{2,1,0:T(8,128)S(1)}, u32[]{:S(2)}, u32[]{:S(2)}) async-start(f32[16,18,128]{2,1,0:T(8,128)} %spread.1), calls=%async_computation.1 | async-start | bytes 393216 | tf_op jit(solution)/shard_map/all_to_all | solution.py:373
  (12 other events, 19.2 us)

commit v7 on v6

--- a/solution.py
+++ b/solution.py
@@ -340,7 +340,7 @@
         "middle",
         [
             jax.ShapeDtypeStruct((rows, width), bf16),
-            jax.ShapeDtypeStruct((32, (channels + width) // 128, 128), f32),
+            jax.ShapeDtypeStruct((16, (channels + width) // 128, 128), f32),
         ],
         [
             pltpu.VMEM((rows, width), f32),
@@ -363,14 +363,13 @@
         gain2,
         specs=[ANY_SPEC, VMEM_SPEC] + [ANY_SPEC] * 3 + [VMEM_SPEC] * 4,
     )
-    sums = lax.all_to_all(sums, ("x", "yh", "yl", "c"), 0, 0)
-    sums = call(
-        spread_kernel, "spread", jax.ShapeDtypeStruct((16,) + sums.shape[1:], f32), [], 1, sums
-    )
-    grad_mixed, sums = lax.optimization_barrier((grad_mixed, sums))
     near_grad = permute(grad_mixed, antipode)
     far_grad = permute(grad_mixed, second_neighbour)
     sums = lax.all_to_all(sums, "z", 0, 0)
+    sums = call(
+        spread_kernel, "spread", jax.ShapeDtypeStruct((32,) + sums.shape[1:], f32), [], 1, sums
+    )
+    sums = lax.all_to_all(sums, ("x", "yh", "yl", "c"), 0, 0)
 
     grad_input = call(
         last_kernel,

time: 133 us -> 129 us (0.970)
  the two profiles are of different devices: /device:TPU:2 before, /device:TPU:1 now
where the time goes in v7:
time: 129 us; the launch traced here: 128 us
  starting transfers between devices  63.1 us (49%)
  waiting for transfers between devices  24 us (19%)
  Pallas kernels  23.7 us (18%)
  local copies, waits for them, and re-layouts  13.6 us (11%)
  other arithmetic  2.32 us (2%)
    ppermute x10, starting transfers between devices, permute(): return lax.ppermute(value, AXES, pairs)  36.5 us
    pallas_call x8, Pallas kernels, call(): pl.pallas_call(kernel, name=name, out_shape=out_shape, in_specs=specs or...  23.7 us
    all_to_all x1, starting transfers between devices, body(): sums = lax.all_to_all(sums, 'z', 0, 0)  15.1 us
    ppermute x10, waiting for transfers between devices, permute(): return lax.ppermute(value, AXES, pairs)  14 us
    unnamed x48, local copies, waits for them, and re-layouts  11.7 us
    all_to_all x1, starting transfers between devices, body(): sums = lax.all_to_all(sums, ('x', 'yh', 'yl', 'c'), 0, 0)  11.5 us
    all_to_all x1, waiting for transfers between devices, body(): sums = lax.all_to_all(sums, 'z', 0, 0)  7.32 us
    all_to_all x1, waiting for transfers between devices, body(): sums = lax.all_to_all(sums, ('x', 'yh', 'yl', 'c'), 0, 0)  2.7 us
  transfers between devices with their start and end apart: 12, of which 6 were waited for; matrix products, arithmetic and copies ran while one was open for 2% of the time, Pallas kernels for 10%

profile of v7, /device:TPU:1, one launch (start us, length us, event | category | flops | bytes accessed | tf_op | source)
XLA Modules:
  0.0 127.8 jit_solution(14626724289937364783)
XLA Ops:
  0.6 5.8 %collective-permute-start = (bf16[256,1536]{1,0:T(8,128)(2,1)}, bf16[256,1536]{1,0:T(8,128)(2,1)S(1)}, u32[]{:S(2)}, u32[]{:S(2)}) collective-permute-start(bf16[256,1536]{1,0:T(8,128)(2,1)} %bitcast.14), channel_id=1, source_target_pairs={{0,64},{1,65},{2,66},{3,67},{4,68},{5,69},{6,70},{7,71},{8,72},{9,... | collective-permute-start | bytes 2359304 | tf_op jit(solution)/shard_map/ppermute | solution.py:26
  6.4 1.3 %slice.21 = bf16[2,384,768]{2,1,0:T(8,128)(2,1)S(1)} slice(bf16[3,384,768]{2,1,0:T(8,128)(2,1)} %weight.1), slice={[0:2], [0:384], [0:768]} | slice | bytes 2359296 | tf_op jit(solution)/shard_map/slice | solution.py:292
  9.2 11.4 %collective-permute-done.block = bf16[256,1536]{1,0:T(8,128)(2,1)S(1)} collective-permute-done((bf16[256,1536]{1,0:T(8,128)(2,1)}, bf16[256,1536]{1,0:T(8,128)(2,1)S(1)}, u32[]{:S(2)}, u32[]{:S(2)}) %collective-permute-start) | collective-permute-done | bytes 786464 | tf_op jit(solution)/shard_map/ppermute | solution.py:26
  20.7 6.1 %collective-permute-start.1 = (bf16[2,384,768]{2,1,0:T(8,128)(2,1)S(1)}, bf16[2,384,768]{2,1,0:T(8,128)(2,1)}, u32[]{:S(2)}, u32[]{:S(2)}) collective-permute-start(bf16[2,384,768]{2,1,0:T(8,128)(2,1)S(1)} %slice.21), channel_id=1, source_target_pairs={{0,2},{1,3},{2,64},{3,65},{4,6},{5,7},{6,68},{7,69},{8,10},{9,11},... | collective-permute-start | bytes 3538952 | tf_op jit(solution)/shard_map/ppermute | solution.py:26
  26.8 3.4 %collective-permute-start.2 = (bf16[2,384,768]{2,1,0:T(8,128)(2,1)S(1)}, bf16[2,384,768]{2,1,0:T(8,128)(2,1)}, u32[]{:S(2)}, u32[]{:S(2)}) collective-permute-start(bf16[2,384,768]{2,1,0:T(8,128)(2,1)S(1)} %pad_maximum_fusion), channel_id=1, source_target_pairs={{0,66},{1,67},{2,0},{3,1},{4,70},{5,71},{6,4},{7,5},{8,74},{9,75},... | collective-permute-start | bytes 3538952 | tf_op jit(solution)/shard_map/ppermute | solution.py:26
  30.2 3.2 %collective-permute-start.3 = (bf16[256,1536]{1,0:T(8,128)(2,1)S(1)}, bf16[256,1536]{1,0:T(8,128)(2,1)S(1)}, u32[]{:S(2)}, u32[]{:S(2)}) collective-permute-start(bf16[256,1536]{1,0:T(8,128)(2,1)S(1)} %collective-permute-done.block), channel_id=1, source_target_pairs={{0,128},{1,129},{2,130},{3,131},{4,132},{5,133},{6,134},{7,135},{8... | collective-permute-start | bytes 2359304 | tf_op jit(solution)/shard_map/ppermute | solution.py:26
  33.4 4.2 %collective-permute-start.5 = (bf16[3,384,768]{2,1,0:T(8,128)(2,1)S(1)}, bf16[3,384,768]{2,1,0:T(8,128)(2,1)}, u32[]{:S(2)}, u32[]{:S(2)}) collective-permute-start(bf16[3,384,768]{2,1,0:T(8,128)(2,1)S(1)} %copy-done.2), channel_id=1, source_target_pairs={{0,1},{1,0},{2,3},{3,2},{4,5},{5,4},{6,7},{7,6},{8,9},{9,8},{10,11... | collective-permute-start | bytes 5308424 | tf_op jit(solution)/shard_map/ppermute | solution.py:26
  37.7 1.9 %collective-permute-start.4 = (bf16[384,768]{1,0:T(8,128)(2,1)S(1)}, bf16[384,768]{1,0:T(8,128)(2,1)S(1)}, u32[]{:S(2)}, u32[]{:S(2)}) collective-permute-start(bf16[384,768]{1,0:T(8,128)(2,1)S(1)} %slice_bitcast_fusion), channel_id=1, source_target_pairs={{0,1},{1,0},{2,3},{3,2},{4,5},{5,4},{6,7},{7,6},{8,9},{9,8},{10,11... | collective-permute-start | bytes 1769480 | tf_op jit(solution)/shard_map/ppermute | solution.py:26
  39.6 1.8 %prepare.4 = (bf16[256,1536]{1,0:T(8,128)(2,1)S(1)}, f32[256,1536]{1,0:T(8,128)S(1)}) custom-call(bf16[256,1536]{1,0:T(8,128)(2,1)S(1)} %bitcast.15, f32[1,1536]{1,0:T(1,128)S(1)} %broadcast_in_dim.6.gain), custom_call_target="tpu_custom_call" | custom-call | flops 15728640 | bytes 792576 | tf_op jit(solution)/shard_map/prepare/pallas_call | solution.py:241
  43.4 1.8 %prepare.3 = (bf16[256,1536]{1,0:T(8,128)(2,1)S(1)}, f32[256,1536]{1,0:T(8,128)S(1)}) custom-call(bf16[256,1536]{1,0:T(8,128)(2,1)S(1)} %collective-permute-done.block, f32[1,1536]{1,0:T(1,128)S(1)} %broadcast_in_dim.6.gain), custom_call_target="tpu_custom_call" | custom-call | flops 15728640 | bytes 792576 | tf_op jit(solution)/shard_map/prepare/pallas_call | solution.py:241
  48.1 1.8 %prepare.5 = (bf16[256,1536]{1,0:T(8,128)(2,1)S(1)}, f32[256,1536]{1,0:T(8,128)S(1)}) custom-call(bf16[256,1536]{1,0:T(8,128)(2,1)S(1)} %collective-permute-done.3.block, f32[1,1536]{1,0:T(1,128)S(1)} %broadcast_in_dim.6.gain), custom_call_target="tpu_custom_call" | custom-call | flops 15728640 | bytes 792576 | tf_op jit(solution)/shard_map/prepare/pallas_call | solution.py:241
  52.9 1.5 %collective-permute-done.2.down = bf16[2,384,768]{2,1,0:T(8,128)(2,1)} collective-permute-done((bf16[2,384,768]{2,1,0:T(8,128)(2,1)S(1)}, bf16[2,384,768]{2,1,0:T(8,128)(2,1)}, u32[]{:S(2)}, u32[]{:S(2)}) %collective-permute-start.2) | collective-permute-done | bytes 1179680 | tf_op jit(solution)/shard_map/ppermute | solution.py:26
  54.5 4.6 %collective-permute-start.6 = (bf16[2,384,768]{2,1,0:T(8,128)(2,1)}, bf16[2,384,768]{2,1,0:T(8,128)(2,1)}, u32[]{:S(2)}, u32[]{:S(2)}) collective-permute-start(bf16[2,384,768]{2,1,0:T(8,128)(2,1)} %collective-permute-done.1.up), channel_id=1, source_target_pairs={{0,1},{1,0},{2,3},{3,2},{4,5},{5,4},{6,7},{7,6},{8,9},{9,8},{10,11... | collective-permute-start | bytes 3538952 | tf_op jit(solution)/shard_map/ppermute | solution.py:26
  59.1 2.1 %collective-permute-start.7 = (bf16[2,384,768]{2,1,0:T(8,128)(2,1)}, bf16[2,384,768]{2,1,0:T(8,128)(2,1)}, u32[]{:S(2)}, u32[]{:S(2)}) collective-permute-start(bf16[2,384,768]{2,1,0:T(8,128)(2,1)} %collective-permute-done.2.down), channel_id=1, source_target_pairs={{0,1},{1,0},{2,3},{3,2},{4,5},{5,4},{6,7},{7,6},{8,9},{9,8},{10,11... | collective-permute-start | bytes 3538952 | tf_op jit(solution)/shard_map/ppermute | solution.py:26
  62.4 3.1 %place.1.placed = bf16[4,1536,768]{2,1,0:T(8,128)(2,1)S(1)} custom-call(s32[5]{0:T(128)S(1)} %stack.31.where, bf16[3,384,768]{2,1,0:T(8,128)(2,1)S(1)} %copy-done.2, bf16[384,768]{1,0:T(8,128)(2,1)S(1)} %copy-done.6, bf16[3,384,768]{2,1,0:T(8,128)(2,1)} %collective-permute-done.5.weight_s, bf16[384,768]{1,0:T(8,128)(2,1)S(1)} %copy-done.20, ...), custom_call_target="tpu_custom_call" | custom-call | flops 603979776 | bytes 7077908 | tf_op jit(solution)/shard_map/place/pallas_call | solution.py:241
  65.6 4.2 %early.1 = (bf16[4,1536,768]{2,1,0:T(8,128)(2,1)S(1)}, f32[256,768]{1,0:T(8,128)S(1)}, f32[256,768]{1,0:T(8,128)S(1)}) custom-call(s32[5]{0:T(128)S(1)} %stack.31.where, bf16[256,1536]{1,0:T(8,128)(2,1)S(1)} %copy-done.18, bf16[256,1536]{1,0:T(8,128)(2,1)S(1)} %bitcast.17, bf16[4,1536,768]{2,1,0:T(8,128)(2,1)S(1)} %place.1.placed, ...), custom_call_target="tpu_custom_call", output_to_operand_aliasing={{0}: (3, {})} | custom-call | flops 1207959552 | bytes 13369364 | tf_op jit(solution)/shard_map/early/pallas_call | solution.py:241
  69.9 6.5 %middle.1 = (bf16[256,768]{1,0:T(8,128)(2,1)S(1)}, f32[16,18,128]{2,1,0:T(8,128)}) custom-call(bf16[256,1536]{1,0:T(8,128)(2,1)S(1)} %copy-done.14, bf16[256,1536]{1,0:T(8,128)(2,1)S(1)} %copy-done.16, f32[256,1536]{1,0:T(8,128)S(1)} %copy-done.10, f32[256,1536]{1,0:T(8,128)S(1)} %copy-done.8, f32[256,1536]{1,0:T(8,128)S(1)} %copy-done.12, ...), custom_call_target="tpu_custom_call" | custom-call | flops 3019898880 | bytes 17304576 | tf_op jit(solution)/shard_map/middle/pallas_call | solution.py:241
  76.3 15.1 %all-to-all-start = ((f32[16,18,128]{2,1,0:T(8,128)}), f32[16,18,128]{2,1,0:T(8,128)S(1)}, u32[]{:S(2)}, u32[]{:S(2)}) async-start(f32[16,18,128]{2,1,0:T(8,128)} %get-tuple-element.44), calls=%async_computation | async-start | bytes 393216 | tf_op jit(solution)/shard_map/all_to_all | solution.py:368
  91.4 4.5 %collective-permute-start.8 = (bf16[256,768]{1,0:T(8,128)(2,1)S(1)}, bf16[256,768]{1,0:T(8,128)(2,1)S(1)}, u32[]{:S(2)}, u32[]{:S(2)}) collective-permute-start(bf16[256,768]{1,0:T(8,128)(2,1)S(1)} %get-tuple-element.43.here), channel_id=1, source_target_pairs={{0,64},{1,65},{2,66},{3,67},{4,68},{5,69},{6,70},{7,71},{8,72},{9,... | collective-permute-start | bytes 1179656 | tf_op jit(solution)/shard_map/ppermute | solution.py:26
  96.6 7.3 %all-to-all-done.arrived = f32[16,18,128]{2,1,0:T(8,128)S(1)} async-done(((f32[16,18,128]{2,1,0:T(8,128)}), f32[16,18,128]{2,1,0:T(8,128)S(1)}, u32[]{:S(2)}, u32[]{:S(2)}) %all-to-all-start) | async-done | bytes 147488 | tf_op jit(solution)/shard_map/all_to_all | solution.py:368
  104.8 11.5 %all-to-all-start.1 = ((f32[32,18,128]{2,1,0:T(8,128)}), f32[32,18,128]{2,1,0:T(8,128)S(1)}, u32[]{:S(2)}, u32[]{:S(2)}) async-start(f32[32,18,128]{2,1,0:T(8,128)} %spread.1), calls=%async_computation.1 | async-start | bytes 786432 | tf_op jit(solution)/shard_map/all_to_all | solution.py:372
  116.3 3.7 %copy-done.1 = bf16[4,1536,768]{2,1,0:T(8,128)(2,1)S(1)} copy-done((bf16[4,1536,768]{2,1,0:T(8,128)(2,1)S(1)}, bf16[4,1536,768]{2,1,0:T(8,128)(2,1)}, u32[]{:S(2)}) %copy-start.1) | copy-done | bytes 9437208
  120.0 3.9 %last.1 = bf16[256,1536]{1,0:T(8,128)(2,1)} custom-call(bf16[256,1536]{1,0:T(8,128)(2,1)S(1)} %bitcast.16, bf16[256,1536]{1,0:T(8,128)(2,1)S(1)} %bitcast.18, bf16[256,768]{1,0:T(8,128)(2,1)S(1)} %collective-permute-done.8.near, bf16[256,768]{1,0:T(8,128)(2,1)S(1)} %get-tuple-element.43.here, bf16[256,768]{1,0:T(8,128)(2,1)S(1)} %collective-permute-done.9.far, ...), custom_call_target="tpu_custom_call" | custom-call | flops 1811939328 | bytes 12195840 | tf_op jit(solution)/shard_map/last/pallas_call | solution.py:241
  123.9 2.7 %all-to-all-done.1 = f32[32,18,128]{2,1,0:T(8,128)S(1)} async-done(((f32[32,18,128]{2,1,0:T(8,128)}), f32[32,18,128]{2,1,0:T(8,128)S(1)}, u32[]{:S(2)}, u32[]{:S(2)}) %all-to-all-start.1) | async-done | bytes 294944 | tf_op jit(solution)/shard_map/all_to_all | solution.py:372
  (68 shorter events, 13.3 us)
Async XLA Ops:
  0.6 7.2 %copy-start.21 = (bf16[192,1536]{1,0:T(8,128)(2,1)S(1)}, bf16[192,1536]{1,0:T(8,128)(2,1)}, u32[]{:S(2)}) copy-start(bf16[192,1536]{1,0:T(8,128)(2,1)} %param.8) | copy-start | bytes 1769476
  0.6 20.1 %collective-permute-start = (bf16[256,1536]{1,0:T(8,128)(2,1)}, bf16[256,1536]{1,0:T(8,128)(2,1)S(1)}, u32[]{:S(2)}, u32[]{:S(2)}) collective-permute-start(bf16[256,1536]{1,0:T(8,128)(2,1)} %bitcast.14), channel_id=1, source_target_pairs={{0,64},{1,65},{2,66},{3,67},{4,68},{5,69},{6,70},{7,71},{8,72},{9,... | collective-permute-start | bytes 2359304 | tf_op jit(solution)/shard_map/ppermute | solution.py:26
  9.1 24.3 %copy-start.2 = (bf16[3,384,768]{2,1,0:T(8,128)(2,1)S(1)}, bf16[3,384,768]{2,1,0:T(8,128)(2,1)}, u32[]{:S(2)}) copy-start(bf16[3,384,768]{2,1,0:T(8,128)(2,1)} %weight.1) | copy-start | bytes 5308420
  9.2 30.4 %copy-start.22 = (f32[1536]{0:T(1024)S(1)}, f32[1536]{0:T(1024)}, u32[]{:S(2)}) copy-start(f32[1536]{0:T(1024)} %param.9) | copy-start | bytes 18436
  9.2 30.4 %copy-start.3 = (bf16[2,128,1536]{2,1,0:T(8,128)(2,1)S(1)}, bf16[2,128,1536]{2,1,0:T(8,128)(2,1)}, u32[]{:S(2)}) copy-start(bf16[2,128,1536]{2,1,0:T(8,128)(2,1)} %param.6) | copy-start | bytes 2359300
  20.7 32.2 %collective-permute-start.1 = (bf16[2,384,768]{2,1,0:T(8,128)(2,1)S(1)}, bf16[2,384,768]{2,1,0:T(8,128)(2,1)}, u32[]{:S(2)}, u32[]{:S(2)}) collective-permute-start(bf16[2,384,768]{2,1,0:T(8,128)(2,1)S(1)} %slice.21), channel_id=1, source_target_pairs={{0,2},{1,3},{2,64},{3,65},{4,6},{5,7},{6,68},{7,69},{8,10},{9,11},... | collective-permute-start | bytes 3538952 | tf_op jit(solution)/shard_map/ppermute | solution.py:26
  26.8 27.6 %collective-permute-start.2 = (bf16[2,384,768]{2,1,0:T(8,128)(2,1)S(1)}, bf16[2,384,768]{2,1,0:T(8,128)(2,1)}, u32[]{:S(2)}, u32[]{:S(2)}) collective-permute-start(bf16[2,384,768]{2,1,0:T(8,128)(2,1)S(1)} %pad_maximum_fusion), channel_id=1, source_target_pairs={{0,66},{1,67},{2,0},{3,1},{4,70},{5,71},{6,4},{7,5},{8,74},{9,75},... | collective-permute-start | bytes 3538952 | tf_op jit(solution)/shard_map/ppermute | solution.py:26
  30.2 17.9 %collective-permute-start.3 = (bf16[256,1536]{1,0:T(8,128)(2,1)S(1)}, bf16[256,1536]{1,0:T(8,128)(2,1)S(1)}, u32[]{:S(2)}, u32[]{:S(2)}) collective-permute-start(bf16[256,1536]{1,0:T(8,128)(2,1)S(1)} %collective-permute-done.block), channel_id=1, source_target_pairs={{0,128},{1,129},{2,130},{3,131},{4,132},{5,133},{6,134},{7,135},{8... | collective-permute-start | bytes 2359304 | tf_op jit(solution)/shard_map/ppermute | solution.py:26
  33.4 28.0 %collective-permute-start.5 = (bf16[3,384,768]{2,1,0:T(8,128)(2,1)S(1)}, bf16[3,384,768]{2,1,0:T(8,128)(2,1)}, u32[]{:S(2)}, u32[]{:S(2)}) collective-permute-start(bf16[3,384,768]{2,1,0:T(8,128)(2,1)S(1)} %copy-done.2), channel_id=1, source_target_pairs={{0,1},{1,0},{2,3},{3,2},{4,5},{5,4},{6,7},{7,6},{8,9},{9,8},{10,11... | collective-permute-start | bytes 5308424 | tf_op jit(solution)/shard_map/ppermute | solution.py:26
  37.7 14.2 %collective-permute-start.4 = (bf16[384,768]{1,0:T(8,128)(2,1)S(1)}, bf16[384,768]{1,0:T(8,128)(2,1)S(1)}, u32[]{:S(2)}, u32[]{:S(2)}) collective-permute-start(bf16[384,768]{1,0:T(8,128)(2,1)S(1)} %slice_bitcast_fusion), channel_id=1, source_target_pairs={{0,1},{1,0},{2,3},{3,2},{4,5},{5,4},{6,7},{7,6},{8,9},{9,8},{10,11... | collective-permute-start | bytes 1769480 | tf_op jit(solution)/shard_map/ppermute | solution.py:26
  39.6 21.6 %copy-start.23 = (f32[768]{0:T(1024)S(1)}, f32[768]{0:T(1024)}, u32[]{:S(2)}) copy-start(f32[768]{0:T(1024)} %param.10) | copy-start | bytes 9220
  39.6 21.7 %copy-start.6 = (bf16[384,768]{1,0:T(8,128)(2,1)S(1)}, bf16[384,768]{1,0:T(8,128)(2,1)}, u32[]{:S(2)}) copy-start(bf16[384,768]{1,0:T(8,128)(2,1)} %get-tuple-element.45.folded) | copy-start | bytes 1769476
  54.5 11.0 %collective-permute-start.6 = (bf16[2,384,768]{2,1,0:T(8,128)(2,1)}, bf16[2,384,768]{2,1,0:T(8,128)(2,1)}, u32[]{:S(2)}, u32[]{:S(2)}) collective-permute-start(bf16[2,384,768]{2,1,0:T(8,128)(2,1)} %collective-permute-done.1.up), channel_id=1, source_target_pairs={{0,1},{1,0},{2,3},{3,2},{4,5},{5,4},{6,7},{7,6},{8,9},{9,8},{10,11... | collective-permute-start | bytes 3538952 | tf_op jit(solution)/shard_map/ppermute | solution.py:26
  59.1 6.4 %collective-permute-start.7 = (bf16[2,384,768]{2,1,0:T(8,128)(2,1)}, bf16[2,384,768]{2,1,0:T(8,128)(2,1)}, u32[]{:S(2)}, u32[]{:S(2)}) collective-permute-start(bf16[2,384,768]{2,1,0:T(8,128)(2,1)} %collective-permute-done.2.down), channel_id=1, source_target_pairs={{0,1},{1,0},{2,3},{3,2},{4,5},{5,4},{6,7},{7,6},{8,9},{9,8},{10,11... | collective-permute-start | bytes 3538952 | tf_op jit(solution)/shard_map/ppermute | solution.py:26
  65.5 4.3 %copy-start.8 = (f32[256,1536]{1,0:T(8,128)S(1)}, f32[256,1536]{1,0:T(8,128)}, u32[]{:S(2)}) copy-start(f32[256,1536]{1,0:T(8,128)} %copy-done.7) | copy-start | bytes 4718596
  65.5 4.3 %copy-start.10 = (f32[256,1536]{1,0:T(8,128)S(1)}, f32[256,1536]{1,0:T(8,128)}, u32[]{:S(2)}) copy-start(f32[256,1536]{1,0:T(8,128)} %copy-done.9) | copy-start | bytes 4718596
  65.6 4.3 %copy-start.12 = (f32[256,1536]{1,0:T(8,128)S(1)}, f32[256,1536]{1,0:T(8,128)}, u32[]{:S(2)}) copy-start(f32[256,1536]{1,0:T(8,128)} %copy-done.11) | copy-start | bytes 4718596
  65.6 4.3 %copy-start.14 = (bf16[256,1536]{1,0:T(8,128)(2,1)S(1)}, bf16[256,1536]{1,0:T(8,128)(2,1)}, u32[]{:S(2)}) copy-start(bf16[256,1536]{1,0:T(8,128)(2,1)} %copy-done.13) | copy-start | bytes 2359300
  69.8 6.5 %copy-start = (bf16[4,1536,768]{2,1,0:T(8,128)(2,1)}, bf16[4,1536,768]{2,1,0:T(8,128)(2,1)S(1)}, u32[]{:S(2)}) copy-start(bf16[4,1536,768]{2,1,0:T(8,128)(2,1)S(1)} %get-tuple-element.40.whole) | copy-start | bytes 28311556
  76.3 40.0 %copy-start.5 = (bf16[2,128,1536]{2,1,0:T(8,128)(2,1)S(1)}, bf16[2,128,1536]{2,1,0:T(8,128)(2,1)}, u32[]{:S(2)}) copy-start(bf16[2,128,1536]{2,1,0:T(8,128)(2,1)} %param.11) | copy-start | bytes 2359300
  76.3 27.6 %all-to-all-start = ((f32[16,18,128]{2,1,0:T(8,128)}), f32[16,18,128]{2,1,0:T(8,128)S(1)}, u32[]{:S(2)}, u32[]{:S(2)}) async-start(f32[16,18,128]{2,1,0:T(8,128)} %get-tuple-element.44), calls=%async_computation | async-start | bytes 393216 | tf_op jit(solution)/shard_map/all_to_all | solution.py:368
  91.4 24.9 %collective-permute-start.8 = (bf16[256,768]{1,0:T(8,128)(2,1)S(1)}, bf16[256,768]{1,0:T(8,128)(2,1)S(1)}, u32[]{:S(2)}, u32[]{:S(2)}) collective-permute-start(bf16[256,768]{1,0:T(8,128)(2,1)S(1)} %get-tuple-element.43.here), channel_id=1, source_target_pairs={{0,64},{1,65},{2,66},{3,67},{4,68},{5,69},{6,70},{7,71},{8,72},{9,... | collective-permute-start | bytes 1179656 | tf_op jit(solution)/shard_map/ppermute | solution.py:26
  96.0 20.3 %collective-permute-start.9 = (bf16[256,768]{1,0:T(8,128)(2,1)S(1)}, bf16[256,768]{1,0:T(8,128)(2,1)S(1)}, u32[]{:S(2)}, u32[]{:S(2)}) collective-permute-start(bf16[256,768]{1,0:T(8,128)(2,1)S(1)} %get-tuple-element.43.here), channel_id=1, source_target_pairs={{64,128},{65,129},{66,130},{67,131},{68,132},{69,133},{70,134},{71... | collective-permute-start | bytes 1179656 | tf_op jit(solution)/shard_map/ppermute | solution.py:26
  104.8 21.8 %all-to-all-start.1 = ((f32[32,18,128]{2,1,0:T(8,128)}), f32[32,18,128]{2,1,0:T(8,128)S(1)}, u32[]{:S(2)}, u32[]{:S(2)}) async-start(f32[32,18,128]{2,1,0:T(8,128)} %spread.1), calls=%async_computation.1 | async-start | bytes 786432 | tf_op jit(solution)/shard_map/all_to_all | solution.py:372
  (13 other events, 23.5 us)

commit v8 on v7

--- a/solution.py
+++ b/solution.py
@@ -90,7 +90,7 @@
         a = unit * gain[...]
         t, slope = bend(a)
         hidden[rows, :] = (0.5 * a * (1.0 + t)).astype(jnp.bfloat16)
-        weigh[rows, :] = slope * unit
+        weigh[rows, :] = (slope * unit).astype(jnp.bfloat16)
 
     over_rows(block.shape[0], step)
 
@@ -201,9 +201,9 @@
     put(channels, jnp.sum(partial[...], axis=0, keepdims=True))
     for n in range(0, channels, 256):
         cols = slice(n, n + 256)
-        terms = dot_t(grad_mixed[...], whole[0, cols, :]) * e0[:, cols]
-        terms += dot_t(grad_mixed[...], whole[1, cols, :]) * e1[:, cols]
-        terms += dot_t(grad_mixed[...], whole[2, cols, :]) * e2[:, cols]
+        terms = dot_t(grad_mixed[...], whole[0, cols, :]) * e0[:, cols].astype(jnp.float32)
+        terms += dot_t(grad_mixed[...], whole[1, cols, :]) * e1[:, cols].astype(jnp.float32)
+        terms += dot_t(grad_mixed[...], whole[2, cols, :]) * e2[:, cols].astype(jnp.float32)
         put(n, jnp.sum(terms, axis=0, keepdims=True))
 
 
@@ -278,7 +278,7 @@
         return call(
             prepare_kernel,
             "prepare",
-            [jax.ShapeDtypeStruct(block.shape, bf16), jax.ShapeDtypeStruct(block.shape, f32)],
+            [jax.ShapeDtypeStruct(block.shape, bf16)] * 2,
             [],
             40 * block.size,
             block,
@@ -346,9 +346,9 @@
             pltpu.VMEM((rows, width), f32),
             pltpu.VMEM((8, width), f32),
             pltpu.VMEM((rows, channels), bf16),
-            pltpu.VMEM((rows, channels), f32),
-            pltpu.VMEM((rows, channels), f32),
-            pltpu.VMEM((rows, channels), f32),
+            pltpu.VMEM((rows, channels), bf16),
+            pltpu.VMEM((rows, channels), bf16),
+            pltpu.VMEM((rows, channels), bf16),
             pltpu.SemaphoreType.DMA((4,)),
         ],
         5 * work,

time: 129 us -> 128 us (level)
  no operation moved by 1% of the time
where the time goes in v8:
time: 128 us
  starting transfers between devices  63.1 us (49%)
  waiting for transfers between devices  24.7 us (19%)
  Pallas kernels  23.5 us (18%)
  local copies, waits for them, and re-layouts  12.8 us (10%)
  other arithmetic  2.32 us (2%)
    ppermute x10, starting transfers between devices, permute(): return lax.ppermute(value, AXES, pairs)  36.5 us
    pallas_call x8, Pallas kernels, call(): pl.pallas_call(kernel, name=name, out_shape=out_shape, in_specs=specs or...  23.5 us
    all_to_all x1, starting transfers between devices, body(): sums = lax.all_to_all(sums, 'z', 0, 0)  15.1 us
    ppermute x10, waiting for transfers between devices, permute(): return lax.ppermute(value, AXES, pairs)  14.7 us
    all_to_all x1, starting transfers between devices, body(): sums = lax.all_to_all(sums, ('x', 'yh', 'yl', 'c'), 0, 0)  11.5 us
    unnamed x48, local copies, waits for them, and re-layouts  11 us
    all_to_all x1, waiting for transfers between devices, body(): sums = lax.all_to_all(sums, 'z', 0, 0)  7.33 us
    all_to_all x1, waiting for transfers between devices, body(): sums = lax.all_to_all(sums, ('x', 'yh', 'yl', 'c'), 0, 0)  2.68 us
  transfers between devices with their start and end apart: 12, of which 6 were waited for; matrix products, arithmetic and copies ran while one was open for 2% of the time, Pallas kernels for 10%

profile of v8, /device:TPU:1, one launch (start us, length us, event | category | flops | bytes accessed | tf_op | source)
XLA Modules:
  0.0 127.6 jit_solution(10406862961139734629)
XLA Ops:
  0.6 5.8 %collective-permute-start = (bf16[256,1536]{1,0:T(8,128)(2,1)}, bf16[256,1536]{1,0:T(8,128)(2,1)S(1)}, u32[]{:S(2)}, u32[]{:S(2)}) collective-permute-start(bf16[256,1536]{1,0:T(8,128)(2,1)} %bitcast.14), channel_id=1, source_target_pairs={{0,64},{1,65},{2,66},{3,67},{4,68},{5,69},{6,70},{7,71},{8,72},{9,... | collective-permute-start | bytes 2359304 | tf_op jit(solution)/shard_map/ppermute | solution.py:26
  6.4 1.3 %slice.21 = bf16[2,384,768]{2,1,0:T(8,128)(2,1)S(1)} slice(bf16[3,384,768]{2,1,0:T(8,128)(2,1)} %weight.1), slice={[0:2], [0:384], [0:768]} | slice | bytes 2359296 | tf_op jit(solution)/shard_map/slice | solution.py:292
  9.2 11.4 %collective-permute-done.block = bf16[256,1536]{1,0:T(8,128)(2,1)S(1)} collective-permute-done((bf16[256,1536]{1,0:T(8,128)(2,1)}, bf16[256,1536]{1,0:T(8,128)(2,1)S(1)}, u32[]{:S(2)}, u32[]{:S(2)}) %collective-permute-start) | collective-permute-done | bytes 786464 | tf_op jit(solution)/shard_map/ppermute | solution.py:26
  20.7 6.1 %collective-permute-start.1 = (bf16[2,384,768]{2,1,0:T(8,128)(2,1)S(1)}, bf16[2,384,768]{2,1,0:T(8,128)(2,1)}, u32[]{:S(2)}, u32[]{:S(2)}) collective-permute-start(bf16[2,384,768]{2,1,0:T(8,128)(2,1)S(1)} %slice.21), channel_id=1, source_target_pairs={{0,2},{1,3},{2,64},{3,65},{4,6},{5,7},{6,68},{7,69},{8,10},{9,11},... | collective-permute-start | bytes 3538952 | tf_op jit(solution)/shard_map/ppermute | solution.py:26
  26.8 3.4 %collective-permute-start.2 = (bf16[2,384,768]{2,1,0:T(8,128)(2,1)S(1)}, bf16[2,384,768]{2,1,0:T(8,128)(2,1)}, u32[]{:S(2)}, u32[]{:S(2)}) collective-permute-start(bf16[2,384,768]{2,1,0:T(8,128)(2,1)S(1)} %pad_maximum_fusion), channel_id=1, source_target_pairs={{0,66},{1,67},{2,0},{3,1},{4,70},{5,71},{6,4},{7,5},{8,74},{9,75},... | collective-permute-start | bytes 3538952 | tf_op jit(solution)/shard_map/ppermute | solution.py:26
  30.2 3.2 %collective-permute-start.3 = (bf16[256,1536]{1,0:T(8,128)(2,1)S(1)}, bf16[256,1536]{1,0:T(8,128)(2,1)S(1)}, u32[]{:S(2)}, u32[]{:S(2)}) collective-permute-start(bf16[256,1536]{1,0:T(8,128)(2,1)S(1)} %collective-permute-done.block), channel_id=1, source_target_pairs={{0,128},{1,129},{2,130},{3,131},{4,132},{5,133},{6,134},{7,135},{8... | collective-permute-start | bytes 2359304 | tf_op jit(solution)/shard_map/ppermute | solution.py:26
  33.4 4.2 %collective-permute-start.5 = (bf16[3,384,768]{2,1,0:T(8,128)(2,1)S(1)}, bf16[3,384,768]{2,1,0:T(8,128)(2,1)}, u32[]{:S(2)}, u32[]{:S(2)}) collective-permute-start(bf16[3,384,768]{2,1,0:T(8,128)(2,1)S(1)} %copy-done.2), channel_id=1, source_target_pairs={{0,1},{1,0},{2,3},{3,2},{4,5},{5,4},{6,7},{7,6},{8,9},{9,8},{10,11... | collective-permute-start | bytes 5308424 | tf_op jit(solution)/shard_map/ppermute | solution.py:26
  37.7 1.9 %collective-permute-start.4 = (bf16[384,768]{1,0:T(8,128)(2,1)S(1)}, bf16[384,768]{1,0:T(8,128)(2,1)S(1)}, u32[]{:S(2)}, u32[]{:S(2)}) collective-permute-start(bf16[384,768]{1,0:T(8,128)(2,1)S(1)} %slice_bitcast_fusion), channel_id=1, source_target_pairs={{0,1},{1,0},{2,3},{3,2},{4,5},{5,4},{6,7},{7,6},{8,9},{9,8},{10,11... | collective-permute-start | bytes 1769480 | tf_op jit(solution)/shard_map/ppermute | solution.py:26
  39.6 1.8 %prepare.4 = (bf16[256,1536]{1,0:T(8,128)(2,1)S(1)}, bf16[256,1536]{1,0:T(8,128)(2,1)S(1)}) custom-call(bf16[256,1536]{1,0:T(8,128)(2,1)S(1)} %bitcast.15, f32[1,1536]{1,0:T(1,128)S(1)} %broadcast_in_dim.6.gain), custom_call_target="tpu_custom_call" | custom-call | flops 15728640 | bytes 792576 | tf_op jit(solution)/shard_map/prepare/pallas_call | solution.py:241
  43.2 1.8 %prepare.3 = (bf16[256,1536]{1,0:T(8,128)(2,1)S(1)}, bf16[256,1536]{1,0:T(8,128)(2,1)S(1)}) custom-call(bf16[256,1536]{1,0:T(8,128)(2,1)S(1)} %collective-permute-done.block, f32[1,1536]{1,0:T(1,128)S(1)} %broadcast_in_dim.6.gain), custom_call_target="tpu_custom_call" | custom-call | flops 15728640 | bytes 792576 | tf_op jit(solution)/shard_map/prepare/pallas_call | solution.py:241
  48.1 1.8 %prepare.5 = (bf16[256,1536]{1,0:T(8,128)(2,1)S(1)}, bf16[256,1536]{1,0:T(8,128)(2,1)S(1)}) custom-call(bf16[256,1536]{1,0:T(8,128)(2,1)S(1)} %collective-permute-done.3.block, f32[1,1536]{1,0:T(1,128)S(1)} %broadcast_in_dim.6.gain), custom_call_target="tpu_custom_call" | custom-call | flops 15728640 | bytes 792576 | tf_op jit(solution)/shard_map/prepare/pallas_call | solution.py:241
  52.9 1.5 %collective-permute-done.2.down = bf16[2,384,768]{2,1,0:T(8,128)(2,1)} collective-permute-done((bf16[2,384,768]{2,1,0:T(8,128)(2,1)S(1)}, bf16[2,384,768]{2,1,0:T(8,128)(2,1)}, u32[]{:S(2)}, u32[]{:S(2)}) %collective-permute-start.2) | collective-permute-done | bytes 1179680 | tf_op jit(solution)/shard_map/ppermute | solution.py:26
  54.5 4.6 %collective-permute-start.6 = (bf16[2,384,768]{2,1,0:T(8,128)(2,1)}, bf16[2,384,768]{2,1,0:T(8,128)(2,1)}, u32[]{:S(2)}, u32[]{:S(2)}) collective-permute-start(bf16[2,384,768]{2,1,0:T(8,128)(2,1)} %collective-permute-done.1.up), channel_id=1, source_target_pairs={{0,1},{1,0},{2,3},{3,2},{4,5},{5,4},{6,7},{7,6},{8,9},{9,8},{10,11... | collective-permute-start | bytes 3538952 | tf_op jit(solution)/shard_map/ppermute | solution.py:26
  59.1 2.1 %collective-permute-start.7 = (bf16[2,384,768]{2,1,0:T(8,128)(2,1)}, bf16[2,384,768]{2,1,0:T(8,128)(2,1)}, u32[]{:S(2)}, u32[]{:S(2)}) collective-permute-start(bf16[2,384,768]{2,1,0:T(8,128)(2,1)} %collective-permute-done.2.down), channel_id=1, source_target_pairs={{0,1},{1,0},{2,3},{3,2},{4,5},{5,4},{6,7},{7,6},{8,9},{9,8},{10,11... | collective-permute-start | bytes 3538952 | tf_op jit(solution)/shard_map/ppermute | solution.py:26
  62.4 3.1 %place.1.placed = bf16[4,1536,768]{2,1,0:T(8,128)(2,1)S(1)} custom-call(s32[5]{0:T(128)S(1)} %stack.31.where, bf16[3,384,768]{2,1,0:T(8,128)(2,1)S(1)} %copy-done.2, bf16[384,768]{1,0:T(8,128)(2,1)S(1)} %copy-done.6, bf16[3,384,768]{2,1,0:T(8,128)(2,1)} %collective-permute-done.5.weight_s, bf16[384,768]{1,0:T(8,128)(2,1)S(1)} %copy-done.20, ...), custom_call_target="tpu_custom_call" | custom-call | flops 603979776 | bytes 7077908 | tf_op jit(solution)/shard_map/place/pallas_call | solution.py:241
  65.6 4.2 %early.1 = (bf16[4,1536,768]{2,1,0:T(8,128)(2,1)S(1)}, f32[256,768]{1,0:T(8,128)S(1)}, f32[256,768]{1,0:T(8,128)S(1)}) custom-call(s32[5]{0:T(128)S(1)} %stack.31.where, bf16[256,1536]{1,0:T(8,128)(2,1)S(1)} %copy-done.18, bf16[256,1536]{1,0:T(8,128)(2,1)S(1)} %bitcast.17, bf16[4,1536,768]{2,1,0:T(8,128)(2,1)S(1)} %place.1.placed, ...), custom_call_target="tpu_custom_call", output_to_operand_aliasing={{0}: (3, {})} | custom-call | flops 1207959552 | bytes 13369364 | tf_op jit(solution)/shard_map/early/pallas_call | solution.py:241
  69.9 6.2 %middle.1 = (bf16[256,768]{1,0:T(8,128)(2,1)S(1)}, f32[16,18,128]{2,1,0:T(8,128)}) custom-call(bf16[256,1536]{1,0:T(8,128)(2,1)S(1)} %copy-done.10, bf16[256,1536]{1,0:T(8,128)(2,1)S(1)} %copy-done.14, bf16[256,1536]{1,0:T(8,128)(2,1)S(1)} %copy-done.12, bf16[256,1536]{1,0:T(8,128)(2,1)S(1)} %copy-done.8, bf16[256,1536]{1,0:T(8,128)(2,1)S(1)} %copy-done.16, ...), custom_call_target="tpu_custom_call" | custom-call | flops 3019898880 | bytes 14945280 | tf_op jit(solution)/shard_map/middle/pallas_call | solution.py:241
  76.1 15.1 %all-to-all-start = ((f32[16,18,128]{2,1,0:T(8,128)}), f32[16,18,128]{2,1,0:T(8,128)S(1)}, u32[]{:S(2)}, u32[]{:S(2)}) async-start(f32[16,18,128]{2,1,0:T(8,128)} %get-tuple-element.44), calls=%async_computation | async-start | bytes 393216 | tf_op jit(solution)/shard_map/all_to_all | solution.py:368
  91.2 4.5 %collective-permute-start.8 = (bf16[256,768]{1,0:T(8,128)(2,1)S(1)}, bf16[256,768]{1,0:T(8,128)(2,1)S(1)}, u32[]{:S(2)}, u32[]{:S(2)}) collective-permute-start(bf16[256,768]{1,0:T(8,128)(2,1)S(1)} %get-tuple-element.43.here), channel_id=1, source_target_pairs={{0,64},{1,65},{2,66},{3,67},{4,68},{5,69},{6,70},{7,71},{8,72},{9,... | collective-permute-start | bytes 1179656 | tf_op jit(solution)/shard_map/ppermute | solution.py:26
  96.4 7.3 %all-to-all-done.arrived = f32[16,18,128]{2,1,0:T(8,128)S(1)} async-done(((f32[16,18,128]{2,1,0:T(8,128)}), f32[16,18,128]{2,1,0:T(8,128)S(1)}, u32[]{:S(2)}, u32[]{:S(2)}) %all-to-all-start) | async-done | bytes 147488 | tf_op jit(solution)/shard_map/all_to_all | solution.py:368
  104.5 11.5 %all-to-all-start.1 = ((f32[32,18,128]{2,1,0:T(8,128)}), f32[32,18,128]{2,1,0:T(8,128)S(1)}, u32[]{:S(2)}, u32[]{:S(2)}) async-start(f32[32,18,128]{2,1,0:T(8,128)} %spread.1), calls=%async_computation.1 | async-start | bytes 786432 | tf_op jit(solution)/shard_map/all_to_all | solution.py:372
  116.1 3.7 %copy-done.1 = bf16[4,1536,768]{2,1,0:T(8,128)(2,1)S(1)} copy-done((bf16[4,1536,768]{2,1,0:T(8,128)(2,1)S(1)}, bf16[4,1536,768]{2,1,0:T(8,128)(2,1)}, u32[]{:S(2)}) %copy-start.1) | copy-done | bytes 9437208
  119.8 3.9 %last.1 = bf16[256,1536]{1,0:T(8,128)(2,1)} custom-call(bf16[256,1536]{1,0:T(8,128)(2,1)S(1)} %bitcast.16, bf16[256,1536]{1,0:T(8,128)(2,1)S(1)} %bitcast.18, bf16[256,768]{1,0:T(8,128)(2,1)S(1)} %collective-permute-done.8.near, bf16[256,768]{1,0:T(8,128)(2,1)S(1)} %get-tuple-element.43.here, bf16[256,768]{1,0:T(8,128)(2,1)S(1)} %collective-permute-done.9.far, ...), custom_call_target="tpu_custom_call" | custom-call | flops 1811939328 | bytes 12195840 | tf_op jit(solution)/shard_map/last/pallas_call | solution.py:241
  123.7 2.7 %all-to-all-done.1 = f32[32,18,128]{2,1,0:T(8,128)S(1)} async-done(((f32[32,18,128]{2,1,0:T(8,128)}), f32[32,18,128]{2,1,0:T(8,128)S(1)}, u32[]{:S(2)}, u32[]{:S(2)}) %all-to-all-start.1) | async-done | bytes 294944 | tf_op jit(solution)/shard_map/all_to_all | solution.py:372
  (68 shorter events, 13.3 us)
Async XLA Ops:
  0.6 7.2 %copy-start.21 = (bf16[192,1536]{1,0:T(8,128)(2,1)S(1)}, bf16[192,1536]{1,0:T(8,128)(2,1)}, u32[]{:S(2)}) copy-start(bf16[192,1536]{1,0:T(8,128)(2,1)} %param.8) | copy-start | bytes 1769476
  0.6 20.1 %collective-permute-start = (bf16[256,1536]{1,0:T(8,128)(2,1)}, bf16[256,1536]{1,0:T(8,128)(2,1)S(1)}, u32[]{:S(2)}, u32[]{:S(2)}) collective-permute-start(bf16[256,1536]{1,0:T(8,128)(2,1)} %bitcast.14), channel_id=1, source_target_pairs={{0,64},{1,65},{2,66},{3,67},{4,68},{5,69},{6,70},{7,71},{8,72},{9,... | collective-permute-start | bytes 2359304 | tf_op jit(solution)/shard_map/ppermute | solution.py:26
  9.1 24.3 %copy-start.2 = (bf16[3,384,768]{2,1,0:T(8,128)(2,1)S(1)}, bf16[3,384,768]{2,1,0:T(8,128)(2,1)}, u32[]{:S(2)}) copy-start(bf16[3,384,768]{2,1,0:T(8,128)(2,1)} %weight.1) | copy-start | bytes 5308420
  9.2 30.4 %copy-start.22 = (f32[1536]{0:T(1024)S(1)}, f32[1536]{0:T(1024)}, u32[]{:S(2)}) copy-start(f32[1536]{0:T(1024)} %param.9) | copy-start | bytes 18436
  9.2 30.4 %copy-start.3 = (bf16[2,128,1536]{2,1,0:T(8,128)(2,1)S(1)}, bf16[2,128,1536]{2,1,0:T(8,128)(2,1)}, u32[]{:S(2)}) copy-start(bf16[2,128,1536]{2,1,0:T(8,128)(2,1)} %param.6) | copy-start | bytes 2359300
  20.7 32.2 %collective-permute-start.1 = (bf16[2,384,768]{2,1,0:T(8,128)(2,1)S(1)}, bf16[2,384,768]{2,1,0:T(8,128)(2,1)}, u32[]{:S(2)}, u32[]{:S(2)}) collective-permute-start(bf16[2,384,768]{2,1,0:T(8,128)(2,1)S(1)} %slice.21), channel_id=1, source_target_pairs={{0,2},{1,3},{2,64},{3,65},{4,6},{5,7},{6,68},{7,69},{8,10},{9,11},... | collective-permute-start | bytes 3538952 | tf_op jit(solution)/shard_map/ppermute | solution.py:26
  26.8 27.6 %collective-permute-start.2 = (bf16[2,384,768]{2,1,0:T(8,128)(2,1)S(1)}, bf16[2,384,768]{2,1,0:T(8,128)(2,1)}, u32[]{:S(2)}, u32[]{:S(2)}) collective-permute-start(bf16[2,384,768]{2,1,0:T(8,128)(2,1)S(1)} %pad_maximum_fusion), channel_id=1, source_target_pairs={{0,66},{1,67},{2,0},{3,1},{4,70},{5,71},{6,4},{7,5},{8,74},{9,75},... | collective-permute-start | bytes 3538952 | tf_op jit(solution)/shard_map/ppermute | solution.py:26
  30.2 17.9 %collective-permute-start.3 = (bf16[256,1536]{1,0:T(8,128)(2,1)S(1)}, bf16[256,1536]{1,0:T(8,128)(2,1)S(1)}, u32[]{:S(2)}, u32[]{:S(2)}) collective-permute-start(bf16[256,1536]{1,0:T(8,128)(2,1)S(1)} %collective-permute-done.block), channel_id=1, source_target_pairs={{0,128},{1,129},{2,130},{3,131},{4,132},{5,133},{6,134},{7,135},{8... | collective-permute-start | bytes 2359304 | tf_op jit(solution)/shard_map/ppermute | solution.py:26
  33.4 28.0 %collective-permute-start.5 = (bf16[3,384,768]{2,1,0:T(8,128)(2,1)S(1)}, bf16[3,384,768]{2,1,0:T(8,128)(2,1)}, u32[]{:S(2)}, u32[]{:S(2)}) collective-permute-start(bf16[3,384,768]{2,1,0:T(8,128)(2,1)S(1)} %copy-done.2), channel_id=1, source_target_pairs={{0,1},{1,0},{2,3},{3,2},{4,5},{5,4},{6,7},{7,6},{8,9},{9,8},{10,11... | collective-permute-start | bytes 5308424 | tf_op jit(solution)/shard_map/ppermute | solution.py:26
  37.7 14.0 %collective-permute-start.4 = (bf16[384,768]{1,0:T(8,128)(2,1)S(1)}, bf16[384,768]{1,0:T(8,128)(2,1)S(1)}, u32[]{:S(2)}, u32[]{:S(2)}) collective-permute-start(bf16[384,768]{1,0:T(8,128)(2,1)S(1)} %slice_bitcast_fusion), channel_id=1, source_target_pairs={{0,1},{1,0},{2,3},{3,2},{4,5},{5,4},{6,7},{7,6},{8,9},{9,8},{10,11... | collective-permute-start | bytes 1769480 | tf_op jit(solution)/shard_map/ppermute | solution.py:26
  39.6 21.6 %copy-start.23 = (f32[768]{0:T(1024)S(1)}, f32[768]{0:T(1024)}, u32[]{:S(2)}) copy-start(f32[768]{0:T(1024)} %param.10) | copy-start | bytes 9220
  39.6 21.7 %copy-start.6 = (bf16[384,768]{1,0:T(8,128)(2,1)S(1)}, bf16[384,768]{1,0:T(8,128)(2,1)}, u32[]{:S(2)}) copy-start(bf16[384,768]{1,0:T(8,128)(2,1)} %get-tuple-element.45.folded) | copy-start | bytes 1769476
  54.5 11.0 %collective-permute-start.6 = (bf16[2,384,768]{2,1,0:T(8,128)(2,1)}, bf16[2,384,768]{2,1,0:T(8,128)(2,1)}, u32[]{:S(2)}, u32[]{:S(2)}) collective-permute-start(bf16[2,384,768]{2,1,0:T(8,128)(2,1)} %collective-permute-done.1.up), channel_id=1, source_target_pairs={{0,1},{1,0},{2,3},{3,2},{4,5},{5,4},{6,7},{7,6},{8,9},{9,8},{10,11... | collective-permute-start | bytes 3538952 | tf_op jit(solution)/shard_map/ppermute | solution.py:26
  59.1 6.4 %collective-permute-start.7 = (bf16[2,384,768]{2,1,0:T(8,128)(2,1)}, bf16[2,384,768]{2,1,0:T(8,128)(2,1)}, u32[]{:S(2)}, u32[]{:S(2)}) collective-permute-start(bf16[2,384,768]{2,1,0:T(8,128)(2,1)} %collective-permute-done.2.down), channel_id=1, source_target_pairs={{0,1},{1,0},{2,3},{3,2},{4,5},{5,4},{6,7},{7,6},{8,9},{9,8},{10,11... | collective-permute-start | bytes 3538952 | tf_op jit(solution)/shard_map/ppermute | solution.py:26
  65.5 4.3 %copy-start.8 = (bf16[256,1536]{1,0:T(8,128)(2,1)S(1)}, bf16[256,1536]{1,0:T(8,128)(2,1)}, u32[]{:S(2)}) copy-start(bf16[256,1536]{1,0:T(8,128)(2,1)} %copy-done.7) | copy-start | bytes 2359300
  65.5 4.3 %copy-start.10 = (bf16[256,1536]{1,0:T(8,128)(2,1)S(1)}, bf16[256,1536]{1,0:T(8,128)(2,1)}, u32[]{:S(2)}) copy-start(bf16[256,1536]{1,0:T(8,128)(2,1)} %copy-done.9) | copy-start | bytes 2359300
  65.6 4.3 %copy-start.12 = (bf16[256,1536]{1,0:T(8,128)(2,1)S(1)}, bf16[256,1536]{1,0:T(8,128)(2,1)}, u32[]{:S(2)}) copy-start(bf16[256,1536]{1,0:T(8,128)(2,1)} %copy-done.11) | copy-start | bytes 2359300
  65.6 4.3 %copy-start.14 = (bf16[256,1536]{1,0:T(8,128)(2,1)S(1)}, bf16[256,1536]{1,0:T(8,128)(2,1)}, u32[]{:S(2)}) copy-start(bf16[256,1536]{1,0:T(8,128)(2,1)} %copy-done.13) | copy-start | bytes 2359300
  69.8 6.3 %copy-start = (bf16[4,1536,768]{2,1,0:T(8,128)(2,1)}, bf16[4,1536,768]{2,1,0:T(8,128)(2,1)S(1)}, u32[]{:S(2)}) copy-start(bf16[4,1536,768]{2,1,0:T(8,128)(2,1)S(1)} %get-tuple-element.40.whole) | copy-start | bytes 28311556
  76.1 40.0 %copy-start.5 = (bf16[2,128,1536]{2,1,0:T(8,128)(2,1)S(1)}, bf16[2,128,1536]{2,1,0:T(8,128)(2,1)}, u32[]{:S(2)}) copy-start(bf16[2,128,1536]{2,1,0:T(8,128)(2,1)} %param.11) | copy-start | bytes 2359300
  76.1 27.6 %all-to-all-start = ((f32[16,18,128]{2,1,0:T(8,128)}), f32[16,18,128]{2,1,0:T(8,128)S(1)}, u32[]{:S(2)}, u32[]{:S(2)}) async-start(f32[16,18,128]{2,1,0:T(8,128)} %get-tuple-element.44), calls=%async_computation | async-start | bytes 393216 | tf_op jit(solution)/shard_map/all_to_all | solution.py:368
  91.2 24.9 %collective-permute-start.8 = (bf16[256,768]{1,0:T(8,128)(2,1)S(1)}, bf16[256,768]{1,0:T(8,128)(2,1)S(1)}, u32[]{:S(2)}, u32[]{:S(2)}) collective-permute-start(bf16[256,768]{1,0:T(8,128)(2,1)S(1)} %get-tuple-element.43.here), channel_id=1, source_target_pairs={{0,64},{1,65},{2,66},{3,67},{4,68},{5,69},{6,70},{7,71},{8,72},{9,... | collective-permute-start | bytes 1179656 | tf_op jit(solution)/shard_map/ppermute | solution.py:26
  95.7 20.3 %collective-permute-start.9 = (bf16[256,768]{1,0:T(8,128)(2,1)S(1)}, bf16[256,768]{1,0:T(8,128)(2,1)S(1)}, u32[]{:S(2)}, u32[]{:S(2)}) collective-permute-start(bf16[256,768]{1,0:T(8,128)(2,1)S(1)} %get-tuple-element.43.here), channel_id=1, source_target_pairs={{64,128},{65,129},{66,130},{67,131},{68,132},{69,133},{70,134},{71... | collective-permute-start | bytes 1179656 | tf_op jit(solution)/shard_map/ppermute | solution.py:26
  104.5 21.8 %all-to-all-start.1 = ((f32[32,18,128]{2,1,0:T(8,128)}), f32[32,18,128]{2,1,0:T(8,128)S(1)}, u32[]{:S(2)}, u32[]{:S(2)}) async-start(f32[32,18,128]{2,1,0:T(8,128)} %spread.1), calls=%async_computation.1 | async-start | bytes 786432 | tf_op jit(solution)/shard_map/all_to_all | solution.py:372
  (13 other events, 22.7 us)

commit v9 on v7

--- a/solution.py
+++ b/solution.py
@@ -212,15 +212,19 @@
     sums[...] = jnp.broadcast_to(total, sums.shape)
 
 
-def last_kernel(block, cotangent, near, here, far, whole, gain, result, grads):
+def last_kernel(
+    block, cotangent, near, here, far, away, gain, result, grads, whole, semaphores
+):
+    fetched = fetch(
+        [away.at[k] for k in (1, 2, 0)], [whole.at[k] for k in (1, 2, 0)], semaphores
+    )
     rows, channels = block.shape
-    for n in range(0, channels, 256):
-        cols = slice(n, n + 256)
-        grads[:, cols] = (
-            dot_t(here[...], whole[1, cols, :])
-            + dot_t(near[...], whole[2, cols, :])
-            + dot_t(far[...], whole[0, cols, :])
-        )
+    for i, (k, grad) in enumerate(((1, here), (2, near), (0, far))):
+        fetched(i)
+        for n in range(0, channels, 256):
+            cols = slice(n, n + 256)
+            product = dot_t(grad[...], whole[k, cols, :])
+            grads[:, cols] = product if i == 0 else grads[:, cols] + product
 
     def step(at):
         unit, scale = normed(block[at, :].astype(jnp.float32))
@@ -234,6 +238,7 @@
 VMEM_SPEC = pl.BlockSpec(memory_space=pltpu.VMEM)
 SMEM_SPEC = pl.BlockSpec(memory_space=pltpu.SMEM)
 ANY_SPEC = pl.BlockSpec(memory_space=pl.ANY)
+HBM_SPEC = pl.BlockSpec(memory_space=pltpu.HBM)
 
 
 def call(kernel, name, out_shape, scratch, flops, *operands, specs=None, aliases=None):
@@ -311,7 +316,7 @@
         work,
         where,
         *pieces[:6],
-        specs=[SMEM_SPEC] + [ANY_SPEC] * 6,
+        specs=[SMEM_SPEC] + [HBM_SPEC] * 6,
     )
     whole, centre, grad2 = call(
         early_kernel,
@@ -332,7 +337,7 @@
         cotangent,
         placed,
         *pieces[6:],
-        specs=[SMEM_SPEC] + [ANY_SPEC] * 2 + [VMEM_SPEC] + [ANY_SPEC] * 2,
+        specs=[SMEM_SPEC] + [HBM_SPEC] * 2 + [VMEM_SPEC] + [HBM_SPEC] * 2,
         aliases={3: 0},
     )
     grad_mixed, sums = call(
@@ -361,7 +366,7 @@
         centre,
         grad2,
         gain2,
-        specs=[ANY_SPEC, VMEM_SPEC] + [ANY_SPEC] * 3 + [VMEM_SPEC] * 4,
+        specs=[HBM_SPEC, VMEM_SPEC] + [HBM_SPEC] * 3 + [VMEM_SPEC] * 4,
     )
     near_grad = permute(grad_mixed, antipode)
     far_grad = permute(grad_mixed, second_neighbour)
@@ -375,7 +380,11 @@
         last_kernel,
         "last",
         jax.ShapeDtypeStruct(inputs.shape, bf16),
-        [pltpu.VMEM(inputs.shape, f32)],
+        [
+            pltpu.VMEM(inputs.shape, f32),
+            pltpu.VMEM((3, channels, width), bf16),
+            pltpu.SemaphoreType.DMA((3,)),
+        ],
         3 * work,
         inputs,
         cotangent,
@@ -384,6 +393,7 @@
         far_grad,
         whole,
         gain1,
+        specs=[VMEM_SPEC] * 5 + [HBM_SPEC, VMEM_SPEC],
     )
     lines = channels // 128
     first_sum = jnp.sum(sums[:, :lines], axis=0).reshape(-1)

time: 129 us -> 129 us (level)
  transfers between devices with their start and end apart: 12 -> 12, of which waited for: 6 -> 6; matrix products, arithmetic and copies ran while one was open for 2% -> 2% of each run, Pallas kernels for 10% -> 11%
where the time goes in v9:
time: 129 us; the launch traced here: 128 us
  starting transfers between devices  63.1 us (49%)
  Pallas kernels  24.6 us (19%)
  waiting for transfers between devices  23.1 us (18%)
  local copies, waits for them, and re-layouts  13.6 us (11%)
  other arithmetic  2.32 us (2%)
    ppermute x10, starting transfers between devices, permute(): return lax.ppermute(value, AXES, pairs)  36.5 us
    pallas_call x8, Pallas kernels, call(): pl.pallas_call(kernel, name=name, out_shape=out_shape, in_specs=specs or...  24.6 us
    all_to_all x1, starting transfers between devices, body(): sums = lax.all_to_all(sums, 'z', 0, 0)  15.1 us
    ppermute x10, waiting for transfers between devices, permute(): return lax.ppermute(value, AXES, pairs)  14 us
    unnamed x48, local copies, waits for them, and re-layouts  11.7 us
    all_to_all x1, starting transfers between devices, body(): sums = lax.all_to_all(sums, ('x', 'yh', 'yl', 'c'), 0, 0)  11.5 us
    all_to_all x1, waiting for transfers between devices, body(): sums = lax.all_to_all(sums, 'z', 0, 0)  7.32 us
  transfers between devices with their start and end apart: 12, of which 6 were waited for; matrix products, arithmetic and copies ran while one was open for 2% of the time, Pallas kernels for 11%

profile of v9, /device:TPU:1, one launch (start us, length us, event | category | flops | bytes accessed | tf_op | source)
XLA Modules:
  0.0 127.8 jit_solution(18427528810015687417)
XLA Ops:
  0.6 5.8 %collective-permute-start = (bf16[256,1536]{1,0:T(8,128)(2,1)}, bf16[256,1536]{1,0:T(8,128)(2,1)S(1)}, u32[]{:S(2)}, u32[]{:S(2)}) collective-permute-start(bf16[256,1536]{1,0:T(8,128)(2,1)} %bitcast.14), channel_id=1, source_target_pairs={{0,64},{1,65},{2,66},{3,67},{4,68},{5,69},{6,70},{7,71},{8,72},{9,... | collective-permute-start | bytes 2359304 | tf_op jit(solution)/shard_map/ppermute | solution.py:26
  6.4 1.3 %slice.21 = bf16[2,384,768]{2,1,0:T(8,128)(2,1)S(1)} slice(bf16[3,384,768]{2,1,0:T(8,128)(2,1)} %weight.1), slice={[0:2], [0:384], [0:768]} | slice | bytes 2359296 | tf_op jit(solution)/shard_map/slice | solution.py:297
  9.2 11.4 %collective-permute-done.block = bf16[256,1536]{1,0:T(8,128)(2,1)S(1)} collective-permute-done((bf16[256,1536]{1,0:T(8,128)(2,1)}, bf16[256,1536]{1,0:T(8,128)(2,1)S(1)}, u32[]{:S(2)}, u32[]{:S(2)}) %collective-permute-start) | collective-permute-done | bytes 786464 | tf_op jit(solution)/shard_map/ppermute | solution.py:26
  20.7 6.1 %collective-permute-start.1 = (bf16[2,384,768]{2,1,0:T(8,128)(2,1)S(1)}, bf16[2,384,768]{2,1,0:T(8,128)(2,1)}, u32[]{:S(2)}, u32[]{:S(2)}) collective-permute-start(bf16[2,384,768]{2,1,0:T(8,128)(2,1)S(1)} %slice.21), channel_id=1, source_target_pairs={{0,2},{1,3},{2,64},{3,65},{4,6},{5,7},{6,68},{7,69},{8,10},{9,11},... | collective-permute-start | bytes 3538952 | tf_op jit(solution)/shard_map/ppermute | solution.py:26
  26.8 3.4 %collective-permute-start.2 = (bf16[2,384,768]{2,1,0:T(8,128)(2,1)S(1)}, bf16[2,384,768]{2,1,0:T(8,128)(2,1)}, u32[]{:S(2)}, u32[]{:S(2)}) collective-permute-start(bf16[2,384,768]{2,1,0:T(8,128)(2,1)S(1)} %pad_maximum_fusion), channel_id=1, source_target_pairs={{0,66},{1,67},{2,0},{3,1},{4,70},{5,71},{6,4},{7,5},{8,74},{9,75},... | collective-permute-start | bytes 3538952 | tf_op jit(solution)/shard_map/ppermute | solution.py:26
  30.2 3.2 %collective-permute-start.3 = (bf16[256,1536]{1,0:T(8,128)(2,1)S(1)}, bf16[256,1536]{1,0:T(8,128)(2,1)S(1)}, u32[]{:S(2)}, u32[]{:S(2)}) collective-permute-start(bf16[256,1536]{1,0:T(8,128)(2,1)S(1)} %collective-permute-done.block), channel_id=1, source_target_pairs={{0,128},{1,129},{2,130},{3,131},{4,132},{5,133},{6,134},{7,135},{8... | collective-permute-start | bytes 2359304 | tf_op jit(solution)/shard_map/ppermute | solution.py:26
  33.4 4.2 %collective-permute-start.5 = (bf16[3,384,768]{2,1,0:T(8,128)(2,1)S(1)}, bf16[3,384,768]{2,1,0:T(8,128)(2,1)}, u32[]{:S(2)}, u32[]{:S(2)}) collective-permute-start(bf16[3,384,768]{2,1,0:T(8,128)(2,1)S(1)} %copy-done.2), channel_id=1, source_target_pairs={{0,1},{1,0},{2,3},{3,2},{4,5},{5,4},{6,7},{7,6},{8,9},{9,8},{10,11... | collective-permute-start | bytes 5308424 | tf_op jit(solution)/shard_map/ppermute | solution.py:26
  37.7 1.9 %collective-permute-start.4 = (bf16[384,768]{1,0:T(8,128)(2,1)S(1)}, bf16[384,768]{1,0:T(8,128)(2,1)S(1)}, u32[]{:S(2)}, u32[]{:S(2)}) collective-permute-start(bf16[384,768]{1,0:T(8,128)(2,1)S(1)} %slice_bitcast_fusion), channel_id=1, source_target_pairs={{0,1},{1,0},{2,3},{3,2},{4,5},{5,4},{6,7},{7,6},{8,9},{9,8},{10,11... | collective-permute-start | bytes 1769480 | tf_op jit(solution)/shard_map/ppermute | solution.py:26
  39.6 1.8 %prepare.4 = (bf16[256,1536]{1,0:T(8,128)(2,1)S(1)}, f32[256,1536]{1,0:T(8,128)S(1)}) custom-call(bf16[256,1536]{1,0:T(8,128)(2,1)S(1)} %bitcast.15, f32[1,1536]{1,0:T(1,128)S(1)} %broadcast_in_dim.6.gain), custom_call_target="tpu_custom_call" | custom-call | flops 15728640 | bytes 792576 | tf_op jit(solution)/shard_map/prepare/pallas_call | solution.py:246
  43.4 1.8 %prepare.3 = (bf16[256,1536]{1,0:T(8,128)(2,1)S(1)}, f32[256,1536]{1,0:T(8,128)S(1)}) custom-call(bf16[256,1536]{1,0:T(8,128)(2,1)S(1)} %collective-permute-done.block, f32[1,1536]{1,0:T(1,128)S(1)} %broadcast_in_dim.6.gain), custom_call_target="tpu_custom_call" | custom-call | flops 15728640 | bytes 792576 | tf_op jit(solution)/shard_map/prepare/pallas_call | solution.py:246
  48.1 1.8 %prepare.5 = (bf16[256,1536]{1,0:T(8,128)(2,1)S(1)}, f32[256,1536]{1,0:T(8,128)S(1)}) custom-call(bf16[256,1536]{1,0:T(8,128)(2,1)S(1)} %collective-permute-done.3.block, f32[1,1536]{1,0:T(1,128)S(1)} %broadcast_in_dim.6.gain), custom_call_target="tpu_custom_call" | custom-call | flops 15728640 | bytes 792576 | tf_op jit(solution)/shard_map/prepare/pallas_call | solution.py:246
  52.9 1.5 %collective-permute-done.2.down = bf16[2,384,768]{2,1,0:T(8,128)(2,1)} collective-permute-done((bf16[2,384,768]{2,1,0:T(8,128)(2,1)S(1)}, bf16[2,384,768]{2,1,0:T(8,128)(2,1)}, u32[]{:S(2)}, u32[]{:S(2)}) %collective-permute-start.2) | collective-permute-done | bytes 1179680 | tf_op jit(solution)/shard_map/ppermute | solution.py:26
  54.5 4.6 %collective-permute-start.6 = (bf16[2,384,768]{2,1,0:T(8,128)(2,1)}, bf16[2,384,768]{2,1,0:T(8,128)(2,1)}, u32[]{:S(2)}, u32[]{:S(2)}) collective-permute-start(bf16[2,384,768]{2,1,0:T(8,128)(2,1)} %collective-permute-done.1.up), channel_id=1, source_target_pairs={{0,1},{1,0},{2,3},{3,2},{4,5},{5,4},{6,7},{7,6},{8,9},{9,8},{10,11... | collective-permute-start | bytes 3538952 | tf_op jit(solution)/shard_map/ppermute | solution.py:26
  59.1 2.1 %collective-permute-start.7 = (bf16[2,384,768]{2,1,0:T(8,128)(2,1)}, bf16[2,384,768]{2,1,0:T(8,128)(2,1)}, u32[]{:S(2)}, u32[]{:S(2)}) collective-permute-start(bf16[2,384,768]{2,1,0:T(8,128)(2,1)} %collective-permute-done.2.down), channel_id=1, source_target_pairs={{0,1},{1,0},{2,3},{3,2},{4,5},{5,4},{6,7},{7,6},{8,9},{9,8},{10,11... | collective-permute-start | bytes 3538952 | tf_op jit(solution)/shard_map/ppermute | solution.py:26
  62.4 3.1 %place.1.placed = bf16[4,1536,768]{2,1,0:T(8,128)(2,1)S(1)} custom-call(s32[5]{0:T(128)S(1)} %stack.31.where, bf16[3,384,768]{2,1,0:T(8,128)(2,1)S(1)} %copy-done.2, bf16[384,768]{1,0:T(8,128)(2,1)S(1)} %copy-done.6, bf16[3,384,768]{2,1,0:T(8,128)(2,1)} %collective-permute-done.5.weight_s, bf16[384,768]{1,0:T(8,128)(2,1)S(1)} %copy-done.20, ...), custom_call_target="tpu_custom_call" | custom-call | flops 603979776 | bytes 7077908 | tf_op jit(solution)/shard_map/place/pallas_call | solution.py:246
  65.6 4.2 %early.1 = (bf16[4,1536,768]{2,1,0:T(8,128)(2,1)S(1)}, f32[256,768]{1,0:T(8,128)S(1)}, f32[256,768]{1,0:T(8,128)S(1)}) custom-call(s32[5]{0:T(128)S(1)} %stack.31.where, bf16[256,1536]{1,0:T(8,128)(2,1)S(1)} %copy-done.18, bf16[256,1536]{1,0:T(8,128)(2,1)S(1)} %bitcast.17, bf16[4,1536,768]{2,1,0:T(8,128)(2,1)S(1)} %place.1.placed, ...), custom_call_target="tpu_custom_call", output_to_operand_aliasing={{0}: (3, {})} | custom-call | flops 1207959552 | bytes 13369364 | tf_op jit(solution)/shard_map/early/pallas_call | solution.py:246
  69.9 6.5 %middle.1 = (bf16[256,768]{1,0:T(8,128)(2,1)S(1)}, f32[16,18,128]{2,1,0:T(8,128)}) custom-call(bf16[256,1536]{1,0:T(8,128)(2,1)S(1)} %copy-done.14, bf16[256,1536]{1,0:T(8,128)(2,1)S(1)} %copy-done.16, f32[256,1536]{1,0:T(8,128)S(1)} %copy-done.10, f32[256,1536]{1,0:T(8,128)S(1)} %copy-done.8, f32[256,1536]{1,0:T(8,128)S(1)} %copy-done.12, ...), custom_call_target="tpu_custom_call" | custom-call | flops 3019898880 | bytes 17304576 | tf_op jit(solution)/shard_map/middle/pallas_call | solution.py:246
  76.3 15.1 %all-to-all-start = ((f32[16,18,128]{2,1,0:T(8,128)}), f32[16,18,128]{2,1,0:T(8,128)S(1)}, u32[]{:S(2)}, u32[]{:S(2)}) async-start(f32[16,18,128]{2,1,0:T(8,128)} %get-tuple-element.44), calls=%async_computation | async-start | bytes 393216 | tf_op jit(solution)/shard_map/all_to_all | solution.py:373
  91.4 4.5 %collective-permute-start.8 = (bf16[256,768]{1,0:T(8,128)(2,1)S(1)}, bf16[256,768]{1,0:T(8,128)(2,1)S(1)}, u32[]{:S(2)}, u32[]{:S(2)}) collective-permute-start(bf16[256,768]{1,0:T(8,128)(2,1)S(1)} %get-tuple-element.43.here), channel_id=1, source_target_pairs={{0,64},{1,65},{2,66},{3,67},{4,68},{5,69},{6,70},{7,71},{8,72},{9,... | collective-permute-start | bytes 1179656 | tf_op jit(solution)/shard_map/ppermute | solution.py:26
  96.6 7.3 %all-to-all-done.arrived = f32[16,18,128]{2,1,0:T(8,128)S(1)} async-done(((f32[16,18,128]{2,1,0:T(8,128)}), f32[16,18,128]{2,1,0:T(8,128)S(1)}, u32[]{:S(2)}, u32[]{:S(2)}) %all-to-all-start) | async-done | bytes 147488 | tf_op jit(solution)/shard_map/all_to_all | solution.py:373
  104.8 11.5 %all-to-all-start.1 = ((f32[32,18,128]{2,1,0:T(8,128)}), f32[32,18,128]{2,1,0:T(8,128)S(1)}, u32[]{:S(2)}, u32[]{:S(2)}) async-start(f32[32,18,128]{2,1,0:T(8,128)} %spread.1), calls=%async_computation.1 | async-start | bytes 786432 | tf_op jit(solution)/shard_map/all_to_all | solution.py:377
  116.3 3.7 %copy-done.1 = bf16[4,1536,768]{2,1,0:T(8,128)(2,1)S(1)} copy-done((bf16[4,1536,768]{2,1,0:T(8,128)(2,1)S(1)}, bf16[4,1536,768]{2,1,0:T(8,128)(2,1)}, u32[]{:S(2)}) %copy-start.1) | copy-done | bytes 9437208
  120.0 4.8 %last.1 = bf16[256,1536]{1,0:T(8,128)(2,1)} custom-call(bf16[256,1536]{1,0:T(8,128)(2,1)S(1)} %bitcast.16, bf16[256,1536]{1,0:T(8,128)(2,1)S(1)} %bitcast.18, bf16[256,768]{1,0:T(8,128)(2,1)S(1)} %collective-permute-done.8.near, bf16[256,768]{1,0:T(8,128)(2,1)S(1)} %get-tuple-element.43.here, bf16[256,768]{1,0:T(8,128)(2,1)S(1)} %collective-permute-done.9.far, ...), custom_call_target="tpu_custom_call" | custom-call | flops 1811939328 | bytes 12195840 | tf_op jit(solution)/shard_map/last/pallas_call | solution.py:246
  124.8 1.8 %all-to-all-done.1 = f32[32,18,128]{2,1,0:T(8,128)S(1)} async-done(((f32[32,18,128]{2,1,0:T(8,128)}), f32[32,18,128]{2,1,0:T(8,128)S(1)}, u32[]{:S(2)}, u32[]{:S(2)}) %all-to-all-start.1) | async-done | bytes 294944 | tf_op jit(solution)/shard_map/all_to_all | solution.py:377
  (68 shorter events, 13.3 us)
Async XLA Ops:
  0.6 7.2 %copy-start.21 = (bf16[192,1536]{1,0:T(8,128)(2,1)S(1)}, bf16[192,1536]{1,0:T(8,128)(2,1)}, u32[]{:S(2)}) copy-start(bf16[192,1536]{1,0:T(8,128)(2,1)} %param.8) | copy-start | bytes 1769476
  0.6 20.1 %collective-permute-start = (bf16[256,1536]{1,0:T(8,128)(2,1)}, bf16[256,1536]{1,0:T(8,128)(2,1)S(1)}, u32[]{:S(2)}, u32[]{:S(2)}) collective-permute-start(bf16[256,1536]{1,0:T(8,128)(2,1)} %bitcast.14), channel_id=1, source_target_pairs={{0,64},{1,65},{2,66},{3,67},{4,68},{5,69},{6,70},{7,71},{8,72},{9,... | collective-permute-start | bytes 2359304 | tf_op jit(solution)/shard_map/ppermute | solution.py:26
  9.1 24.3 %copy-start.2 = (bf16[3,384,768]{2,1,0:T(8,128)(2,1)S(1)}, bf16[3,384,768]{2,1,0:T(8,128)(2,1)}, u32[]{:S(2)}) copy-start(bf16[3,384,768]{2,1,0:T(8,128)(2,1)} %weight.1) | copy-start | bytes 5308420
  9.2 30.4 %copy-start.22 = (f32[1536]{0:T(1024)S(1)}, f32[1536]{0:T(1024)}, u32[]{:S(2)}) copy-start(f32[1536]{0:T(1024)} %param.9) | copy-start | bytes 18436
  9.2 30.4 %copy-start.3 = (bf16[2,128,1536]{2,1,0:T(8,128)(2,1)S(1)}, bf16[2,128,1536]{2,1,0:T(8,128)(2,1)}, u32[]{:S(2)}) copy-start(bf16[2,128,1536]{2,1,0:T(8,128)(2,1)} %param.6) | copy-start | bytes 2359300
  20.7 32.2 %collective-permute-start.1 = (bf16[2,384,768]{2,1,0:T(8,128)(2,1)S(1)}, bf16[2,384,768]{2,1,0:T(8,128)(2,1)}, u32[]{:S(2)}, u32[]{:S(2)}) collective-permute-start(bf16[2,384,768]{2,1,0:T(8,128)(2,1)S(1)} %slice.21), channel_id=1, source_target_pairs={{0,2},{1,3},{2,64},{3,65},{4,6},{5,7},{6,68},{7,69},{8,10},{9,11},... | collective-permute-start | bytes 3538952 | tf_op jit(solution)/shard_map/ppermute | solution.py:26
  26.8 27.6 %collective-permute-start.2 = (bf16[2,384,768]{2,1,0:T(8,128)(2,1)S(1)}, bf16[2,384,768]{2,1,0:T(8,128)(2,1)}, u32[]{:S(2)}, u32[]{:S(2)}) collective-permute-start(bf16[2,384,768]{2,1,0:T(8,128)(2,1)S(1)} %pad_maximum_fusion), channel_id=1, source_target_pairs={{0,66},{1,67},{2,0},{3,1},{4,70},{5,71},{6,4},{7,5},{8,74},{9,75},... | collective-permute-start | bytes 3538952 | tf_op jit(solution)/shard_map/ppermute | solution.py:26
  30.2 17.9 %collective-permute-start.3 = (bf16[256,1536]{1,0:T(8,128)(2,1)S(1)}, bf16[256,1536]{1,0:T(8,128)(2,1)S(1)}, u32[]{:S(2)}, u32[]{:S(2)}) collective-permute-start(bf16[256,1536]{1,0:T(8,128)(2,1)S(1)} %collective-permute-done.block), channel_id=1, source_target_pairs={{0,128},{1,129},{2,130},{3,131},{4,132},{5,133},{6,134},{7,135},{8... | collective-permute-start | bytes 2359304 | tf_op jit(solution)/shard_map/ppermute | solution.py:26
  33.4 28.0 %collective-permute-start.5 = (bf16[3,384,768]{2,1,0:T(8,128)(2,1)S(1)}, bf16[3,384,768]{2,1,0:T(8,128)(2,1)}, u32[]{:S(2)}, u32[]{:S(2)}) collective-permute-start(bf16[3,384,768]{2,1,0:T(8,128)(2,1)S(1)} %copy-done.2), channel_id=1, source_target_pairs={{0,1},{1,0},{2,3},{3,2},{4,5},{5,4},{6,7},{7,6},{8,9},{9,8},{10,11... | collective-permute-start | bytes 5308424 | tf_op jit(solution)/shard_map/ppermute | solution.py:26
  37.7 14.2 %collective-permute-start.4 = (bf16[384,768]{1,0:T(8,128)(2,1)S(1)}, bf16[384,768]{1,0:T(8,128)(2,1)S(1)}, u32[]{:S(2)}, u32[]{:S(2)}) collective-permute-start(bf16[384,768]{1,0:T(8,128)(2,1)S(1)} %slice_bitcast_fusion), channel_id=1, source_target_pairs={{0,1},{1,0},{2,3},{3,2},{4,5},{5,4},{6,7},{7,6},{8,9},{9,8},{10,11... | collective-permute-start | bytes 1769480 | tf_op jit(solution)/shard_map/ppermute | solution.py:26
  39.6 21.6 %copy-start.23 = (f32[768]{0:T(1024)S(1)}, f32[768]{0:T(1024)}, u32[]{:S(2)}) copy-start(f32[768]{0:T(1024)} %param.10) | copy-start | bytes 9220
  39.6 21.7 %copy-start.6 = (bf16[384,768]{1,0:T(8,128)(2,1)S(1)}, bf16[384,768]{1,0:T(8,128)(2,1)}, u32[]{:S(2)}) copy-start(bf16[384,768]{1,0:T(8,128)(2,1)} %get-tuple-element.45.folded) | copy-start | bytes 1769476
  54.5 11.0 %collective-permute-start.6 = (bf16[2,384,768]{2,1,0:T(8,128)(2,1)}, bf16[2,384,768]{2,1,0:T(8,128)(2,1)}, u32[]{:S(2)}, u32[]{:S(2)}) collective-permute-start(bf16[2,384,768]{2,1,0:T(8,128)(2,1)} %collective-permute-done.1.up), channel_id=1, source_target_pairs={{0,1},{1,0},{2,3},{3,2},{4,5},{5,4},{6,7},{7,6},{8,9},{9,8},{10,11... | collective-permute-start | bytes 3538952 | tf_op jit(solution)/shard_map/ppermute | solution.py:26
  59.1 6.4 %collective-permute-start.7 = (bf16[2,384,768]{2,1,0:T(8,128)(2,1)}, bf16[2,384,768]{2,1,0:T(8,128)(2,1)}, u32[]{:S(2)}, u32[]{:S(2)}) collective-permute-start(bf16[2,384,768]{2,1,0:T(8,128)(2,1)} %collective-permute-done.2.down), channel_id=1, source_target_pairs={{0,1},{1,0},{2,3},{3,2},{4,5},{5,4},{6,7},{7,6},{8,9},{9,8},{10,11... | collective-permute-start | bytes 3538952 | tf_op jit(solution)/shard_map/ppermute | solution.py:26
  65.5 4.3 %copy-start.8 = (f32[256,1536]{1,0:T(8,128)S(1)}, f32[256,1536]{1,0:T(8,128)}, u32[]{:S(2)}) copy-start(f32[256,1536]{1,0:T(8,128)} %copy-done.7) | copy-start | bytes 4718596
  65.5 4.3 %copy-start.10 = (f32[256,1536]{1,0:T(8,128)S(1)}, f32[256,1536]{1,0:T(8,128)}, u32[]{:S(2)}) copy-start(f32[256,1536]{1,0:T(8,128)} %copy-done.9) | copy-start | bytes 4718596
  65.6 4.3 %copy-start.12 = (f32[256,1536]{1,0:T(8,128)S(1)}, f32[256,1536]{1,0:T(8,128)}, u32[]{:S(2)}) copy-start(f32[256,1536]{1,0:T(8,128)} %copy-done.11) | copy-start | bytes 4718596
  65.6 4.3 %copy-start.14 = (bf16[256,1536]{1,0:T(8,128)(2,1)S(1)}, bf16[256,1536]{1,0:T(8,128)(2,1)}, u32[]{:S(2)}) copy-start(bf16[256,1536]{1,0:T(8,128)(2,1)} %copy-done.13) | copy-start | bytes 2359300
  69.8 6.5 %copy-start = (bf16[4,1536,768]{2,1,0:T(8,128)(2,1)}, bf16[4,1536,768]{2,1,0:T(8,128)(2,1)S(1)}, u32[]{:S(2)}) copy-start(bf16[4,1536,768]{2,1,0:T(8,128)(2,1)S(1)} %get-tuple-element.40.whole.away) | copy-start | bytes 28311556
  76.3 40.0 %copy-start.5 = (bf16[2,128,1536]{2,1,0:T(8,128)(2,1)S(1)}, bf16[2,128,1536]{2,1,0:T(8,128)(2,1)}, u32[]{:S(2)}) copy-start(bf16[2,128,1536]{2,1,0:T(8,128)(2,1)} %param.11) | copy-start | bytes 2359300
  76.3 27.6 %all-to-all-start = ((f32[16,18,128]{2,1,0:T(8,128)}), f32[16,18,128]{2,1,0:T(8,128)S(1)}, u32[]{:S(2)}, u32[]{:S(2)}) async-start(f32[16,18,128]{2,1,0:T(8,128)} %get-tuple-element.44), calls=%async_computation | async-start | bytes 393216 | tf_op jit(solution)/shard_map/all_to_all | solution.py:373
  91.4 24.9 %collective-permute-start.8 = (bf16[256,768]{1,0:T(8,128)(2,1)S(1)}, bf16[256,768]{1,0:T(8,128)(2,1)S(1)}, u32[]{:S(2)}, u32[]{:S(2)}) collective-permute-start(bf16[256,768]{1,0:T(8,128)(2,1)S(1)} %get-tuple-element.43.here), channel_id=1, source_target_pairs={{0,64},{1,65},{2,66},{3,67},{4,68},{5,69},{6,70},{7,71},{8,72},{9,... | collective-permute-start | bytes 1179656 | tf_op jit(solution)/shard_map/ppermute | solution.py:26
  96.0 20.3 %collective-permute-start.9 = (bf16[256,768]{1,0:T(8,128)(2,1)S(1)}, bf16[256,768]{1,0:T(8,128)(2,1)S(1)}, u32[]{:S(2)}, u32[]{:S(2)}) collective-permute-start(bf16[256,768]{1,0:T(8,128)(2,1)S(1)} %get-tuple-element.43.here), channel_id=1, source_target_pairs={{64,128},{65,129},{66,130},{67,131},{68,132},{69,133},{70,134},{71... | collective-permute-start | bytes 1179656 | tf_op jit(solution)/shard_map/ppermute | solution.py:26
  104.8 21.8 %all-to-all-start.1 = ((f32[32,18,128]{2,1,0:T(8,128)}), f32[32,18,128]{2,1,0:T(8,128)S(1)}, u32[]{:S(2)}, u32[]{:S(2)}) async-start(f32[32,18,128]{2,1,0:T(8,128)} %spread.1), calls=%async_computation.1 | async-start | bytes 786432 | tf_op jit(solution)/shard_map/all_to_all | solution.py:377
  (13 other events, 23.5 us)
